TPU v7x, 128 devices: a whole 4x4x4 slice. The times are simulated.
128 devices in a mesh: row: 8 (over z, core), col: 16 (over y, x).
Axes of the slice: x: 4, y: 4, z: 4, core: 2. Of those that a mesh axis runs over, the one named last changes fastest.
Arguments:
- emb: bfloat16 [524288, 512], P(('row', 'col')), may hold values from -6 to 6
- tiles: bfloat16 [2048, 4, 256, 256], P(('row', 'col')), may hold values from -0.375 to 0.375
- msg_src: int32 [2048, 4], P(('row', 'col')), may hold values from 0 to 15
- msg_dst: int32 [2048, 4], P(('row', 'col')), may hold values from 0 to 16, as said below
- msg_count: int32 [2048, 4], P(('row', 'col')), may hold values from 1 to 256
- weight: bfloat16 [512, 512], replicated, may hold values from -0.25 to 0.25
- docs: bfloat16 [512, 512], P('row'), may hold values from -0.059814453 to 0.099609375
- doc_labels: int32 [512, 8], replicated, may hold values from 0 to 524287
Outputs:
- hidden: bfloat16 [524288, 512], P(('row', 'col'))
- grad_docs: float32 [512, 512], P('row')
- grad_weight: float32 [512, 512], replicated
Inputs may be any that keep to these rules, and one draw needn't show every extreme that they name: For each sending device and each column of its row, the used slots (msg_dst below 16) come first and 16 marks an unused slot. In every row of devices some column receives all 4 slots used from every sender of that row.
All inputs are finite; a program needn't handle non-finite values.
Results may differ from a plain program's by a relative error of at most 0.0052.
Values may be sent and summed in bfloat16 or wider, within the bound.
No kernel may reach another device: no remote copies, remote signals or barrier semaphores. Data moves between devices by JAX's collectives and lax.ppermute only.
A program may use at most 192 MiB of HBM per device.

v0:
```python
import functools

import jax
import jax.numpy as jnp
from jax import lax
from jax.experimental import pallas as pl
from jax.experimental.pallas import tpu as pltpu
from jax.sharding import PartitionSpec as P


BF = jnp.bfloat16
F32 = jnp.float32
CHUNK_ROWS = (192, 64)
STEP_ROWS = 32
RING = 4


def wrap(i):
    return lax.rem(i + RING, RING)


def shift_pairs(axis, by):
    pairs = []
    for y in range(RING):
        for x in range(RING):
            ty, tx = ((y + by) % RING, x) if axis == "y" else (y, (x + by) % RING)
            pairs.append((y * RING + x, ty * RING + tx))
    return pairs


def shift(v, axis, by):
    return lax.ppermute(v, "col", shift_pairs(axis, by))


def message_kernel(order_ref, src_ref, emb_ref, *refs):
    d = pl.program_id(0)
    for j in range(RING):
        tile_ref, out_ref = refs[j], refs[j - RING]
        p = order_ref[j * RING + d]
        for q in range(tile_ref.shape[1]):
            out_ref[0, q] = jnp.dot(
                tile_ref[0, q], emb_ref[src_ref[p, q]], preferred_element_type=F32
            ).astype(BF)


def messages_of(order, src, blocks, tiles, row, rows, half, after):
    _, cap, blk, _ = tiles.shape
    n_blk, _, width = blocks.shape
    at = row // rows
    part = width // 2
    shape = (RING, cap, rows, part)
    return pl.pallas_call(
        message_kernel,
        grid_spec=pltpu.PrefetchScalarGridSpec(
            num_scalar_prefetch=2,
            grid=(RING,),
            in_specs=[
                pl.BlockSpec((n_blk, blk, part), lambda i, o, s: (0, 0, half),
                             pipeline_mode=pl.Buffered(1)),
            ] + [
                pl.BlockSpec((1, cap, rows, blk),
                             lambda i, o, s, j=j: (o[j * RING + i], 0, at, 0))
                for j in range(RING)
            ] + [pl.BlockSpec(memory_space=pl.ANY)] * len(after),
            out_specs=[pl.BlockSpec((1,) + shape[1:], lambda i, o, s: (i, 0, 0, 0))] * RING,
        ),
        out_shape=[jax.ShapeDtypeStruct(shape, BF)] * RING,
    )(order, src, blocks, *[tiles] * RING, *after)


def add_slots(acc_ref, table_ref, y, x, half, ahead, parts, columns):
    n_blk = acc_ref.shape[0]
    cap = parts[0].shape[1]
    for came, ref in enumerate(parts):
        if half == 0:
            s = y * RING + wrap(x - came)
            p = wrap(y + ahead) * RING + x
        else:
            s = wrap(y - came) * RING + x
            p = y * RING + wrap(x + ahead)

        def add(q, carry):
            dst = table_ref[s, p * 2 * cap + q]
            cnt = table_ref[s, p * 2 * cap + cap + q].astype(F32)

            @pl.when(dst < n_blk)
            def _():
                acc_ref[dst, :, columns] = (
                    acc_ref[dst, :, columns] + cnt * ref[0, q].astype(F32)
                )

            return carry

        lax.fori_loop(0, cap, add, 0)


def far_kernel(half, pos_ref, table_ref, *refs):
    parts, (low_ref, high_ref, acc_ref) = refs[:RING], refs[-3:]
    acc_ref[...] = jnp.zeros_like(acc_ref)
    add_slots(acc_ref, table_ref, pos_ref[0], pos_ref[1], half, 2, parts, slice(None))
    n = low_ref.shape[0]
    low_ref[...] = acc_ref[:n].astype(BF)
    high_ref[...] = acc_ref[n:].astype(BF)


def near_kernel(half, pos_ref, table_ref, *refs):
    ones, threes = refs[:RING], refs[RING:2 * RING]
    low_in, high_in, up_ref, down_ref, acc_ref = refs[2 * RING:]
    n = low_in.shape[0]
    acc_ref[:n] = low_in[...].astype(F32)
    acc_ref[n:] = jnp.zeros_like(acc_ref[n:])
    add_slots(acc_ref, table_ref, pos_ref[0], pos_ref[1], half, 1, ones, slice(None))
    up_ref[...] = acc_ref[...].astype(BF)
    acc_ref[:n] = jnp.zeros_like(acc_ref[:n])
    acc_ref[n:] = high_in[...].astype(F32)
    add_slots(acc_ref, table_ref, pos_ref[0], pos_ref[1], half, 3, threes, slice(None))
    down_ref[...] = acc_ref[...].astype(BF)


SMEM = pl.BlockSpec(memory_space=pltpu.SMEM)


def slot_spec(part, step_rows, ahead):
    return pl.BlockSpec((1, part.shape[1], step_rows, part.shape[3]),
                        lambda i: (ahead, 0, i, 0))


def far_sums(half, pos, table, parts, n_blk, after):
    _, _, rows, cols = parts[0].shape
    step_rows = min(STEP_ROWS, rows)
    n = n_blk // 2
    return pl.pallas_call(
        functools.partial(far_kernel, half),
        grid=(rows // step_rows,),
        in_specs=[SMEM, SMEM] + [slot_spec(a, step_rows, 2) for a in parts]
        + [pl.BlockSpec(memory_space=pl.ANY)] * len(after),
        out_specs=[pl.BlockSpec((n, step_rows, cols), lambda i: (0, i, 0))] * 2,
        out_shape=[jax.ShapeDtypeStruct((n, rows, cols), BF)] * 2,
        scratch_shapes=[pltpu.VMEM((n_blk, step_rows, cols), F32)],
    )(pos, table, *parts, *after)


def near_sums(half, pos, table, parts, low, high):
    _, _, rows, cols = parts[0].shape
    step_rows = min(STEP_ROWS, rows)
    n = low.shape[0]
    rowed = lambda k: pl.BlockSpec((k, step_rows, cols), lambda i: (0, i, 0))
    return pl.pallas_call(
        functools.partial(near_kernel, half),
        grid=(rows // step_rows,),
        in_specs=[SMEM, SMEM] + [slot_spec(a, step_rows, 1) for a in parts]
        + [slot_spec(a, step_rows, 3) for a in parts] + [rowed(n), rowed(n)],
        out_specs=[rowed(2 * n)] * 2,
        out_shape=[jax.ShapeDtypeStruct((2 * n, rows, cols), BF)] * 2,
        scratch_shapes=[pltpu.VMEM((2 * n, step_rows, cols), F32)],
    )(pos, table, *parts, *parts, low, high)


def head_kernel(first, row, blk, labels_total, pos_count,
                pos_ref, table_ref, inv_ref, near_ref, *refs):
    mine = (refs[:RING], refs[RING:2 * RING])
    refs = refs[2 * RING:]
    sums = (refs[:2], refs[2:4])
    emb_ref, labels_ref, w_ref, docs_ref = refs[4:8]
    rest = refs[8:]
    if first:
        hid_ref, gd_ref, gw_ref, acc_ref, agg_ref, ds_ref = rest
    else:
        gd_in, gw_in, _, hid_ref, gd_ref, gw_ref, acc_ref, agg_ref, ds_ref = rest
    step = pl.program_id(0)

    @pl.when(step == 0)
    def _():
        if first:
            gd_ref[...] = jnp.zeros_like(gd_ref)
            gw_ref[...] = jnp.zeros_like(gw_ref)
        else:
            gd_ref[...] = gd_in[...]
            gw_ref[...] = gw_in[...]

    n_blk, rows, width = emb_ref.shape
    part = width // 2
    for half in range(2):
        columns = slice(half * part, (half + 1) * part)
        up, down = sums[half]
        for b in range(n_blk):
            acc_ref[b, :, columns] = (
                float(blk) * emb_ref[b, :, columns].astype(F32)
                + up[b].astype(F32) + down[b].astype(F32)
            )
        add_slots(acc_ref, table_ref, pos_ref[0], pos_ref[1], half, 0, mine[half], columns)
    for b in range(n_blk):
        agg_ref[b * rows:(b + 1) * rows, :] = (acc_ref[b] * inv_ref[b]).astype(BF)
    agg = agg_ref[...]
    pre = jnp.dot(agg, w_ref[...], preferred_element_type=F32)
    sig = 1.0 / (1.0 + jnp.exp(-pre))
    hid = (pre * sig).astype(BF)
    for b in range(n_blk):
        hid_ref[b] = hid[b * rows:(b + 1) * rows, :]
    scores = lax.dot_general(hid, docs_ref[...], (((1,), (1,)), ((), ())),
                             preferred_element_type=F32)
    prob = 1.0 / (1.0 + jnp.exp(-scores))
    for b in range(n_blk):
        one = prob[b * rows:(b + 1) * rows, :]
        ds_ref[b * rows:(b + 1) * rows, :] = (one * (1.0 / labels_total)).astype(BF)

        @pl.when(near_ref[(b * blk + row) // rows + step] > 0)
        def _():
            ids = b * blk + row + step * rows + lax.broadcasted_iota(jnp.int32, one.shape, 0)
            hit = labels_ref[0:1, :] == ids
            for j in range(1, labels_ref.shape[0]):
                hit = hit | (labels_ref[j:j + 1, :] == ids)
            ds_ref[b * rows:(b + 1) * rows, :] = jnp.where(
                hit, (one - 1.0) * (1.0 / pos_count), one * (1.0 / labels_total)
            ).astype(BF)
    ds = ds_ref[...]
    gd_ref[...] += lax.dot_general(ds, hid, (((0,), (0,)), ((), ())),
                                   preferred_element_type=F32)
    dhid = jnp.dot(ds, docs_ref[...], preferred_element_type=F32)
    dpre = (dhid * sig * (1.0 + pre * (1.0 - sig))).astype(BF)
    gw_ref[...] += lax.dot_general(agg, dpre, (((0,), (0,)), ((), ())),
                                   preferred_element_type=F32)


def head(pos, table, inv, near, mine, sums, blocks, labels, weight, docs, carry, row,
         labels_total, pos_count):
    n_blk, blk, width = blocks.shape
    rows = mine[0][0].shape[2]
    step_rows = min(STEP_ROWS, rows)
    at = row // step_rows
    n_doc = docs.shape[0]
    first = carry is None
    full = lambda a: pl.BlockSpec(a, lambda i: (0, 0), pipeline_mode=pl.Buffered(1))
    rowed = lambda n: pl.BlockSpec((n_blk, step_rows, n), lambda i: (0, at + i, 0))
    in_specs = [SMEM, SMEM, SMEM, SMEM]
    args = [pos, table, inv, near]
    for group in mine:
        in_specs += [slot_spec(a, step_rows, 0) for a in group]
        args += list(group)
    for group in sums:
        in_specs += [pl.BlockSpec((n_blk, step_rows, width // 2), lambda i: (0, i, 0))] * 2
        args += list(group)
    in_specs += [rowed(width), full(labels.shape), full(weight.shape), full(docs.shape)]
    args += [blocks, labels, weight, docs]
    aliases = {}
    if not first:
        hid, gd, gw = carry
        in_specs += [full(gd.shape), full(gw.shape), pl.BlockSpec(memory_space=pl.ANY)]
        aliases = {len(args) + 2: 0}
        args += [gd, gw, hid]
    return pl.pallas_call(
        functools.partial(head_kernel, first, row, blk, labels_total, pos_count),
        grid=(rows // step_rows,),
        in_specs=in_specs,
        out_specs=[rowed(width),
                   pl.BlockSpec((n_doc, width), lambda i: (0, 0)),
                   pl.BlockSpec((width, width), lambda i: (0, 0))],
        out_shape=[jax.ShapeDtypeStruct(blocks.shape, BF),
                   jax.ShapeDtypeStruct((n_doc, width), F32),
                   jax.ShapeDtypeStruct((width, width), F32)],
        scratch_shapes=[pltpu.VMEM((n_blk, step_rows, width), F32),
                        pltpu.VMEM((n_blk * step_rows, width), BF),
                        pltpu.VMEM((n_blk * step_rows, n_doc), BF)],
        input_output_aliases=aliases,
        compiler_params=pltpu.CompilerParams(vmem_limit_bytes=48 << 20),
    )(*args)


def swap(x, axis):
    return lax.all_to_all(x, axis, split_axis=0, concat_axis=0, tiled=True)


def spread(x, axis, n):
    return swap(jnp.broadcast_to(x[None], (n,) + x.shape), axis)


def per_device(emb, tiles, msg_src, msg_dst, msg_count, weight, docs, doc_labels):
    n_col = lax.axis_size("col")
    n_row = lax.axis_size("row")
    label_dev, width = emb.shape
    n_peer, cap, blk, _ = tiles.shape
    blk_dev = label_dev // blk
    labels_total = float(label_dev * n_row * n_col)
    pos_count = doc_labels.shape[1]
    n_doc = docs.shape[0] * n_row
    blocks = emb.reshape(blk_dev, blk, width)
    col = lax.axis_index("col")
    y, x = col // RING, col % RING
    pos = jnp.stack([y, x]).astype(jnp.int32)
    steps = jnp.arange(n_peer, dtype=jnp.int32)
    outer, inner = steps // RING, steps % RING
    orders = (wrap(y + inner) * RING + wrap(x + outer), wrap(y + outer) * RING + wrap(x + inner))
    axes = (("x", "y"), ("y", "x"))

    table = jnp.concatenate([msg_dst, msg_count], axis=1).reshape(-1)
    table = spread(table, "col", n_col).reshape(n_col, n_col * 2 * cap)
    share = docs.shape[0] // n_col
    regroup = lambda a: a.reshape((n_row, n_col, share) + a.shape[1:]).swapaxes(0, 1).reshape(a.shape)
    gathered = spread(docs, "row", n_row).reshape(n_doc, width)
    all_docs = regroup(gathered)
    base = (lax.axis_index("row") * n_col + col) * label_dev
    labels = regroup(doc_labels).T - base

    n_chunk = len(CHUNK_ROWS)
    starts = [sum(CHUNK_ROWS[:k]) for k in range(n_chunk)]
    came = [[None, None] for _ in CHUNK_ROWS]
    lows = [[None, None] for _ in CHUNK_ROWS]
    ends = [[None, None] for _ in CHUNK_ROWS]

    def send(k):
        for half in range(2):
            after = {(0, 1): [table], (1, 1): [gathered]}.get((k, half), [])
            after = after + lows[k - 2] if k >= 2 else after
            out = messages_of(orders[half], msg_src, blocks, tiles,
                        starts[k], CHUNK_ROWS[k], half, after)
            came[k][half] = [out[0]] + [shift(out[j], axes[half][0], j) for j in range(1, RING)]

    def combine(k):
        for half in range(2):
            second = axes[half][1]
            after = [came[k + 1][h][0] for h in range(2)] if k + 1 < n_chunk else []
            low, high = far_sums(half, pos, table, came[k][half],
                              blk_dev, after)
            lows[k][half] = low
            ends[k][half] = (shift(low, second, 1),
                             shift(high, second, -1))

    send(0)
    for k in range(n_chunk):
        if k + 1 < n_chunk:
            send(k + 1)
        combine(k)

    arrive = lax.dynamic_slice_in_dim(table, col * 2 * cap, 2 * cap, 1)
    dst = arrive[:, :cap].reshape(-1)
    cnt = arrive[:, cap:].reshape(-1).astype(F32)
    hot = dst[None, :] == jnp.arange(blk_dev, dtype=jnp.int32)[:, None]
    inv = 1.0 / (float(blk) + jnp.sum(jnp.where(hot, cnt[None, :], 0.0), axis=1))
    group = jnp.where((labels >= 0) & (labels < label_dev), labels // STEP_ROWS, -1).reshape(-1)
    near = jnp.max((group[None, :] == jnp.arange(label_dev // STEP_ROWS)[:, None]).astype(jnp.int32),
                   axis=1)

    carry = None
    for k, row in enumerate(starts):
        sums = []
        for half in range(2):
            second = axes[half][1]
            up, down = near_sums(half, pos, table, came[k][half],
                             *ends[k][half])
            sums.append((shift(up, second, 1),
                         shift(down, second, -1)))
        carry = head(pos, table, inv, near, came[k], sums, blocks, labels, weight, all_docs, carry,
                     row, labels_total, float(pos_count))
    hidden, gd, gw = carry

    part_of = n_doc // n_col
    lane = width // share
    both = jnp.concatenate([gd, gw], axis=1).astype(BF)
    part = swap(both.reshape(n_col, part_of, 2 * width), "col")
    part = jnp.sum(part.astype(F32), axis=0).astype(BF)
    own = part[:, :width].reshape(n_row, share * share, lane)
    own = jnp.pad(own, ((0, 0), (0, part_of - share * share), (0, 0)))
    out = jnp.broadcast_to(part[None, :, width:], (n_row, part_of, width))
    part = swap(jnp.concatenate([out, own], axis=2), "row")
    part = jnp.sum(part.astype(F32), axis=0).astype(BF)
    whole = spread(part, "col", n_col)
    grad_weight = whole[:, :, :width].reshape(n_doc, width)
    grad_docs = whole[:, :share * share, width:].reshape(docs.shape)
    return hidden.reshape(label_dev, width), grad_docs.astype(F32), grad_weight.astype(F32)


def solution(mesh):
    in_specs = (
        P(("row", "col"), None),
        P(("row", "col"), None, None, None),
        P(("row", "col"), None),
        P(("row", "col"), None),
        P(("row", "col"), None),
        P(),
        P("row", None),
        P(),
    )
    out_specs = (P(("row", "col"), None), P("row", None), P())

    return jax.shard_map(
        per_device, mesh=mesh, in_specs=in_specs, out_specs=out_specs, check_vma=False
    )
```

profile of v0, /device:TPU:0, one launch (start us, length us, event | category | flops | bytes accessed | tf_op | source)
XLA Modules:
  0.0 385.8 jit_solution(14619237320772539327)
XLA Ops:
  2.6 8.3 %shard_map.109 = (bf16[4,4,192,256]{3,2,1,0:T(8,128)(2,1)}, bf16[4,4,192,256]{3,2,1,0:T(8,128)(2,1)}, bf16[4,4,192,256]{3,2,1,0:T(8,128)(2,1)}, bf16[4,4,192,256]{3,2,1,0:T(8,128)(2,1)}) custom-call(s32[16]{0:T(128)} %fusion.8.order_ref, s32[16,4]{1,0:T(8,128)} %copy.54.src_ref, bf16[16,256,512]{2,1,0:T(8,128)(2,1)} %bitcast.37, ...), custom_call_target="tpu_custom_call" | custom-call | tf_op jit(solution)/shard_map/pallas_call | solution.py:52
  12.4 2.7 collective-permute-start.15
  17.4 4.6 %all-to-all-start = ((s32[16,1,128]{2,1,0:T(1,128)}), s32[16,1,128]{2,1,0:T(1,128)S(1)}, u32[]{:S(2)}, u32[]{:S(2)}) async-start(s32[16,1,128]{2,1,0:T(1,128)} %broadcast_in_dim.25), calls=%async_computation | async-start | bytes 16384 | tf_op jit(solution)/shard_map/all_to_all | solution.py:270
  22.6 63.3 %all-to-all-done = s32[16,1,128]{2,1,0:T(1,128)S(1)} async-done(((s32[16,1,128]{2,1,0:T(1,128)}), s32[16,1,128]{2,1,0:T(1,128)S(1)}, u32[]{:S(2)}, u32[]{:S(2)}) %all-to-all-start) | async-done | bytes 8224 | tf_op jit(solution)/shard_map/all_to_all | solution.py:270
  86.5 8.3 %shard_map.110 = (bf16[4,4,192,256]{3,2,1,0:T(8,128)(2,1)}, bf16[4,4,192,256]{3,2,1,0:T(8,128)(2,1)}, bf16[4,4,192,256]{3,2,1,0:T(8,128)(2,1)}, bf16[4,4,192,256]{3,2,1,0:T(8,128)(2,1)}) custom-call(s32[16]{0:T(128)} %fusion.12.order_ref, s32[16,4]{1,0:T(8,128)} %copy.54.src_ref, bf16[16,256,512]{2,1,0:T(8,128)(2,1)} %bitcast.38, ...), custom_call_target="tpu_custom_call" | custom-call | tf_op jit(solution)/shard_map/pallas_call | solution.py:52
  99.5 5.3 %all-to-all-start.1 = ((bf16[8,64,512]{2,1,0:T(8,128)(2,1)}), bf16[8,64,512]{2,1,0:T(8,128)(2,1)}, u32[]{:S(2)}, u32[]{:S(2)}) async-start(bf16[8,64,512]{2,1,0:T(8,128)(2,1)} %broadcast_in_dim.46), calls=%async_computation.1 | async-start | bytes 1048576 | tf_op jit(solution)/shard_map/all_to_all | solution.py:270
  104.8 6.1 %shard_map.103 = (bf16[4,4,64,256]{3,2,1,0:T(8,128)(2,1)}, bf16[4,4,64,256]{3,2,1,0:T(8,128)(2,1)}, bf16[4,4,64,256]{3,2,1,0:T(8,128)(2,1)}, bf16[4,4,64,256]{3,2,1,0:T(8,128)(2,1)}) custom-call(s32[16]{0:T(128)} %fusion.8.order_ref, s32[16,4]{1,0:T(8,128)} %copy.54.src_ref, bf16[16,256,512]{2,1,0:T(8,128)(2,1)} %bitcast.39, ...), custom_call_target="tpu_custom_call" | custom-call | tf_op jit(solution)/shard_map/pallas_call | solution.py:52
  116.6 6.1 %shard_map.104 = (bf16[4,4,64,256]{3,2,1,0:T(8,128)(2,1)}, bf16[4,4,64,256]{3,2,1,0:T(8,128)(2,1)}, bf16[4,4,64,256]{3,2,1,0:T(8,128)(2,1)}, bf16[4,4,64,256]{3,2,1,0:T(8,128)(2,1)}) custom-call(s32[16]{0:T(128)} %fusion.12.order_ref, s32[16,4]{1,0:T(8,128)} %copy.54.src_ref, bf16[16,256,512]{2,1,0:T(8,128)(2,1)} %bitcast.40, ...), custom_call_target="tpu_custom_call" | custom-call | tf_op jit(solution)/shard_map/pallas_call | solution.py:52
  122.7 5.6 %shard_map.111 = (bf16[8,192,256]{2,1,0:T(8,128)(2,1)}, bf16[8,192,256]{2,1,0:T(8,128)(2,1)}) custom-call(s32[2]{0:T(128)} %pad_add_fusion.1.pos_ref, s32[16,128]{1,0:T(8,128)} %bitcast.25, bf16[4,4,192,256]{3,2,1,0:T(8,128)(2,1)} %get-tuple-element.57.refs_0_.refs_4_, bf16[4,4,192,256]{3,2,1,0:T(8,128)(2,1)} %copy-done.23, ...), custom_call_target="tpu_custom_call" | custom-call | tf_op jit(solution)/shard_map/pallas_call | solution.py:132
  128.3 36.1 %collective-permute-done.17.refs_1_.refs_5_ = bf16[4,4,192,256]{3,2,1,0:T(8,128)(2,1)} collective-permute-done((bf16[4,4,192,256]{3,2,1,0:T(8,128)(2,1)}, bf16[4,4,192,256]{3,2,1,0:T(8,128)(2,1)}, u32[]{:S(2)}, u32[]{:S(2)}) %collective-permute-start.17) | collective-permute-done | bytes 1572896 | tf_op jit(solution)/shard_map/ppermute | solution.py:32
  166.6 2.4 collective-permute-start.2
  169.0 3.2 collective-permute-start.21
  172.2 5.6 %shard_map.113 = (bf16[8,192,256]{2,1,0:T(8,128)(2,1)}, bf16[8,192,256]{2,1,0:T(8,128)(2,1)}) custom-call(s32[2]{0:T(128)} %pad_add_fusion.1.pos_ref, s32[16,128]{1,0:T(8,128)} %bitcast.26, bf16[4,4,192,256]{3,2,1,0:T(8,128)(2,1)} %get-tuple-element.61.refs_0_.refs_4_, bf16[4,4,192,256]{3,2,1,0:T(8,128)(2,1)} %collective-permute-done.17.refs_1_.refs_5_, ...), custom_call_target="tpu_custom_call" | custom-call | tf_op jit(solution)/shard_map/pallas_call | solution.py:132
  177.9 3.2 collective-permute-start.25
  181.9 2.5 shard_map.105
  185.9 7.9 %shard_map.112 = (bf16[16,192,256]{2,1,0:T(8,128)(2,1)}, bf16[16,192,256]{2,1,0:T(8,128)(2,1)}) custom-call(s32[2]{0:T(128)} %pad_add_fusion.1.pos_ref, s32[16,128]{1,0:T(8,128)} %bitcast.28, bf16[4,4,192,256]{3,2,1,0:T(8,128)(2,1)} %get-tuple-element.57.refs_0_.refs_4_, bf16[4,4,192,256]{3,2,1,0:T(8,128)(2,1)} %copy-done.23, ...), custom_call_target="tpu_custom_call" | custom-call | tf_op jit(solution)/shard_map/pallas_call | solution.py:148
  197.3 7.9 %shard_map.114 = (bf16[16,192,256]{2,1,0:T(8,128)(2,1)}, bf16[16,192,256]{2,1,0:T(8,128)(2,1)}) custom-call(s32[2]{0:T(128)} %pad_add_fusion.1.pos_ref, s32[16,128]{1,0:T(8,128)} %bitcast.29, bf16[4,4,192,256]{3,2,1,0:T(8,128)(2,1)} %get-tuple-element.61.refs_0_.refs_4_, bf16[4,4,192,256]{3,2,1,0:T(8,128)(2,1)} %collective-permute-done.17.refs_1_.refs_5_, ...), custom_call_target="tpu_custom_call" | custom-call | tf_op jit(solution)/shard_map/pallas_call | solution.py:148
  209.1 33.8 %collective-permute-done.4.refs_2_.refs_6_ = bf16[4,4,64,256]{3,2,1,0:T(8,128)(2,1)S(1)} collective-permute-done((bf16[4,4,64,256]{3,2,1,0:T(8,128)(2,1)S(1)}, bf16[4,4,64,256]{3,2,1,0:T(8,128)(2,1)S(1)}, u32[]{:S(2)}, u32[]{:S(2)}) %collective-permute-start.4) | collective-permute-done | bytes 524320 | tf_op jit(solution)/shard_map/ppermute | solution.py:32
  242.9 3.5 collective-permute-start.27
  246.4 4.8 %collective-permute-done.5.refs_3_.refs_7_ = bf16[4,4,64,256]{3,2,1,0:T(8,128)(2,1)S(1)} collective-permute-done((bf16[4,4,64,256]{3,2,1,0:T(8,128)(2,1)S(1)}, bf16[4,4,64,256]{3,2,1,0:T(8,128)(2,1)S(1)}, u32[]{:S(2)}, u32[]{:S(2)}) %collective-permute-start.5) | collective-permute-done | bytes 524320 | tf_op jit(solution)/shard_map/ppermute | solution.py:32
  251.2 3.4 collective-permute-start.7
  254.5 2.5 shard_map.107
  258.4 4.2 %collective-permute-start.10 = (bf16[8,64,256]{2,1,0:T(8,128)(2,1)}, bf16[8,64,256]{2,1,0:T(8,128)(2,1)S(1)}, u32[]{:S(2)}, u32[]{:S(2)}) collective-permute-start(bf16[8,64,256]{2,1,0:T(8,128)(2,1)} %get-tuple-element.53), channel_id=1, source_target_pairs={{0,1},{1,2},{2,3},{3,0},{4,5},{5,6},{6,7},{7,4},{8,9},{9,10},{10,1... | collective-permute-start | bytes 786440 | tf_op jit(solution)/shard_map/ppermute | solution.py:32
  262.9 5.0 %collective-permute-done.10.refs_8_ = bf16[8,64,256]{2,1,0:T(8,128)(2,1)S(1)} collective-permute-done((bf16[8,64,256]{2,1,0:T(8,128)(2,1)}, bf16[8,64,256]{2,1,0:T(8,128)(2,1)S(1)}, u32[]{:S(2)}, u32[]{:S(2)}) %collective-permute-start.10) | collective-permute-done | bytes 262176 | tf_op jit(solution)/shard_map/ppermute | solution.py:32
  270.5 3.6 shard_map.106
  274.1 10.0 %collective-permute-done.11.refs_9_ = bf16[8,64,256]{2,1,0:T(8,128)(2,1)S(1)} collective-permute-done((bf16[8,64,256]{2,1,0:T(8,128)(2,1)}, bf16[8,64,256]{2,1,0:T(8,128)(2,1)S(1)}, u32[]{:S(2)}, u32[]{:S(2)}) %collective-permute-start.11) | collective-permute-done | bytes 262176 | tf_op jit(solution)/shard_map/ppermute | solution.py:32
  285.1 3.6 shard_map.108
  299.1 23.1 %shard_map.115 = (bf16[16,256,512]{2,1,0:T(8,128)(2,1)}, f32[512,512]{1,0:T(8,128)S(1)}, f32[512,512]{1,0:T(8,128)S(1)}) custom-call(s32[2]{0:T(128)S(1)} %copy-done.22, s32[16,128]{1,0:T(8,128)S(1)} %bitcast.33, f32[16]{0:T(128)S(1)} %add_divide_fusion.inv_ref, s32[128]{0:T(128)S(1)} %convert_reduce_fusion.near_ref, bf16[4,4,192,256]{3,2,1,0:T(8,128)(2,1)S(1)} %copy-done, ...), custom_call_target="tpu_custom_call" | custom-call | tf_op jit(solution)/shard_map/pallas_call | solution.py:251
  324.3 10.7 %shard_map.116 = (bf16[16,256,512]{2,1,0:T(8,128)(2,1)}, f32[512,512]{1,0:T(8,128)}, f32[512,512]{1,0:T(8,128)}) custom-call(s32[2]{0:T(128)S(1)} %copy-done.22, s32[16,128]{1,0:T(8,128)S(1)} %bitcast.34, f32[16]{0:T(128)S(1)} %add_divide_fusion.inv_ref, s32[128]{0:T(128)S(1)} %convert_reduce_fusion.near_ref, ...), custom_call_target="tpu_custom_call", output_to_operand_aliasing={{0}: (22, {})} | custom-call | tf_op jit(solution)/shard_map/pallas_call | solution.py:251
  336.7 18.1 %all_to_all.28 = bf16[16,32,1024]{2,1,0:T(8,128)(2,1)S(1)} all-to-all(bf16[16,32,1024]{2,1,0:T(8,128)(2,1)S(1)} %pad_maximum_fusion), channel_id=1, replica_groups=mesh['row'=8,'col'=16] {'col'}, dimensions={0} | all-to-all | bytes 2097152 | tf_op jit(solution)/shard_map/all_to_all | solution.py:270
  355.2 12.9 %all_to_all.29 = bf16[8,32,640]{2,1,0:T(8,128)(2,1)S(1)} all-to-all(bf16[8,32,640]{2,1,0:T(8,128)(2,1)S(1)} %fusion.1), channel_id=1, replica_groups=mesh['row'=8,'col'=16] {'row'}, dimensions={0} | all-to-all | bytes 655360 | tf_op jit(solution)/shard_map/all_to_all | solution.py:270
  368.2 15.7 %all_to_all.30 = bf16[16,32,640]{2,1,0:T(8,128)(2,1)S(1)} all-to-all(bf16[16,32,640]{2,1,0:T(8,128)(2,1)S(1)} %broadcast_in_dim.48), channel_id=1, replica_groups=mesh['row'=8,'col'=16] {'col'}, dimensions={0} | all-to-all | bytes 1310720 | tf_op jit(solution)/shard_map/all_to_all | solution.py:270
  (165 shorter events, 50.4 us)
Async XLA Ops:
  10.8 86.4 %collective-permute-start.14 = (bf16[4,4,192,256]{3,2,1,0:T(8,128)(2,1)}, bf16[4,4,192,256]{3,2,1,0:T(8,128)(2,1)S(1)}, u32[]{:S(2)}, u32[]{:S(2)}) collective-permute-start(bf16[4,4,192,256]{3,2,1,0:T(8,128)(2,1)} %get-tuple-element.58), channel_id=1, source_target_pairs={{0,1},{1,2},{2,3},{3,0},{4,5},{5,6},{6,7},{7,4},{8,9},{9,10},{10,1... | collective-permute-start | bytes 4718600 | tf_op jit(solution)/shard_map/ppermute | solution.py:32
  12.4 98.5 %collective-permute-start.15 = (bf16[4,4,192,256]{3,2,1,0:T(8,128)(2,1)}, bf16[4,4,192,256]{3,2,1,0:T(8,128)(2,1)S(1)}, u32[]{:S(2)}, u32[]{:S(2)}) collective-permute-start(bf16[4,4,192,256]{3,2,1,0:T(8,128)(2,1)} %get-tuple-element.59), channel_id=1, source_target_pairs={{0,2},{1,3},{2,0},{3,1},{4,6},{5,7},{6,4},{7,5},{8,10},{9,11},{10,... | collective-permute-start | bytes 4718600 | tf_op jit(solution)/shard_map/ppermute | solution.py:32
  15.2 99.0 %collective-permute-start.16 = (bf16[4,4,192,256]{3,2,1,0:T(8,128)(2,1)}, bf16[4,4,192,256]{3,2,1,0:T(8,128)(2,1)}, u32[]{:S(2)}, u32[]{:S(2)}) collective-permute-start(bf16[4,4,192,256]{3,2,1,0:T(8,128)(2,1)} %get-tuple-element.60), channel_id=1, source_target_pairs={{0,3},{1,0},{2,1},{3,2},{4,7},{5,4},{6,5},{7,6},{8,11},{9,8},{10,9... | collective-permute-start | bytes 4718600 | tf_op jit(solution)/shard_map/ppermute | solution.py:32
  17.4 68.5 %all-to-all-start = ((s32[16,1,128]{2,1,0:T(1,128)}), s32[16,1,128]{2,1,0:T(1,128)S(1)}, u32[]{:S(2)}, u32[]{:S(2)}) async-start(s32[16,1,128]{2,1,0:T(1,128)} %broadcast_in_dim.25), calls=%async_computation | async-start | bytes 16384 | tf_op jit(solution)/shard_map/all_to_all | solution.py:270
  94.8 69.7 %collective-permute-start.17 = (bf16[4,4,192,256]{3,2,1,0:T(8,128)(2,1)}, bf16[4,4,192,256]{3,2,1,0:T(8,128)(2,1)}, u32[]{:S(2)}, u32[]{:S(2)}) collective-permute-start(bf16[4,4,192,256]{3,2,1,0:T(8,128)(2,1)} %get-tuple-element.62), channel_id=1, source_target_pairs={{0,4},{1,5},{2,6},{3,7},{4,8},{5,9},{6,10},{7,11},{8,12},{9,13},{1... | collective-permute-start | bytes 4718600 | tf_op jit(solution)/shard_map/ppermute | solution.py:32
  95.4 71.1 %collective-permute-start.18 = (bf16[4,4,192,256]{3,2,1,0:T(8,128)(2,1)}, bf16[4,4,192,256]{3,2,1,0:T(8,128)(2,1)}, u32[]{:S(2)}, u32[]{:S(2)}) collective-permute-start(bf16[4,4,192,256]{3,2,1,0:T(8,128)(2,1)} %get-tuple-element.63), channel_id=1, source_target_pairs={{0,8},{1,9},{2,10},{3,11},{4,12},{5,13},{6,14},{7,15},{8,0},{9,1},... | collective-permute-start | bytes 4718600 | tf_op jit(solution)/shard_map/ppermute | solution.py:32
  97.3 71.7 %collective-permute-start.19 = (bf16[4,4,192,256]{3,2,1,0:T(8,128)(2,1)}, bf16[4,4,192,256]{3,2,1,0:T(8,128)(2,1)}, u32[]{:S(2)}, u32[]{:S(2)}) collective-permute-start(bf16[4,4,192,256]{3,2,1,0:T(8,128)(2,1)} %get-tuple-element.64), channel_id=1, source_target_pairs={{0,12},{1,13},{2,14},{3,15},{4,0},{5,1},{6,2},{7,3},{8,4},{9,5},{1... | collective-permute-start | bytes 4718600 | tf_op jit(solution)/shard_map/ppermute | solution.py:32
  99.5 17.1 %all-to-all-start.1 = ((bf16[8,64,512]{2,1,0:T(8,128)(2,1)}), bf16[8,64,512]{2,1,0:T(8,128)(2,1)}, u32[]{:S(2)}, u32[]{:S(2)}) async-start(bf16[8,64,512]{2,1,0:T(8,128)(2,1)} %broadcast_in_dim.46), calls=%async_computation.1 | async-start | bytes 1048576 | tf_op jit(solution)/shard_map/all_to_all | solution.py:270
  112.1 65.6 %collective-permute-start = (bf16[4,4,64,256]{3,2,1,0:T(8,128)(2,1)}, bf16[4,4,64,256]{3,2,1,0:T(8,128)(2,1)S(1)}, u32[]{:S(2)}, u32[]{:S(2)}) collective-permute-start(bf16[4,4,64,256]{3,2,1,0:T(8,128)(2,1)} %get-tuple-element.42), channel_id=1, source_target_pairs={{0,1},{1,2},{2,3},{3,0},{4,5},{5,6},{6,7},{7,4},{8,9},{9,10},{10,1... | collective-permute-start | bytes 1572872 | tf_op jit(solution)/shard_map/ppermute | solution.py:32
  114.2 63.7 %collective-permute-start.1 = (bf16[4,4,64,256]{3,2,1,0:T(8,128)(2,1)}, bf16[4,4,64,256]{3,2,1,0:T(8,128)(2,1)S(1)}, u32[]{:S(2)}, u32[]{:S(2)}) collective-permute-start(bf16[4,4,64,256]{3,2,1,0:T(8,128)(2,1)} %get-tuple-element.43), channel_id=1, source_target_pairs={{0,2},{1,3},{2,0},{3,1},{4,6},{5,7},{6,4},{7,5},{8,10},{9,11},{10,... | collective-permute-start | bytes 1572872 | tf_op jit(solution)/shard_map/ppermute | solution.py:32
  164.4 20.0 %collective-permute-start.20 = (bf16[8,192,256]{2,1,0:T(8,128)(2,1)}, bf16[8,192,256]{2,1,0:T(8,128)(2,1)S(1)}, u32[]{:S(2)}, u32[]{:S(2)}) collective-permute-start(bf16[8,192,256]{2,1,0:T(8,128)(2,1)} %get-tuple-element.65), channel_id=1, source_target_pairs={{0,4},{1,5},{2,6},{3,7},{4,8},{5,9},{6,10},{7,11},{8,12},{9,13},{1... | collective-permute-start | bytes 2359304 | tf_op jit(solution)/shard_map/ppermute | solution.py:32
  166.6 14.5 %collective-permute-start.2 = (bf16[4,4,64,256]{3,2,1,0:T(8,128)(2,1)S(1)}, bf16[4,4,64,256]{3,2,1,0:T(8,128)(2,1)S(1)}, u32[]{:S(2)}, u32[]{:S(2)}) collective-permute-start(bf16[4,4,64,256]{3,2,1,0:T(8,128)(2,1)S(1)} %copy-done.37), channel_id=1, source_target_pairs={{0,3},{1,0},{2,1},{3,2},{4,7},{5,4},{6,5},{7,6},{8,11},{9,8},{10,9... | collective-permute-start | bytes 1572872 | tf_op jit(solution)/shard_map/ppermute | solution.py:32
  169.0 16.9 %collective-permute-start.21 = (bf16[8,192,256]{2,1,0:T(8,128)(2,1)}, bf16[8,192,256]{2,1,0:T(8,128)(2,1)}, u32[]{:S(2)}, u32[]{:S(2)}) collective-permute-start(bf16[8,192,256]{2,1,0:T(8,128)(2,1)} %get-tuple-element.66), channel_id=1, source_target_pairs={{0,12},{1,13},{2,14},{3,15},{4,0},{5,1},{6,2},{7,3},{8,4},{9,5},{1... | collective-permute-start | bytes 2359304 | tf_op jit(solution)/shard_map/ppermute | solution.py:32
  177.8 17.2 %collective-permute-start.24 = (bf16[8,192,256]{2,1,0:T(8,128)(2,1)}, bf16[8,192,256]{2,1,0:T(8,128)(2,1)}, u32[]{:S(2)}, u32[]{:S(2)}) collective-permute-start(bf16[8,192,256]{2,1,0:T(8,128)(2,1)} %get-tuple-element.69), channel_id=1, source_target_pairs={{0,1},{1,2},{2,3},{3,0},{4,5},{5,6},{6,7},{7,4},{8,9},{9,10},{10,1... | collective-permute-start | bytes 2359304 | tf_op jit(solution)/shard_map/ppermute | solution.py:32
  177.9 19.4 %collective-permute-start.25 = (bf16[8,192,256]{2,1,0:T(8,128)(2,1)}, bf16[8,192,256]{2,1,0:T(8,128)(2,1)}, u32[]{:S(2)}, u32[]{:S(2)}) collective-permute-start(bf16[8,192,256]{2,1,0:T(8,128)(2,1)} %get-tuple-element.70), channel_id=1, source_target_pairs={{0,3},{1,0},{2,1},{3,2},{4,7},{5,4},{6,5},{7,6},{8,11},{9,8},{10,9... | collective-permute-start | bytes 2359304 | tf_op jit(solution)/shard_map/ppermute | solution.py:32
  181.1 27.4 %collective-permute-start.3 = (bf16[4,4,64,256]{3,2,1,0:T(8,128)(2,1)}, bf16[4,4,64,256]{3,2,1,0:T(8,128)(2,1)S(1)}, u32[]{:S(2)}, u32[]{:S(2)}) collective-permute-start(bf16[4,4,64,256]{3,2,1,0:T(8,128)(2,1)} %get-tuple-element.46), channel_id=1, source_target_pairs={{0,4},{1,5},{2,6},{3,7},{4,8},{5,9},{6,10},{7,11},{8,12},{9,13},{1... | collective-permute-start | bytes 1572872 | tf_op jit(solution)/shard_map/ppermute | solution.py:32
  184.4 22.6 %collective-permute-start.6 = (bf16[8,64,256]{2,1,0:T(8,128)(2,1)}, bf16[8,64,256]{2,1,0:T(8,128)(2,1)S(1)}, u32[]{:S(2)}, u32[]{:S(2)}) collective-permute-start(bf16[8,64,256]{2,1,0:T(8,128)(2,1)} %get-tuple-element.49), channel_id=1, source_target_pairs={{0,4},{1,5},{2,6},{3,7},{4,8},{5,9},{6,10},{7,11},{8,12},{9,13},{1... | collective-permute-start | bytes 786440 | tf_op jit(solution)/shard_map/ppermute | solution.py:32
  193.9 94.8 %collective-permute-start.22 = (bf16[16,192,256]{2,1,0:T(8,128)(2,1)}, bf16[16,192,256]{2,1,0:T(8,128)(2,1)}, u32[]{:S(2)}, u32[]{:S(2)}) collective-permute-start(bf16[16,192,256]{2,1,0:T(8,128)(2,1)} %get-tuple-element.67), channel_id=1, source_target_pairs={{0,4},{1,5},{2,6},{3,7},{4,8},{5,9},{6,10},{7,11},{8,12},{9,13},{1... | collective-permute-start | bytes 4718600 | tf_op jit(solution)/shard_map/ppermute | solution.py:32
  195.0 96.0 %collective-permute-start.23 = (bf16[16,192,256]{2,1,0:T(8,128)(2,1)}, bf16[16,192,256]{2,1,0:T(8,128)(2,1)}, u32[]{:S(2)}, u32[]{:S(2)}) collective-permute-start(bf16[16,192,256]{2,1,0:T(8,128)(2,1)} %get-tuple-element.68), channel_id=1, source_target_pairs={{0,12},{1,13},{2,14},{3,15},{4,0},{5,1},{6,2},{7,3},{8,4},{9,5},{1... | collective-permute-start | bytes 4718600 | tf_op jit(solution)/shard_map/ppermute | solution.py:32
  205.2 57.4 %copy-start.32 = (s32[512,8]{0,1:T(8,128)S(1)}, s32[512,8]{0,1:T(8,128)}, u32[]{:S(2)}) copy-start(s32[512,8]{0,1:T(8,128)} %param.15) | copy-start | bytes 49156
  205.2 87.5 %collective-permute-start.26 = (bf16[16,192,256]{2,1,0:T(8,128)(2,1)}, bf16[16,192,256]{2,1,0:T(8,128)(2,1)}, u32[]{:S(2)}, u32[]{:S(2)}) collective-permute-start(bf16[16,192,256]{2,1,0:T(8,128)(2,1)} %get-tuple-element.71), channel_id=1, source_target_pairs={{0,1},{1,2},{2,3},{3,0},{4,5},{5,6},{6,7},{7,4},{8,9},{9,10},{10,1... | collective-permute-start | bytes 4718600 | tf_op jit(solution)/shard_map/ppermute | solution.py:32
  207.0 63.5 %copy-start.27 = (bf16[8,64,256]{2,1,0:T(8,128)(2,1)}, bf16[8,64,256]{2,1,0:T(8,128)(2,1)S(1)}, u32[]{:S(2)}) copy-start(bf16[8,64,256]{2,1,0:T(8,128)(2,1)S(1)} %collective-permute-done.6.refs_8_) | copy-start | bytes 786436
  207.0 36.0 %collective-permute-start.4 = (bf16[4,4,64,256]{3,2,1,0:T(8,128)(2,1)S(1)}, bf16[4,4,64,256]{3,2,1,0:T(8,128)(2,1)S(1)}, u32[]{:S(2)}, u32[]{:S(2)}) collective-permute-start(bf16[4,4,64,256]{3,2,1,0:T(8,128)(2,1)S(1)} %copy-done.36), channel_id=1, source_target_pairs={{0,8},{1,9},{2,10},{3,11},{4,12},{5,13},{6,14},{7,15},{8,0},{9,1},... | collective-permute-start | bytes 1572872 | tf_op jit(solution)/shard_map/ppermute | solution.py:32
  208.5 42.6 %collective-permute-start.5 = (bf16[4,4,64,256]{3,2,1,0:T(8,128)(2,1)S(1)}, bf16[4,4,64,256]{3,2,1,0:T(8,128)(2,1)S(1)}, u32[]{:S(2)}, u32[]{:S(2)}) collective-permute-start(bf16[4,4,64,256]{3,2,1,0:T(8,128)(2,1)S(1)} %copy-done.35), channel_id=1, source_target_pairs={{0,12},{1,13},{2,14},{3,15},{4,0},{5,1},{6,2},{7,3},{8,4},{9,5},{1... | collective-permute-start | bytes 1572872 | tf_op jit(solution)/shard_map/ppermute | solution.py:32
  242.9 56.0 %collective-permute-start.27 = (bf16[16,192,256]{2,1,0:T(8,128)(2,1)}, bf16[16,192,256]{2,1,0:T(8,128)(2,1)}, u32[]{:S(2)}, u32[]{:S(2)}) collective-permute-start(bf16[16,192,256]{2,1,0:T(8,128)(2,1)} %get-tuple-element.72), channel_id=1, source_target_pairs={{0,3},{1,0},{2,1},{3,2},{4,7},{5,4},{6,5},{7,6},{8,11},{9,8},{10,9... | collective-permute-start | bytes 4718600 | tf_op jit(solution)/shard_map/ppermute | solution.py:32
  251.2 7.2 %collective-permute-start.7 = (bf16[8,64,256]{2,1,0:T(8,128)(2,1)S(1)}, bf16[8,64,256]{2,1,0:T(8,128)(2,1)S(1)}, u32[]{:S(2)}, u32[]{:S(2)}) collective-permute-start(bf16[8,64,256]{2,1,0:T(8,128)(2,1)S(1)} %copy-done.38), channel_id=1, source_target_pairs={{0,12},{1,13},{2,14},{3,15},{4,0},{5,1},{6,2},{7,3},{8,4},{9,5},{1... | collective-permute-start | bytes 786440 | tf_op jit(solution)/shard_map/ppermute | solution.py:32
  258.4 9.5 %collective-permute-start.10 = (bf16[8,64,256]{2,1,0:T(8,128)(2,1)}, bf16[8,64,256]{2,1,0:T(8,128)(2,1)S(1)}, u32[]{:S(2)}, u32[]{:S(2)}) collective-permute-start(bf16[8,64,256]{2,1,0:T(8,128)(2,1)} %get-tuple-element.53), channel_id=1, source_target_pairs={{0,1},{1,2},{2,3},{3,0},{4,5},{5,6},{6,7},{7,4},{8,9},{9,10},{10,1... | collective-permute-start | bytes 786440 | tf_op jit(solution)/shard_map/ppermute | solution.py:32
  267.9 16.2 %collective-permute-start.11 = (bf16[8,64,256]{2,1,0:T(8,128)(2,1)}, bf16[8,64,256]{2,1,0:T(8,128)(2,1)S(1)}, u32[]{:S(2)}, u32[]{:S(2)}) collective-permute-start(bf16[8,64,256]{2,1,0:T(8,128)(2,1)} %get-tuple-element.54), channel_id=1, source_target_pairs={{0,3},{1,0},{2,1},{3,2},{4,7},{5,4},{6,5},{7,6},{8,11},{9,8},{10,9... | collective-permute-start | bytes 786440 | tf_op jit(solution)/shard_map/ppermute | solution.py:32
  284.1 40.1 %collective-permute-start.8 = (bf16[16,64,256]{2,1,0:T(8,128)(2,1)}, bf16[16,64,256]{2,1,0:T(8,128)(2,1)S(1)}, u32[]{:S(2)}, u32[]{:S(2)}) collective-permute-start(bf16[16,64,256]{2,1,0:T(8,128)(2,1)} %get-tuple-element.51), channel_id=1, source_target_pairs={{0,4},{1,5},{2,6},{3,7},{4,8},{5,9},{6,10},{7,11},{8,12},{9,13},{1... | collective-permute-start | bytes 1572872 | tf_op jit(solution)/shard_map/ppermute | solution.py:32
  288.7 35.5 %collective-permute-start.9 = (bf16[16,64,256]{2,1,0:T(8,128)(2,1)}, bf16[16,64,256]{2,1,0:T(8,128)(2,1)}, u32[]{:S(2)}, u32[]{:S(2)}) collective-permute-start(bf16[16,64,256]{2,1,0:T(8,128)(2,1)} %get-tuple-element.52), channel_id=1, source_target_pairs={{0,12},{1,13},{2,14},{3,15},{4,0},{5,1},{6,2},{7,3},{8,4},{9,5},{1... | collective-permute-start | bytes 1572872 | tf_op jit(solution)/shard_map/ppermute | solution.py:32
  291.0 33.2 %collective-permute-start.12 = (bf16[16,64,256]{2,1,0:T(8,128)(2,1)}, bf16[16,64,256]{2,1,0:T(8,128)(2,1)}, u32[]{:S(2)}, u32[]{:S(2)}) collective-permute-start(bf16[16,64,256]{2,1,0:T(8,128)(2,1)} %get-tuple-element.55), channel_id=1, source_target_pairs={{0,1},{1,2},{2,3},{3,0},{4,5},{5,6},{6,7},{7,4},{8,9},{9,10},{10,1... | collective-permute-start | bytes 1572872 | tf_op jit(solution)/shard_map/ppermute | solution.py:32
  292.7 31.5 %collective-permute-start.13 = (bf16[16,64,256]{2,1,0:T(8,128)(2,1)}, bf16[16,64,256]{2,1,0:T(8,128)(2,1)}, u32[]{:S(2)}, u32[]{:S(2)}) collective-permute-start(bf16[16,64,256]{2,1,0:T(8,128)(2,1)} %get-tuple-element.56), channel_id=1, source_target_pairs={{0,3},{1,0},{2,1},{3,2},{4,7},{5,4},{6,5},{7,6},{8,11},{9,8},{10,9... | collective-permute-start | bytes 1572872 | tf_op jit(solution)/shard_map/ppermute | solution.py:32
  (37 other events, 533.3 us)
where the time goes:
time: 388 us; the launch traced here: 386 us
  waiting for transfers between devices  159 us (41%)
  Pallas kernels  102 us (26%)
  starting transfers between devices  58.5 us (15%)
  blocking collectives  46.8 us (12%)
  local copies, waits for them, and re-layouts  13 us (3%)
  other arithmetic  5.34 us (1%)
    ppermute x28, waiting for transfers between devices, shift(): return lax.ppermute(v, 'col', shift_pairs(axis, by))  95.7 us
    all_to_all x2, waiting for transfers between devices, swap(): return lax.all_to_all(x, axis, split_axis=0, concat_axis=0, tiled=True)  63.3 us
    ppermute x28, starting transfers between devices, shift(): return lax.ppermute(v, 'col', shift_pairs(axis, by))  48.5 us
    all_to_all x3, blocking collectives, swap(): return lax.all_to_all(x, axis, split_axis=0, concat_axis=0, tiled=True)  46.8 us
    pallas_call x2, Pallas kernels, head(): pl.pallas_call(functools.partial(head_kernel, first, row, blk, labels_tot...  33.8 us
    pallas_call x4, Pallas kernels, messages_of(): pl.pallas_call(message_kernel, grid_spec=pltpu.PrefetchScalarGridSpec(num...  28.8 us
    pallas_call x4, Pallas kernels, near_sums(): pl.pallas_call(functools.partial(near_kernel, half), grid=(rows // step_r...  23.1 us
    pallas_call x4, Pallas kernels, far_sums(): pl.pallas_call(functools.partial(far_kernel, half), grid=(rows // step_ro...  16.2 us
  transfers between devices with their start and end apart: 30, of which 10 were waited for; matrix products, arithmetic and copies ran while one was open for 2% of the time, Pallas kernels for 22%

commit v1 on v0

--- a/solution.py
+++ b/solution.py
@@ -10,8 +10,9 @@
 
 BF = jnp.bfloat16
 F32 = jnp.float32
-CHUNK_ROWS = (192, 64)
-STEP_ROWS = 32
+CHUNK_ROWS = (128, 128)
+SUM_ROWS = 128
+STEP_ROWS = 64
 RING = 4
 
 
@@ -127,7 +128,7 @@
 
 def far_sums(half, pos, table, parts, n_blk, after):
     _, _, rows, cols = parts[0].shape
-    step_rows = min(STEP_ROWS, rows)
+    step_rows = min(SUM_ROWS, rows)
     n = n_blk // 2
     return pl.pallas_call(
         functools.partial(far_kernel, half),
@@ -142,7 +143,7 @@
 
 def near_sums(half, pos, table, parts, low, high):
     _, _, rows, cols = parts[0].shape
-    step_rows = min(STEP_ROWS, rows)
+    step_rows = min(SUM_ROWS, rows)
     n = low.shape[0]
     rowed = lambda k: pl.BlockSpec((k, step_rows, cols), lambda i: (0, i, 0))
     return pl.pallas_call(
@@ -156,17 +157,20 @@
     )(pos, table, *parts, *parts, low, high)
 
 
-def head_kernel(first, row, blk, labels_total, pos_count,
+def head_kernel(first, last, row, blk, labels_total, pos_count,
                 pos_ref, table_ref, inv_ref, near_ref, *refs):
     mine = (refs[:RING], refs[RING:2 * RING])
     refs = refs[2 * RING:]
     sums = (refs[:2], refs[2:4])
     emb_ref, labels_ref, w_ref, docs_ref = refs[4:8]
     rest = refs[8:]
-    if first:
+    if not first:
+        gd_in, gw_in, _ = rest[:3]
+        rest = rest[3:]
+    if last:
+        hid_ref, both_ref, acc_ref, agg_ref, ds_ref, gd_ref, gw_ref = rest
+    else:
         hid_ref, gd_ref, gw_ref, acc_ref, agg_ref, ds_ref = rest
-    else:
-        gd_in, gw_in, _, hid_ref, gd_ref, gw_ref, acc_ref, agg_ref, ds_ref = rest
     step = pl.program_id(0)
 
     @pl.when(step == 0)
@@ -220,10 +224,15 @@
     dpre = (dhid * sig * (1.0 + pre * (1.0 - sig))).astype(BF)
     gw_ref[...] += lax.dot_general(agg, dpre, (((0,), (0,)), ((), ())),
                                    preferred_element_type=F32)
+    if last:
+        @pl.when(step == pl.num_programs(0) - 1)
+        def _():
+            both_ref[:, :width] = gd_ref[...].astype(BF)
+            both_ref[:, width:] = gw_ref[...].astype(BF)
 
 
 def head(pos, table, inv, near, mine, sums, blocks, labels, weight, docs, carry, row,
-         labels_total, pos_count):
+         last, labels_total, pos_count):
     n_blk, blk, width = blocks.shape
     rows = mine[0][0].shape[2]
     step_rows = min(STEP_ROWS, rows)
@@ -248,19 +257,18 @@
         in_specs += [full(gd.shape), full(gw.shape), pl.BlockSpec(memory_space=pl.ANY)]
         aliases = {len(args) + 2: 0}
         args += [gd, gw, hid]
+    grads = [((n_doc, 2 * width), BF)] if last else [((n_doc, width), F32), ((width, width), F32)]
     return pl.pallas_call(
-        functools.partial(head_kernel, first, row, blk, labels_total, pos_count),
+        functools.partial(head_kernel, first, last, row, blk, labels_total, pos_count),
         grid=(rows // step_rows,),
         in_specs=in_specs,
-        out_specs=[rowed(width),
-                   pl.BlockSpec((n_doc, width), lambda i: (0, 0)),
-                   pl.BlockSpec((width, width), lambda i: (0, 0))],
-        out_shape=[jax.ShapeDtypeStruct(blocks.shape, BF),
-                   jax.ShapeDtypeStruct((n_doc, width), F32),
-                   jax.ShapeDtypeStruct((width, width), F32)],
+        out_specs=[rowed(width)] + [pl.BlockSpec(a, lambda i: (0, 0)) for a, _ in grads],
+        out_shape=[jax.ShapeDtypeStruct(blocks.shape, BF)]
+        + [jax.ShapeDtypeStruct(a, t) for a, t in grads],
         scratch_shapes=[pltpu.VMEM((n_blk, step_rows, width), F32),
                         pltpu.VMEM((n_blk * step_rows, width), BF),
-                        pltpu.VMEM((n_blk * step_rows, n_doc), BF)],
+                        pltpu.VMEM((n_blk * step_rows, n_doc), BF)]
+        + ([pltpu.VMEM((n_doc, width), F32), pltpu.VMEM((width, width), F32)] if last else []),
         input_output_aliases=aliases,
         compiler_params=pltpu.CompilerParams(vmem_limit_bytes=48 << 20),
     )(*args)
@@ -350,12 +358,11 @@
             sums.append((shift(up, second, 1),
                          shift(down, second, -1)))
         carry = head(pos, table, inv, near, came[k], sums, blocks, labels, weight, all_docs, carry,
-                     row, labels_total, float(pos_count))
-    hidden, gd, gw = carry
+                     row, k == n_chunk - 1, labels_total, float(pos_count))
+    hidden, both = carry
 
     part_of = n_doc // n_col
     lane = width // share
-    both = jnp.concatenate([gd, gw], axis=1).astype(BF)
     part = swap(both.reshape(n_col, part_of, 2 * width), "col")
     part = jnp.sum(part.astype(F32), axis=0).astype(BF)
     own = part[:, :width].reshape(n_row, share * share, lane)

time: 388 us -> 353 us (0.910)
  Pallas kernels: 102 us -> 85.3 us
  starting transfers between devices: 58.5 us -> 43.9 us
    ppermute x28, starting transfers between devices: 48.5 us -> 31.9 us  [shift(): return lax.ppermute(v, 'col', shift_pairs(axis, by))]
    ppermute x28, waiting for transfers between devices: 95.7 us -> 103 us  [shift(): return lax.ppermute(v, 'col', shift_pairs(axis, by))]
    all_to_all x2, waiting for transfers between devices: 63.3 us -> 56.3 us  [swap(): return lax.all_to_all(x, axis, split_axis=0, concat_axis=0, tiled=True)]
    pallas_call x4, Pallas kernels: 23.1 us -> 17.2 us  [near_sums(): pl.pallas_call(functools.partial(near_kernel, half), grid=(rows // step_r...]
    pallas_call x4, Pallas kernels: 16.2 us -> 11 us  [far_sums(): pl.pallas_call(functools.partial(far_kernel, half), grid=(rows // step_ro...]
    pallas_call x2, Pallas kernels: 33.8 us -> 29.7 us  [head(): pl.pallas_call(functools.partial(head_kernel, first, last, row, blk, labe...]
  transfers between devices with their start and end apart: 30 -> 30, of which waited for: 10 -> 17; matrix products, arithmetic and copies ran while one was open for 2% -> 2% of each run, Pallas kernels for 22% -> 18%
where the time goes in v1:
time: 353 us; the launch traced here: 352 us
  waiting for transfers between devices  159 us (45%)
  Pallas kernels  85.3 us (24%)
  blocking collectives  48.2 us (14%)
  starting transfers between devices  43.9 us (12%)
  local copies, waits for them, and re-layouts  11 us (3%)
  other arithmetic  3.58 us (1%)
    ppermute x28, waiting for transfers between devices, shift(): return lax.ppermute(v, 'col', shift_pairs(axis, by))  103 us
    all_to_all x2, waiting for transfers between devices, swap(): return lax.all_to_all(x, axis, split_axis=0, concat_axis=0, tiled=True)  56.3 us
    all_to_all x3, blocking collectives, swap(): return lax.all_to_all(x, axis, split_axis=0, concat_axis=0, tiled=True)  48.2 us
    ppermute x28, starting transfers between devices, shift(): return lax.ppermute(v, 'col', shift_pairs(axis, by))  31.9 us
    pallas_call x2, Pallas kernels, head(): pl.pallas_call(functools.partial(head_kernel, first, last, row, blk, labe...  29.7 us
    pallas_call x4, Pallas kernels, messages_of(): pl.pallas_call(message_kernel, grid_spec=pltpu.PrefetchScalarGridSpec(num...  27.4 us
    pallas_call x4, Pallas kernels, near_sums(): pl.pallas_call(functools.partial(near_kernel, half), grid=(rows // step_r...  17.2 us
    all_to_all x2, starting transfers between devices, swap(): return lax.all_to_all(x, axis, split_axis=0, concat_axis=0, tiled=True)  12 us
  transfers between devices with their start and end apart: 30, of which 17 were waited for; matrix products, arithmetic and copies ran while one was open for 2% of the time, Pallas kernels for 18%

profile of v1, /device:TPU:0, one launch (start us, length us, event | category | flops | bytes accessed | tf_op | source)
XLA Modules:
  0.0 352.0 jit_solution(18372112963233598499)
XLA Ops:
  2.5 6.8 %shard_map.109 = (bf16[4,4,128,256]{3,2,1,0:T(8,128)(2,1)}, bf16[4,4,128,256]{3,2,1,0:T(8,128)(2,1)}, bf16[4,4,128,256]{3,2,1,0:T(8,128)(2,1)}, bf16[4,4,128,256]{3,2,1,0:T(8,128)(2,1)}) custom-call(s32[16]{0:T(128)} %fusion.8.order_ref, s32[16,4]{1,0:T(8,128)} %copy.54.src_ref, bf16[16,256,512]{2,1,0:T(8,128)(2,1)} %bitcast.37, ...), custom_call_target="tpu_custom_call" | custom-call | tf_op jit(solution)/shard_map/pallas_call | solution.py:53
  15.1 6.8 %shard_map.103 = (bf16[4,4,128,256]{3,2,1,0:T(8,128)(2,1)}, bf16[4,4,128,256]{3,2,1,0:T(8,128)(2,1)}, bf16[4,4,128,256]{3,2,1,0:T(8,128)(2,1)}, bf16[4,4,128,256]{3,2,1,0:T(8,128)(2,1)}) custom-call(s32[16]{0:T(128)} %fusion.8.order_ref, s32[16,4]{1,0:T(8,128)} %copy.54.src_ref, bf16[16,256,512]{2,1,0:T(8,128)(2,1)} %bitcast.38, ...), custom_call_target="tpu_custom_call" | custom-call | tf_op jit(solution)/shard_map/pallas_call | solution.py:53
  23.3 6.7 %all-to-all-start = ((s32[16,1,128]{2,1,0:T(1,128)}), s32[16,1,128]{2,1,0:T(1,128)S(1)}, u32[]{:S(2)}, u32[]{:S(2)}) async-start(s32[16,1,128]{2,1,0:T(1,128)} %broadcast_in_dim.25), calls=%async_computation | async-start | bytes 16384 | tf_op jit(solution)/shard_map/all_to_all | solution.py:278
  30.0 3.4 collective-permute-start.1
  33.4 4.5 %collective-permute-done.14.refs_1_.refs_5_ = bf16[4,4,128,256]{3,2,1,0:T(8,128)(2,1)S(1)} collective-permute-done((bf16[4,4,128,256]{3,2,1,0:T(8,128)(2,1)}, bf16[4,4,128,256]{3,2,1,0:T(8,128)(2,1)S(1)}, u32[]{:S(2)}, u32[]{:S(2)}) %collective-permute-start.14) | collective-permute-done | bytes 1048608 | tf_op jit(solution)/shard_map/ppermute | solution.py:33
  39.0 46.5 %all-to-all-done = s32[16,1,128]{2,1,0:T(1,128)S(1)} async-done(((s32[16,1,128]{2,1,0:T(1,128)}), s32[16,1,128]{2,1,0:T(1,128)S(1)}, u32[]{:S(2)}, u32[]{:S(2)}) %all-to-all-start) | async-done | bytes 8224 | tf_op jit(solution)/shard_map/all_to_all | solution.py:278
  86.1 7.0 %shard_map.110 = (bf16[4,4,128,256]{3,2,1,0:T(8,128)(2,1)}, bf16[4,4,128,256]{3,2,1,0:T(8,128)(2,1)}, bf16[4,4,128,256]{3,2,1,0:T(8,128)(2,1)}, bf16[4,4,128,256]{3,2,1,0:T(8,128)(2,1)}) custom-call(s32[16]{0:T(128)} %fusion.12.order_ref, s32[16,4]{1,0:T(8,128)} %copy.54.src_ref, bf16[16,256,512]{2,1,0:T(8,128)(2,1)} %bitcast.39, ...), custom_call_target="tpu_custom_call" | custom-call | tf_op jit(solution)/shard_map/pallas_call | solution.py:53
  98.0 5.3 %all-to-all-start.1 = ((bf16[8,64,512]{2,1,0:T(8,128)(2,1)}), bf16[8,64,512]{2,1,0:T(8,128)(2,1)}, u32[]{:S(2)}, u32[]{:S(2)}) async-start(bf16[8,64,512]{2,1,0:T(8,128)(2,1)} %broadcast_in_dim.46), calls=%async_computation.1 | async-start | bytes 1048576 | tf_op jit(solution)/shard_map/all_to_all | solution.py:278
  103.9 9.8 %all-to-all-done.1 = bf16[8,64,512]{2,1,0:T(8,128)(2,1)} async-done(((bf16[8,64,512]{2,1,0:T(8,128)(2,1)}), bf16[8,64,512]{2,1,0:T(8,128)(2,1)}, u32[]{:S(2)}, u32[]{:S(2)}) %all-to-all-start.1) | async-done | bytes 524320 | tf_op jit(solution)/shard_map/all_to_all | solution.py:278
  113.7 6.8 %shard_map.104 = (bf16[4,4,128,256]{3,2,1,0:T(8,128)(2,1)}, bf16[4,4,128,256]{3,2,1,0:T(8,128)(2,1)}, bf16[4,4,128,256]{3,2,1,0:T(8,128)(2,1)}, bf16[4,4,128,256]{3,2,1,0:T(8,128)(2,1)}) custom-call(s32[16]{0:T(128)} %fusion.12.order_ref, s32[16,4]{1,0:T(8,128)} %copy.54.src_ref, bf16[16,256,512]{2,1,0:T(8,128)(2,1)} %bitcast.40, ...), custom_call_target="tpu_custom_call" | custom-call | tf_op jit(solution)/shard_map/pallas_call | solution.py:53
  126.6 11.3 %collective-permute-done.17.refs_1_.refs_5_ = bf16[4,4,128,256]{3,2,1,0:T(8,128)(2,1)S(1)} collective-permute-done((bf16[4,4,128,256]{3,2,1,0:T(8,128)(2,1)}, bf16[4,4,128,256]{3,2,1,0:T(8,128)(2,1)S(1)}, u32[]{:S(2)}, u32[]{:S(2)}) %collective-permute-start.17) | collective-permute-done | bytes 1048608 | tf_op jit(solution)/shard_map/ppermute | solution.py:33
  137.9 4.7 %collective-permute-done.18.refs_2_.refs_6_ = bf16[4,4,128,256]{3,2,1,0:T(8,128)(2,1)} collective-permute-done((bf16[4,4,128,256]{3,2,1,0:T(8,128)(2,1)}, bf16[4,4,128,256]{3,2,1,0:T(8,128)(2,1)}, u32[]{:S(2)}, u32[]{:S(2)}) %collective-permute-start.18) | collective-permute-done | bytes 1048608 | tf_op jit(solution)/shard_map/ppermute | solution.py:33
  147.0 4.5 %collective-permute-done.20.refs_8_ = bf16[8,128,256]{2,1,0:T(8,128)(2,1)} collective-permute-done((bf16[8,128,256]{2,1,0:T(8,128)(2,1)}, bf16[8,128,256]{2,1,0:T(8,128)(2,1)}, u32[]{:S(2)}, u32[]{:S(2)}) %collective-permute-start.20) | collective-permute-done | bytes 524320 | tf_op jit(solution)/shard_map/ppermute | solution.py:33
  151.5 3.8 %collective-permute-done.21.refs_9_ = bf16[8,128,256]{2,1,0:T(8,128)(2,1)} collective-permute-done((bf16[8,128,256]{2,1,0:T(8,128)(2,1)}, bf16[8,128,256]{2,1,0:T(8,128)(2,1)}, u32[]{:S(2)}, u32[]{:S(2)}) %collective-permute-start.21) | collective-permute-done | bytes 524320 | tf_op jit(solution)/shard_map/ppermute | solution.py:33
  158.7 7.1 %collective-permute-done.24.refs_8_ = bf16[8,128,256]{2,1,0:T(8,128)(2,1)S(1)} collective-permute-done((bf16[8,128,256]{2,1,0:T(8,128)(2,1)}, bf16[8,128,256]{2,1,0:T(8,128)(2,1)S(1)}, u32[]{:S(2)}, u32[]{:S(2)}) %collective-permute-start.24) | collective-permute-done | bytes 524320 | tf_op jit(solution)/shard_map/ppermute | solution.py:33
  167.7 4.2 %collective-permute-start.7 = (bf16[8,128,256]{2,1,0:T(8,128)(2,1)}, bf16[8,128,256]{2,1,0:T(8,128)(2,1)S(1)}, u32[]{:S(2)}, u32[]{:S(2)}) collective-permute-start(bf16[8,128,256]{2,1,0:T(8,128)(2,1)} %get-tuple-element.49), channel_id=1, source_target_pairs={{0,12},{1,13},{2,14},{3,15},{4,0},{5,1},{6,2},{7,3},{8,4},{9,5},{1... | collective-permute-start | bytes 1572872 | tf_op jit(solution)/shard_map/ppermute | solution.py:33
  171.9 4.3 %shard_map.112 = (bf16[16,128,256]{2,1,0:T(8,128)(2,1)}, bf16[16,128,256]{2,1,0:T(8,128)(2,1)}) custom-call(s32[2]{0:T(128)} %pad_add_fusion.1.pos_ref, s32[16,128]{1,0:T(8,128)} %bitcast.27, bf16[4,4,128,256]{3,2,1,0:T(8,128)(2,1)} %get-tuple-element.56.refs_0_.refs_4_, bf16[4,4,128,256]{3,2,1,0:T(8,128)(2,1)} %copy-done.4, ...), custom_call_target="tpu_custom_call" | custom-call | tf_op jit(solution)/shard_map/pallas_call | solution.py:149
  176.1 4.3 %shard_map.114 = (bf16[16,128,256]{2,1,0:T(8,128)(2,1)}, bf16[16,128,256]{2,1,0:T(8,128)(2,1)}) custom-call(s32[2]{0:T(128)} %pad_add_fusion.1.pos_ref, s32[16,128]{1,0:T(8,128)} %bitcast.28, bf16[4,4,128,256]{3,2,1,0:T(8,128)(2,1)} %get-tuple-element.60.refs_0_.refs_4_, bf16[4,4,128,256]{3,2,1,0:T(8,128)(2,1)} %copy-done.14, ...), custom_call_target="tpu_custom_call" | custom-call | tf_op jit(solution)/shard_map/pallas_call | solution.py:149
  180.4 13.6 %collective-permute-done.3.refs_1_.refs_5_ = bf16[4,4,128,256]{3,2,1,0:T(8,128)(2,1)S(1)} collective-permute-done((bf16[4,4,128,256]{3,2,1,0:T(8,128)(2,1)}, bf16[4,4,128,256]{3,2,1,0:T(8,128)(2,1)S(1)}, u32[]{:S(2)}, u32[]{:S(2)}) %collective-permute-start.3) | collective-permute-done | bytes 1048608 | tf_op jit(solution)/shard_map/ppermute | solution.py:33
  194.0 4.8 %collective-permute-done.4.refs_2_.refs_6_ = bf16[4,4,128,256]{3,2,1,0:T(8,128)(2,1)} collective-permute-done((bf16[4,4,128,256]{3,2,1,0:T(8,128)(2,1)}, bf16[4,4,128,256]{3,2,1,0:T(8,128)(2,1)}, u32[]{:S(2)}, u32[]{:S(2)}) %collective-permute-start.4) | collective-permute-done | bytes 1048608 | tf_op jit(solution)/shard_map/ppermute | solution.py:33
  200.3 2.8 shard_map.107
  203.1 4.7 %collective-permute-done.6.refs_8_ = bf16[8,128,256]{2,1,0:T(8,128)(2,1)S(1)} collective-permute-done((bf16[8,128,256]{2,1,0:T(8,128)(2,1)}, bf16[8,128,256]{2,1,0:T(8,128)(2,1)S(1)}, u32[]{:S(2)}, u32[]{:S(2)}) %collective-permute-start.6) | collective-permute-done | bytes 524320 | tf_op jit(solution)/shard_map/ppermute | solution.py:33
  207.7 3.7 %collective-permute-done.7.refs_9_ = bf16[8,128,256]{2,1,0:T(8,128)(2,1)S(1)} collective-permute-done((bf16[8,128,256]{2,1,0:T(8,128)(2,1)}, bf16[8,128,256]{2,1,0:T(8,128)(2,1)S(1)}, u32[]{:S(2)}, u32[]{:S(2)}) %collective-permute-start.7) | collective-permute-done | bytes 524320 | tf_op jit(solution)/shard_map/ppermute | solution.py:33
  212.2 4.3 %shard_map.106 = (bf16[16,128,256]{2,1,0:T(8,128)(2,1)}, bf16[16,128,256]{2,1,0:T(8,128)(2,1)}) custom-call(s32[2]{0:T(128)} %pad_add_fusion.1.pos_ref, s32[16,128]{1,0:T(8,128)} %bitcast.30, bf16[4,4,128,256]{3,2,1,0:T(8,128)(2,1)} %get-tuple-element.40.refs_0_.refs_4_, bf16[4,4,128,256]{3,2,1,0:T(8,128)(2,1)} %copy-done.1, ...), custom_call_target="tpu_custom_call" | custom-call | tf_op jit(solution)/shard_map/pallas_call | solution.py:149
  216.5 16.7 %collective-permute-done.10.refs_8_ = bf16[8,128,256]{2,1,0:T(8,128)(2,1)S(1)} collective-permute-done((bf16[8,128,256]{2,1,0:T(8,128)(2,1)}, bf16[8,128,256]{2,1,0:T(8,128)(2,1)S(1)}, u32[]{:S(2)}, u32[]{:S(2)}) %collective-permute-start.10) | collective-permute-done | bytes 524320 | tf_op jit(solution)/shard_map/ppermute | solution.py:33
  237.0 4.3 %shard_map.108 = (bf16[16,128,256]{2,1,0:T(8,128)(2,1)}, bf16[16,128,256]{2,1,0:T(8,128)(2,1)}) custom-call(s32[2]{0:T(128)} %pad_add_fusion.1.pos_ref, s32[16,128]{1,0:T(8,128)} %bitcast.31, bf16[4,4,128,256]{3,2,1,0:T(8,128)(2,1)} %get-tuple-element.44.refs_0_.refs_4_.refs_5_, bf16[4,4,128,256]{3,2,1,0:T(8,128)(2,1)} %copy-done.15, ...), custom_call_target="tpu_custom_call" | custom-call | tf_op jit(solution)/shard_map/pallas_call | solution.py:149
  249.6 18.2 %collective-permute-done.27.refs_11_ = bf16[16,128,256]{2,1,0:T(8,128)(2,1)} collective-permute-done((bf16[16,128,256]{2,1,0:T(8,128)(2,1)}, bf16[16,128,256]{2,1,0:T(8,128)(2,1)}, u32[]{:S(2)}, u32[]{:S(2)}) %collective-permute-start.27) | collective-permute-done | bytes 1048608 | tf_op jit(solution)/shard_map/ppermute | solution.py:33
  267.9 14.5 %shard_map.115 = (bf16[16,256,512]{2,1,0:T(8,128)(2,1)}, f32[512,512]{1,0:T(8,128)S(1)}, f32[512,512]{1,0:T(8,128)S(1)}) custom-call(s32[2]{0:T(128)S(1)} %copy-done.13, s32[16,128]{1,0:T(8,128)S(1)} %bitcast.32, f32[16]{0:T(128)S(1)} %add_divide_fusion.inv_ref, s32[64]{0:T(128)S(1)} %convert_reduce_fusion.near_ref, bf16[4,4,128,256]{3,2,1,0:T(8,128)(2,1)S(1)} %copy-done.3, ...), custom_call_target="tpu_custom_call" | custom-call | tf_op jit(solution)/shard_map/pallas_call | solution.py:261
  286.3 15.2 %shard_map.116 = (bf16[16,256,512]{2,1,0:T(8,128)(2,1)}, bf16[512,1024]{1,0:T(8,128)(2,1)S(1)}) custom-call(s32[2]{0:T(128)S(1)} %copy-done.13, s32[16,128]{1,0:T(8,128)S(1)} %bitcast.33, f32[16]{0:T(128)S(1)} %add_divide_fusion.inv_ref, s32[64]{0:T(128)S(1)} %convert_reduce_fusion.near_ref, ...), custom_call_target="tpu_custom_call", output_to_operand_aliasing={{0}: (22, {})} | custom-call | tf_op jit(solution)/shard_map/pallas_call | solution.py:261
  301.5 19.0 %all_to_all.28 = bf16[16,32,1024]{2,1,0:T(8,128)(2,1)S(1)} all-to-all(bf16[16,32,1024]{2,1,0:T(8,128)(2,1)S(1)} %bitcast.34), channel_id=1, replica_groups=mesh['row'=8,'col'=16] {'col'}, dimensions={0} | all-to-all | bytes 2097152 | tf_op jit(solution)/shard_map/all_to_all | solution.py:278
  320.8 13.4 %all_to_all.29 = bf16[8,32,640]{2,1,0:T(8,128)(2,1)S(1)} all-to-all(bf16[8,32,640]{2,1,0:T(8,128)(2,1)S(1)} %fusion.1), channel_id=1, replica_groups=mesh['row'=8,'col'=16] {'row'}, dimensions={0} | all-to-all | bytes 655360 | tf_op jit(solution)/shard_map/all_to_all | solution.py:278
  334.4 15.8 %all_to_all.30 = bf16[16,32,640]{2,1,0:T(8,128)(2,1)S(1)} all-to-all(bf16[16,32,640]{2,1,0:T(8,128)(2,1)S(1)} %broadcast_in_dim.48), channel_id=1, replica_groups=mesh['row'=8,'col'=16] {'col'}, dimensions={0} | all-to-all | bytes 1310720 | tf_op jit(solution)/shard_map/all_to_all | solution.py:278
  (136 shorter events, 52.5 us)
Async XLA Ops:
  9.3 28.6 %collective-permute-start.14 = (bf16[4,4,128,256]{3,2,1,0:T(8,128)(2,1)}, bf16[4,4,128,256]{3,2,1,0:T(8,128)(2,1)S(1)}, u32[]{:S(2)}, u32[]{:S(2)}) collective-permute-start(bf16[4,4,128,256]{3,2,1,0:T(8,128)(2,1)} %get-tuple-element.57), channel_id=1, source_target_pairs={{0,1},{1,2},{2,3},{3,0},{4,5},{5,6},{6,7},{7,4},{8,9},{9,10},{10,1... | collective-permute-start | bytes 3145736 | tf_op jit(solution)/shard_map/ppermute | solution.py:33
  10.9 82.2 %collective-permute-start.15 = (bf16[4,4,128,256]{3,2,1,0:T(8,128)(2,1)}, bf16[4,4,128,256]{3,2,1,0:T(8,128)(2,1)}, u32[]{:S(2)}, u32[]{:S(2)}) collective-permute-start(bf16[4,4,128,256]{3,2,1,0:T(8,128)(2,1)} %get-tuple-element.58), channel_id=1, source_target_pairs={{0,2},{1,3},{2,0},{3,1},{4,6},{5,7},{6,4},{7,5},{8,10},{9,11},{10,... | collective-permute-start | bytes 3145736 | tf_op jit(solution)/shard_map/ppermute | solution.py:33
  13.7 80.2 %collective-permute-start.16 = (bf16[4,4,128,256]{3,2,1,0:T(8,128)(2,1)}, bf16[4,4,128,256]{3,2,1,0:T(8,128)(2,1)}, u32[]{:S(2)}, u32[]{:S(2)}) collective-permute-start(bf16[4,4,128,256]{3,2,1,0:T(8,128)(2,1)} %get-tuple-element.59), channel_id=1, source_target_pairs={{0,3},{1,0},{2,1},{3,2},{4,7},{5,4},{6,5},{7,6},{8,11},{9,8},{10,9... | collective-permute-start | bytes 3145736 | tf_op jit(solution)/shard_map/ppermute | solution.py:33
  21.9 73.8 %collective-permute-start = (bf16[4,4,128,256]{3,2,1,0:T(8,128)(2,1)}, bf16[4,4,128,256]{3,2,1,0:T(8,128)(2,1)S(1)}, u32[]{:S(2)}, u32[]{:S(2)}) collective-permute-start(bf16[4,4,128,256]{3,2,1,0:T(8,128)(2,1)} %get-tuple-element.41), channel_id=1, source_target_pairs={{0,1},{1,2},{2,3},{3,0},{4,5},{5,6},{6,7},{7,4},{8,9},{9,10},{10,1... | collective-permute-start | bytes 3145736 | tf_op jit(solution)/shard_map/ppermute | solution.py:33
  23.3 62.2 %all-to-all-start = ((s32[16,1,128]{2,1,0:T(1,128)}), s32[16,1,128]{2,1,0:T(1,128)S(1)}, u32[]{:S(2)}, u32[]{:S(2)}) async-start(s32[16,1,128]{2,1,0:T(1,128)} %broadcast_in_dim.25), calls=%async_computation | async-start | bytes 16384 | tf_op jit(solution)/shard_map/all_to_all | solution.py:278
  30.0 93.3 %collective-permute-start.1 = (bf16[4,4,128,256]{3,2,1,0:T(8,128)(2,1)}, bf16[4,4,128,256]{3,2,1,0:T(8,128)(2,1)S(1)}, u32[]{:S(2)}, u32[]{:S(2)}) collective-permute-start(bf16[4,4,128,256]{3,2,1,0:T(8,128)(2,1)} %get-tuple-element.42), channel_id=1, source_target_pairs={{0,2},{1,3},{2,0},{3,1},{4,6},{5,7},{6,4},{7,5},{8,10},{9,11},{10,... | collective-permute-start | bytes 3145736 | tf_op jit(solution)/shard_map/ppermute | solution.py:33
  37.9 55.2 %copy-start.4 = (bf16[4,4,128,256]{3,2,1,0:T(8,128)(2,1)}, bf16[4,4,128,256]{3,2,1,0:T(8,128)(2,1)S(1)}, u32[]{:S(2)}) copy-start(bf16[4,4,128,256]{3,2,1,0:T(8,128)(2,1)S(1)} %collective-permute-done.14.refs_1_.refs_5_) | copy-start | bytes 3145732
  37.9 86.0 %collective-permute-start.2 = (bf16[4,4,128,256]{3,2,1,0:T(8,128)(2,1)}, bf16[4,4,128,256]{3,2,1,0:T(8,128)(2,1)}, u32[]{:S(2)}, u32[]{:S(2)}) collective-permute-start(bf16[4,4,128,256]{3,2,1,0:T(8,128)(2,1)} %get-tuple-element.43), channel_id=1, source_target_pairs={{0,3},{1,0},{2,1},{3,2},{4,7},{5,4},{6,5},{7,6},{8,11},{9,8},{10,9... | collective-permute-start | bytes 3145736 | tf_op jit(solution)/shard_map/ppermute | solution.py:33
  93.1 44.7 %collective-permute-start.17 = (bf16[4,4,128,256]{3,2,1,0:T(8,128)(2,1)}, bf16[4,4,128,256]{3,2,1,0:T(8,128)(2,1)S(1)}, u32[]{:S(2)}, u32[]{:S(2)}) collective-permute-start(bf16[4,4,128,256]{3,2,1,0:T(8,128)(2,1)} %get-tuple-element.61), channel_id=1, source_target_pairs={{0,4},{1,5},{2,6},{3,7},{4,8},{5,9},{6,10},{7,11},{8,12},{9,13},{1... | collective-permute-start | bytes 3145736 | tf_op jit(solution)/shard_map/ppermute | solution.py:33
  93.9 48.7 %collective-permute-start.18 = (bf16[4,4,128,256]{3,2,1,0:T(8,128)(2,1)}, bf16[4,4,128,256]{3,2,1,0:T(8,128)(2,1)}, u32[]{:S(2)}, u32[]{:S(2)}) collective-permute-start(bf16[4,4,128,256]{3,2,1,0:T(8,128)(2,1)} %get-tuple-element.62), channel_id=1, source_target_pairs={{0,8},{1,9},{2,10},{3,11},{4,12},{5,13},{6,14},{7,15},{8,0},{9,1},... | collective-permute-start | bytes 3145736 | tf_op jit(solution)/shard_map/ppermute | solution.py:33
  95.7 48.5 %collective-permute-start.19 = (bf16[4,4,128,256]{3,2,1,0:T(8,128)(2,1)}, bf16[4,4,128,256]{3,2,1,0:T(8,128)(2,1)}, u32[]{:S(2)}, u32[]{:S(2)}) collective-permute-start(bf16[4,4,128,256]{3,2,1,0:T(8,128)(2,1)} %get-tuple-element.63), channel_id=1, source_target_pairs={{0,12},{1,13},{2,14},{3,15},{4,0},{5,1},{6,2},{7,3},{8,4},{9,5},{1... | collective-permute-start | bytes 3145736 | tf_op jit(solution)/shard_map/ppermute | solution.py:33
  98.0 15.7 %all-to-all-start.1 = ((bf16[8,64,512]{2,1,0:T(8,128)(2,1)}), bf16[8,64,512]{2,1,0:T(8,128)(2,1)}, u32[]{:S(2)}, u32[]{:S(2)}) async-start(bf16[8,64,512]{2,1,0:T(8,128)(2,1)} %broadcast_in_dim.46), calls=%async_computation.1 | async-start | bytes 1048576 | tf_op jit(solution)/shard_map/all_to_all | solution.py:278
  123.3 32.7 %copy-start.6 = (bf16[4,4,128,256]{3,2,1,0:T(8,128)(2,1)}, bf16[4,4,128,256]{3,2,1,0:T(8,128)(2,1)S(1)}, u32[]{:S(2)}) copy-start(bf16[4,4,128,256]{3,2,1,0:T(8,128)(2,1)S(1)} %collective-permute-done.1.refs_2_.refs_6_) | copy-start | bytes 3145732
  123.3 28.2 %collective-permute-start.20 = (bf16[8,128,256]{2,1,0:T(8,128)(2,1)}, bf16[8,128,256]{2,1,0:T(8,128)(2,1)}, u32[]{:S(2)}, u32[]{:S(2)}) collective-permute-start(bf16[8,128,256]{2,1,0:T(8,128)(2,1)} %get-tuple-element.64), channel_id=1, source_target_pairs={{0,4},{1,5},{2,6},{3,7},{4,8},{5,9},{6,10},{7,11},{8,12},{9,13},{1... | collective-permute-start | bytes 1572872 | tf_op jit(solution)/shard_map/ppermute | solution.py:33
  123.9 31.4 %collective-permute-start.21 = (bf16[8,128,256]{2,1,0:T(8,128)(2,1)}, bf16[8,128,256]{2,1,0:T(8,128)(2,1)}, u32[]{:S(2)}, u32[]{:S(2)}) collective-permute-start(bf16[8,128,256]{2,1,0:T(8,128)(2,1)} %get-tuple-element.65), channel_id=1, source_target_pairs={{0,12},{1,13},{2,14},{3,15},{4,0},{5,1},{6,2},{7,3},{8,4},{9,5},{1... | collective-permute-start | bytes 1572872 | tf_op jit(solution)/shard_map/ppermute | solution.py:33
  137.8 56.1 %collective-permute-start.3 = (bf16[4,4,128,256]{3,2,1,0:T(8,128)(2,1)}, bf16[4,4,128,256]{3,2,1,0:T(8,128)(2,1)S(1)}, u32[]{:S(2)}, u32[]{:S(2)}) collective-permute-start(bf16[4,4,128,256]{3,2,1,0:T(8,128)(2,1)} %get-tuple-element.45), channel_id=1, source_target_pairs={{0,4},{1,5},{2,6},{3,7},{4,8},{5,9},{6,10},{7,11},{8,12},{9,13},{1... | collective-permute-start | bytes 3145736 | tf_op jit(solution)/shard_map/ppermute | solution.py:33
  142.6 56.2 %collective-permute-start.4 = (bf16[4,4,128,256]{3,2,1,0:T(8,128)(2,1)}, bf16[4,4,128,256]{3,2,1,0:T(8,128)(2,1)}, u32[]{:S(2)}, u32[]{:S(2)}) collective-permute-start(bf16[4,4,128,256]{3,2,1,0:T(8,128)(2,1)} %get-tuple-element.46), channel_id=1, source_target_pairs={{0,8},{1,9},{2,10},{3,11},{4,12},{5,13},{6,14},{7,15},{8,0},{9,1},... | collective-permute-start | bytes 3145736 | tf_op jit(solution)/shard_map/ppermute | solution.py:33
  144.3 56.0 %collective-permute-start.5 = (bf16[4,4,128,256]{3,2,1,0:T(8,128)(2,1)}, bf16[4,4,128,256]{3,2,1,0:T(8,128)(2,1)}, u32[]{:S(2)}, u32[]{:S(2)}) collective-permute-start(bf16[4,4,128,256]{3,2,1,0:T(8,128)(2,1)} %get-tuple-element.47), channel_id=1, source_target_pairs={{0,12},{1,13},{2,14},{3,15},{4,0},{5,1},{6,2},{7,3},{8,4},{9,5},{1... | collective-permute-start | bytes 3145736 | tf_op jit(solution)/shard_map/ppermute | solution.py:33
  151.5 14.3 %collective-permute-start.24 = (bf16[8,128,256]{2,1,0:T(8,128)(2,1)}, bf16[8,128,256]{2,1,0:T(8,128)(2,1)S(1)}, u32[]{:S(2)}, u32[]{:S(2)}) collective-permute-start(bf16[8,128,256]{2,1,0:T(8,128)(2,1)} %get-tuple-element.68), channel_id=1, source_target_pairs={{0,1},{1,2},{2,3},{3,0},{4,5},{5,6},{6,7},{7,4},{8,9},{9,10},{10,1... | collective-permute-start | bytes 1572872 | tf_op jit(solution)/shard_map/ppermute | solution.py:33
  155.3 12.4 %collective-permute-start.25 = (bf16[8,128,256]{2,1,0:T(8,128)(2,1)}, bf16[8,128,256]{2,1,0:T(8,128)(2,1)S(1)}, u32[]{:S(2)}, u32[]{:S(2)}) collective-permute-start(bf16[8,128,256]{2,1,0:T(8,128)(2,1)} %get-tuple-element.69), channel_id=1, source_target_pairs={{0,3},{1,0},{2,1},{3,2},{4,7},{5,4},{6,5},{7,6},{8,11},{9,8},{10,9... | collective-permute-start | bytes 1572872 | tf_op jit(solution)/shard_map/ppermute | solution.py:33
  165.8 41.9 %collective-permute-start.6 = (bf16[8,128,256]{2,1,0:T(8,128)(2,1)}, bf16[8,128,256]{2,1,0:T(8,128)(2,1)S(1)}, u32[]{:S(2)}, u32[]{:S(2)}) collective-permute-start(bf16[8,128,256]{2,1,0:T(8,128)(2,1)} %get-tuple-element.48), channel_id=1, source_target_pairs={{0,4},{1,5},{2,6},{3,7},{4,8},{5,9},{6,10},{7,11},{8,12},{9,13},{1... | collective-permute-start | bytes 1572872 | tf_op jit(solution)/shard_map/ppermute | solution.py:33
  167.7 43.8 %collective-permute-start.7 = (bf16[8,128,256]{2,1,0:T(8,128)(2,1)}, bf16[8,128,256]{2,1,0:T(8,128)(2,1)S(1)}, u32[]{:S(2)}, u32[]{:S(2)}) collective-permute-start(bf16[8,128,256]{2,1,0:T(8,128)(2,1)} %get-tuple-element.49), channel_id=1, source_target_pairs={{0,12},{1,13},{2,14},{3,15},{4,0},{5,1},{6,2},{7,3},{8,4},{9,5},{1... | collective-permute-start | bytes 1572872 | tf_op jit(solution)/shard_map/ppermute | solution.py:33
  194.0 47.4 %collective-permute-start.22 = (bf16[16,128,256]{2,1,0:T(8,128)(2,1)}, bf16[16,128,256]{2,1,0:T(8,128)(2,1)}, u32[]{:S(2)}, u32[]{:S(2)}) collective-permute-start(bf16[16,128,256]{2,1,0:T(8,128)(2,1)} %get-tuple-element.66), channel_id=1, source_target_pairs={{0,4},{1,5},{2,6},{3,7},{4,8},{5,9},{6,10},{7,11},{8,12},{9,13},{1... | collective-permute-start | bytes 3145736 | tf_op jit(solution)/shard_map/ppermute | solution.py:33
  198.8 42.7 %collective-permute-start.23 = (bf16[16,128,256]{2,1,0:T(8,128)(2,1)}, bf16[16,128,256]{2,1,0:T(8,128)(2,1)}, u32[]{:S(2)}, u32[]{:S(2)}) collective-permute-start(bf16[16,128,256]{2,1,0:T(8,128)(2,1)} %get-tuple-element.67), channel_id=1, source_target_pairs={{0,12},{1,13},{2,14},{3,15},{4,0},{5,1},{6,2},{7,3},{8,4},{9,5},{1... | collective-permute-start | bytes 3145736 | tf_op jit(solution)/shard_map/ppermute | solution.py:33
  200.3 43.2 %collective-permute-start.26 = (bf16[16,128,256]{2,1,0:T(8,128)(2,1)}, bf16[16,128,256]{2,1,0:T(8,128)(2,1)}, u32[]{:S(2)}, u32[]{:S(2)}) collective-permute-start(bf16[16,128,256]{2,1,0:T(8,128)(2,1)} %get-tuple-element.70), channel_id=1, source_target_pairs={{0,1},{1,2},{2,3},{3,0},{4,5},{5,6},{6,7},{7,4},{8,9},{9,10},{10,1... | collective-permute-start | bytes 3145736 | tf_op jit(solution)/shard_map/ppermute | solution.py:33
  207.7 25.5 %collective-permute-start.10 = (bf16[8,128,256]{2,1,0:T(8,128)(2,1)}, bf16[8,128,256]{2,1,0:T(8,128)(2,1)S(1)}, u32[]{:S(2)}, u32[]{:S(2)}) collective-permute-start(bf16[8,128,256]{2,1,0:T(8,128)(2,1)} %get-tuple-element.52), channel_id=1, source_target_pairs={{0,1},{1,2},{2,3},{3,0},{4,5},{5,6},{6,7},{7,4},{8,9},{9,10},{10,1... | collective-permute-start | bytes 1572872 | tf_op jit(solution)/shard_map/ppermute | solution.py:33
  211.4 23.5 %collective-permute-start.11 = (bf16[8,128,256]{2,1,0:T(8,128)(2,1)}, bf16[8,128,256]{2,1,0:T(8,128)(2,1)S(1)}, u32[]{:S(2)}, u32[]{:S(2)}) collective-permute-start(bf16[8,128,256]{2,1,0:T(8,128)(2,1)} %get-tuple-element.53), channel_id=1, source_target_pairs={{0,3},{1,0},{2,1},{3,2},{4,7},{5,4},{6,5},{7,6},{8,11},{9,8},{10,9... | collective-permute-start | bytes 1572872 | tf_op jit(solution)/shard_map/ppermute | solution.py:33
  233.2 51.1 %collective-permute-start.8 = (bf16[16,128,256]{2,1,0:T(8,128)(2,1)}, bf16[16,128,256]{2,1,0:T(8,128)(2,1)}, u32[]{:S(2)}, u32[]{:S(2)}) collective-permute-start(bf16[16,128,256]{2,1,0:T(8,128)(2,1)} %get-tuple-element.50), channel_id=1, source_target_pairs={{0,4},{1,5},{2,6},{3,7},{4,8},{5,9},{6,10},{7,11},{8,12},{9,13},{1... | collective-permute-start | bytes 3145736 | tf_op jit(solution)/shard_map/ppermute | solution.py:33
  234.9 49.4 %collective-permute-start.9 = (bf16[16,128,256]{2,1,0:T(8,128)(2,1)}, bf16[16,128,256]{2,1,0:T(8,128)(2,1)}, u32[]{:S(2)}, u32[]{:S(2)}) collective-permute-start(bf16[16,128,256]{2,1,0:T(8,128)(2,1)} %get-tuple-element.51), channel_id=1, source_target_pairs={{0,12},{1,13},{2,14},{3,15},{4,0},{5,1},{6,2},{7,3},{8,4},{9,5},{1... | collective-permute-start | bytes 3145736 | tf_op jit(solution)/shard_map/ppermute | solution.py:33
  241.4 26.4 %collective-permute-start.27 = (bf16[16,128,256]{2,1,0:T(8,128)(2,1)}, bf16[16,128,256]{2,1,0:T(8,128)(2,1)}, u32[]{:S(2)}, u32[]{:S(2)}) collective-permute-start(bf16[16,128,256]{2,1,0:T(8,128)(2,1)} %get-tuple-element.71), channel_id=1, source_target_pairs={{0,3},{1,0},{2,1},{3,2},{4,7},{5,4},{6,5},{7,6},{8,11},{9,8},{10,9... | collective-permute-start | bytes 3145736 | tf_op jit(solution)/shard_map/ppermute | solution.py:33
  241.5 42.9 %collective-permute-start.12 = (bf16[16,128,256]{2,1,0:T(8,128)(2,1)}, bf16[16,128,256]{2,1,0:T(8,128)(2,1)}, u32[]{:S(2)}, u32[]{:S(2)}) collective-permute-start(bf16[16,128,256]{2,1,0:T(8,128)(2,1)} %get-tuple-element.54), channel_id=1, source_target_pairs={{0,1},{1,2},{2,3},{3,0},{4,5},{5,6},{6,7},{7,4},{8,9},{9,10},{10,1... | collective-permute-start | bytes 3145736 | tf_op jit(solution)/shard_map/ppermute | solution.py:33
  243.5 42.8 %collective-permute-start.13 = (bf16[16,128,256]{2,1,0:T(8,128)(2,1)}, bf16[16,128,256]{2,1,0:T(8,128)(2,1)}, u32[]{:S(2)}, u32[]{:S(2)}) collective-permute-start(bf16[16,128,256]{2,1,0:T(8,128)(2,1)} %get-tuple-element.55), channel_id=1, source_target_pairs={{0,3},{1,0},{2,1},{3,2},{4,7},{5,4},{6,5},{7,6},{8,11},{9,8},{10,9... | collective-permute-start | bytes 3145736 | tf_op jit(solution)/shard_map/ppermute | solution.py:33
  (24 other events, 280.2 us)

commit v2 on v1

--- a/solution.py
+++ b/solution.py
@@ -31,6 +31,14 @@
 
 def shift(v, axis, by):
     return lax.ppermute(v, "col", shift_pairs(axis, by))
+
+
+def row_shift(v, to):
+    pairs = []
+    for i in range(lax.axis_size("row")):
+        z, core = to(i // 2, i % 2)
+        pairs.append((i, z * 2 + core))
+    return lax.ppermute(v, "row", pairs)
 
 
 def message_kernel(order_ref, src_ref, emb_ref, *refs):
@@ -317,7 +325,7 @@
 
     def send(k):
         for half in range(2):
-            after = {(0, 1): [table], (1, 1): [gathered]}.get((k, half), [])
+            after = [gathered] if (k, half) == (1, 1) else []
             after = after + lows[k - 2] if k >= 2 else after
             out = messages_of(orders[half], msg_src, blocks, tiles,
                         starts[k], CHUNK_ROWS[k], half, after)
@@ -362,15 +370,16 @@
     hidden, both = carry
 
     part_of = n_doc // n_col
-    lane = width // share
     part = swap(both.reshape(n_col, part_of, 2 * width), "col")
-    part = jnp.sum(part.astype(F32), axis=0).astype(BF)
-    own = part[:, :width].reshape(n_row, share * share, lane)
-    own = jnp.pad(own, ((0, 0), (0, part_of - share * share), (0, 0)))
-    out = jnp.broadcast_to(part[None, :, width:], (n_row, part_of, width))
-    part = swap(jnp.concatenate([out, own], axis=2), "row")
-    part = jnp.sum(part.astype(F32), axis=0).astype(BF)
-    whole = spread(part, "col", n_col)
+    part = jnp.sum(part.astype(F32), axis=0)
+    part = part + row_shift(part.astype(BF), lambda z, core: (z, 1 - core)).astype(F32)
+    sent = part.astype(BF)
+    for by in (1, 2, 3):
+        part = part + row_shift(sent, lambda z, core: ((z + by) % (n_row // 2), core)).astype(F32)
+    part = part.astype(BF)
+    own = lax.dynamic_slice_in_dim(part[:, :width], lax.axis_index("row") * share, share, 0)
+    own = jnp.pad(own.reshape(share * share, width // share), ((0, part_of - share * share), (0, 0)))
+    whole = spread(jnp.concatenate([part[:, width:], own], axis=1), "col", n_col)
     grad_weight = whole[:, :, :width].reshape(n_doc, width)
     grad_docs = whole[:, :share * share, width:].reshape(docs.shape)
     return hidden.reshape(label_dev, width), grad_docs.astype(F32), grad_weight.astype(F32)

time: 353 us -> 342 us (0.969)
  starting transfers between devices: 43.9 us -> 70.2 us
  waiting for transfers between devices: 159 us -> 135 us
  blocking collectives: 48.2 us -> 34.2 us
    all_to_all x2, waiting for transfers between devices: 56.3 us -> 26.9 us  [swap(): return lax.all_to_all(x, axis, split_axis=0, concat_axis=0, tiled=True)]
    ppermute x28, starting transfers between devices: 31.9 us -> 46.5 us  [shift(): return lax.ppermute(v, 'col', shift_pairs(axis, by))]
    all_to_all x3 -> x2, blocking collectives: 48.2 us -> 34.2 us  [swap(): return lax.all_to_all(x, axis, split_axis=0, concat_axis=0, tiled=True)]
    ppermute x0 -> x4, starting transfers between devices: none -> 6.73 us  [row_shift(): return lax.ppermute(v, 'row', pairs)]
    ppermute x0 -> x4, waiting for transfers between devices: none -> 5.13 us  [row_shift(): return lax.ppermute(v, 'row', pairs)]
    all_to_all x2, starting transfers between devices: 12 us -> 17 us  [swap(): return lax.all_to_all(x, axis, split_axis=0, concat_axis=0, tiled=True)]
  transfers between devices with their start and end apart: 30 -> 34, of which waited for: 17 -> 14; matrix products, arithmetic and copies ran while one was open for 2% -> 2% of each run, Pallas kernels for 18% -> 18%
where the time goes in v2:
time: 342 us; the launch traced here: 341 us
  waiting for transfers between devices  135 us (39%)
  Pallas kernels  84.9 us (25%)
  starting transfers between devices  70.2 us (21%)
  blocking collectives  34.2 us (10%)
  local copies, waits for them, and re-layouts  11.9 us (3%)
  other arithmetic  3.46 us (1%)
    ppermute x28, waiting for transfers between devices, shift(): return lax.ppermute(v, 'col', shift_pairs(axis, by))  103 us
    ppermute x28, starting transfers between devices, shift(): return lax.ppermute(v, 'col', shift_pairs(axis, by))  46.5 us
    all_to_all x2, blocking collectives, swap(): return lax.all_to_all(x, axis, split_axis=0, concat_axis=0, tiled=True)  34.2 us
    pallas_call x2, Pallas kernels, head(): pl.pallas_call(functools.partial(head_kernel, first, last, row, blk, labe...  29.7 us
    pallas_call x4, Pallas kernels, messages_of(): pl.pallas_call(message_kernel, grid_spec=pltpu.PrefetchScalarGridSpec(num...  27.4 us
    all_to_all x2, waiting for transfers between devices, swap(): return lax.all_to_all(x, axis, split_axis=0, concat_axis=0, tiled=True)  26.9 us
    all_to_all x2, starting transfers between devices, swap(): return lax.all_to_all(x, axis, split_axis=0, concat_axis=0, tiled=True)  17 us
    pallas_call x4, Pallas kernels, near_sums(): pl.pallas_call(functools.partial(near_kernel, half), grid=(rows // step_r...  17 us
  transfers between devices with their start and end apart: 34, of which 14 were waited for; matrix products, arithmetic and copies ran while one was open for 2% of the time, Pallas kernels for 18%

profile of v2, /device:TPU:0, one launch (start us, length us, event | category | flops | bytes accessed | tf_op | source)
XLA Modules:
  0.0 340.6 jit_solution(5886202872956216441)
XLA Ops:
  2.5 6.8 %shard_map.110 = (bf16[4,4,128,256]{3,2,1,0:T(8,128)(2,1)}, bf16[4,4,128,256]{3,2,1,0:T(8,128)(2,1)}, bf16[4,4,128,256]{3,2,1,0:T(8,128)(2,1)}, bf16[4,4,128,256]{3,2,1,0:T(8,128)(2,1)}) custom-call(s32[16]{0:T(128)} %fusion.13.order_ref, s32[16,4]{1,0:T(8,128)} %copy.54.src_ref, bf16[16,256,512]{2,1,0:T(8,128)(2,1)} %bitcast.36, ...), custom_call_target="tpu_custom_call" | custom-call | tf_op jit(solution)/shard_map/pallas_call | solution.py:61
  11.0 2.9 collective-permute-start.18
  15.7 6.9 %shard_map.109 = (bf16[4,4,128,256]{3,2,1,0:T(8,128)(2,1)}, bf16[4,4,128,256]{3,2,1,0:T(8,128)(2,1)}, bf16[4,4,128,256]{3,2,1,0:T(8,128)(2,1)}, bf16[4,4,128,256]{3,2,1,0:T(8,128)(2,1)}) custom-call(s32[16]{0:T(128)} %fusion.9.order_ref, s32[16,4]{1,0:T(8,128)} %copy.54.src_ref, bf16[16,256,512]{2,1,0:T(8,128)(2,1)} %bitcast.37, ...), custom_call_target="tpu_custom_call" | custom-call | tf_op jit(solution)/shard_map/pallas_call | solution.py:61
  24.1 2.7 collective-permute-start.15
  26.8 8.9 %collective-permute-done.17.refs_1_.refs_5_ = bf16[4,4,128,256]{3,2,1,0:T(8,128)(2,1)S(1)} collective-permute-done((bf16[4,4,128,256]{3,2,1,0:T(8,128)(2,1)}, bf16[4,4,128,256]{3,2,1,0:T(8,128)(2,1)S(1)}, u32[]{:S(2)}, u32[]{:S(2)}) %collective-permute-start.17) | collective-permute-done | bytes 1048608 | tf_op jit(solution)/shard_map/ppermute | solution.py:33
  35.8 2.8 collective-permute-start.16
  38.6 6.8 %shard_map.103 = (bf16[4,4,128,256]{3,2,1,0:T(8,128)(2,1)}, bf16[4,4,128,256]{3,2,1,0:T(8,128)(2,1)}, bf16[4,4,128,256]{3,2,1,0:T(8,128)(2,1)}, bf16[4,4,128,256]{3,2,1,0:T(8,128)(2,1)}) custom-call(s32[16]{0:T(128)} %fusion.9.order_ref, s32[16,4]{1,0:T(8,128)} %copy.54.src_ref, bf16[16,256,512]{2,1,0:T(8,128)(2,1)} %bitcast.38, ...), custom_call_target="tpu_custom_call" | custom-call | tf_op jit(solution)/shard_map/pallas_call | solution.py:61
  45.4 14.0 %collective-permute-done.18.refs_2_.refs_6_ = bf16[4,4,128,256]{3,2,1,0:T(8,128)(2,1)S(1)} collective-permute-done((bf16[4,4,128,256]{3,2,1,0:T(8,128)(2,1)}, bf16[4,4,128,256]{3,2,1,0:T(8,128)(2,1)S(1)}, u32[]{:S(2)}, u32[]{:S(2)}) %collective-permute-start.18) | collective-permute-done | bytes 1048608 | tf_op jit(solution)/shard_map/ppermute | solution.py:33
  62.0 2.7 collective-permute-start.1
  67.0 5.3 %all-to-all-start.1 = ((bf16[8,64,512]{2,1,0:T(8,128)(2,1)}), bf16[8,64,512]{2,1,0:T(8,128)(2,1)}, u32[]{:S(2)}, u32[]{:S(2)}) async-start(bf16[8,64,512]{2,1,0:T(8,128)(2,1)} %broadcast_in_dim.40), calls=%async_computation.1 | async-start | bytes 1048576 | tf_op jit(solution)/shard_map/all_to_all | solution.py:286
  72.5 10.2 %all-to-all-done.1 = bf16[8,64,512]{2,1,0:T(8,128)(2,1)} async-done(((bf16[8,64,512]{2,1,0:T(8,128)(2,1)}), bf16[8,64,512]{2,1,0:T(8,128)(2,1)}, u32[]{:S(2)}, u32[]{:S(2)}) %all-to-all-start.1) | async-done | bytes 524320 | tf_op jit(solution)/shard_map/all_to_all | solution.py:286
  83.3 11.7 %all-to-all-start = ((s32[16,1,128]{2,1,0:T(1,128)}), s32[16,1,128]{2,1,0:T(1,128)S(1)}, u32[]{:S(2)}, u32[]{:S(2)}) async-start(s32[16,1,128]{2,1,0:T(1,128)} %broadcast_in_dim.23), calls=%async_computation | async-start | bytes 16384 | tf_op jit(solution)/shard_map/all_to_all | solution.py:286
  95.6 6.9 %shard_map.104 = (bf16[4,4,128,256]{3,2,1,0:T(8,128)(2,1)}, bf16[4,4,128,256]{3,2,1,0:T(8,128)(2,1)}, bf16[4,4,128,256]{3,2,1,0:T(8,128)(2,1)}, bf16[4,4,128,256]{3,2,1,0:T(8,128)(2,1)}) custom-call(s32[16]{0:T(128)} %fusion.13.order_ref, s32[16,4]{1,0:T(8,128)} %copy.54.src_ref, bf16[16,256,512]{2,1,0:T(8,128)(2,1)} %bitcast.39, ...), custom_call_target="tpu_custom_call" | custom-call | tf_op jit(solution)/shard_map/pallas_call | solution.py:61
  102.6 16.7 %all-to-all-done = s32[16,1,128]{2,1,0:T(1,128)S(1)} async-done(((s32[16,1,128]{2,1,0:T(1,128)}), s32[16,1,128]{2,1,0:T(1,128)S(1)}, u32[]{:S(2)}, u32[]{:S(2)}) %all-to-all-start) | async-done | bytes 8224 | tf_op jit(solution)/shard_map/all_to_all | solution.py:286
  122.5 2.9 collective-permute-start.24
  130.4 2.7 shard_map.111
  140.9 43.0 %collective-permute-done.20.refs_8_ = bf16[8,128,256]{2,1,0:T(8,128)(2,1)} collective-permute-done((bf16[8,128,256]{2,1,0:T(8,128)(2,1)}, bf16[8,128,256]{2,1,0:T(8,128)(2,1)}, u32[]{:S(2)}, u32[]{:S(2)}) %collective-permute-start.20) | collective-permute-done | bytes 524320 | tf_op jit(solution)/shard_map/ppermute | solution.py:33
  184.2 3.0 collective-permute-start.7
  187.2 4.2 %shard_map.114 = (bf16[16,128,256]{2,1,0:T(8,128)(2,1)}, bf16[16,128,256]{2,1,0:T(8,128)(2,1)}) custom-call(s32[2]{0:T(128)} %pad_add_fusion.1.pos_ref, s32[16,128]{1,0:T(8,128)} %bitcast.26, bf16[4,4,128,256]{3,2,1,0:T(8,128)(2,1)} %get-tuple-element.60.refs_0_.refs_4_, bf16[4,4,128,256]{3,2,1,0:T(8,128)(2,1)} %copy-done.14, ...), custom_call_target="tpu_custom_call" | custom-call | tf_op jit(solution)/shard_map/pallas_call | solution.py:157
  191.4 4.3 %shard_map.112 = (bf16[16,128,256]{2,1,0:T(8,128)(2,1)}, bf16[16,128,256]{2,1,0:T(8,128)(2,1)}) custom-call(s32[2]{0:T(128)} %pad_add_fusion.1.pos_ref, s32[16,128]{1,0:T(8,128)} %bitcast.27, bf16[4,4,128,256]{3,2,1,0:T(8,128)(2,1)} %get-tuple-element.56.refs_0_.refs_4_, bf16[4,4,128,256]{3,2,1,0:T(8,128)(2,1)} %copy-done.4, ...), custom_call_target="tpu_custom_call" | custom-call | tf_op jit(solution)/shard_map/pallas_call | solution.py:157
  196.3 2.7 collective-permute-start.27
  201.9 3.2 collective-permute-start.11
  205.1 4.3 %shard_map.106 = (bf16[16,128,256]{2,1,0:T(8,128)(2,1)}, bf16[16,128,256]{2,1,0:T(8,128)(2,1)}) custom-call(s32[2]{0:T(128)} %pad_add_fusion.1.pos_ref, s32[16,128]{1,0:T(8,128)} %bitcast.29, bf16[4,4,128,256]{3,2,1,0:T(8,128)(2,1)} %get-tuple-element.40.refs_0_.refs_4_, bf16[4,4,128,256]{3,2,1,0:T(8,128)(2,1)} %copy-done.2, ...), custom_call_target="tpu_custom_call" | custom-call | tf_op jit(solution)/shard_map/pallas_call | solution.py:157
  209.4 22.4 %collective-permute-done.10.refs_8_ = bf16[8,128,256]{2,1,0:T(8,128)(2,1)S(1)} collective-permute-done((bf16[8,128,256]{2,1,0:T(8,128)(2,1)}, bf16[8,128,256]{2,1,0:T(8,128)(2,1)S(1)}, u32[]{:S(2)}, u32[]{:S(2)}) %collective-permute-start.10) | collective-permute-done | bytes 524320 | tf_op jit(solution)/shard_map/ppermute | solution.py:33
  233.9 4.2 %shard_map.108 = (bf16[16,128,256]{2,1,0:T(8,128)(2,1)}, bf16[16,128,256]{2,1,0:T(8,128)(2,1)}) custom-call(s32[2]{0:T(128)} %pad_add_fusion.1.pos_ref, s32[16,128]{1,0:T(8,128)} %bitcast.30, bf16[4,4,128,256]{3,2,1,0:T(8,128)(2,1)} %get-tuple-element.44.refs_0_.refs_4_.refs_5_, bf16[4,4,128,256]{3,2,1,0:T(8,128)(2,1)} %copy-done.16, ...), custom_call_target="tpu_custom_call" | custom-call | tf_op jit(solution)/shard_map/pallas_call | solution.py:157
  239.7 3.1 collective-permute-start.13
  247.6 10.5 %collective-permute-done.23.refs_9_ = bf16[16,128,256]{2,1,0:T(8,128)(2,1)} collective-permute-done((bf16[16,128,256]{2,1,0:T(8,128)(2,1)}, bf16[16,128,256]{2,1,0:T(8,128)(2,1)}, u32[]{:S(2)}, u32[]{:S(2)}) %collective-permute-start.23) | collective-permute-done | bytes 1048608 | tf_op jit(solution)/shard_map/ppermute | solution.py:33
  258.2 14.5 %shard_map.115 = (bf16[16,256,512]{2,1,0:T(8,128)(2,1)}, f32[512,512]{1,0:T(8,128)S(1)}, f32[512,512]{1,0:T(8,128)S(1)}) custom-call(s32[2]{0:T(128)S(1)} %copy-done.13, s32[16,128]{1,0:T(8,128)S(1)} %bitcast.31, f32[16]{0:T(128)S(1)} %add_divide_fusion.inv_ref, s32[64]{0:T(128)S(1)} %convert_reduce_fusion.1.near_ref, ...), custom_call_target="tpu_custom_call" | custom-call | tf_op jit(solution)/shard_map/pallas_call | solution.py:269
  277.1 15.2 %shard_map.116 = (bf16[16,256,512]{2,1,0:T(8,128)(2,1)}, bf16[512,1024]{1,0:T(8,128)(2,1)S(1)}) custom-call(s32[2]{0:T(128)S(1)} %copy-done.13, s32[16,128]{1,0:T(8,128)S(1)} %bitcast.32, f32[16]{0:T(128)S(1)} %add_divide_fusion.inv_ref, s32[64]{0:T(128)S(1)} %convert_reduce_fusion.1.near_ref, ...), custom_call_target="tpu_custom_call", output_to_operand_aliasing={{0}: (22, {})} | custom-call | tf_op jit(solution)/shard_map/pallas_call | solution.py:269
  292.2 19.4 %all_to_all.23 = bf16[16,32,1024]{2,1,0:T(8,128)(2,1)S(1)} all-to-all(bf16[16,32,1024]{2,1,0:T(8,128)(2,1)S(1)} %bitcast.33), channel_id=1, replica_groups=mesh['row'=8,'col'=16] {'col'}, dimensions={0} | all-to-all | bytes 2097152 | tf_op jit(solution)/shard_map/all_to_all | solution.py:286
  315.7 3.8 %collective-permute-start.30 = (bf16[32,1024]{1,0:T(8,128)(2,1)S(1)}, bf16[32,1024]{1,0:T(8,128)(2,1)S(1)}, u32[]{:S(2)}, u32[]{:S(2)}) collective-permute-start(bf16[32,1024]{1,0:T(8,128)(2,1)S(1)} %fusion), channel_id=1, source_target_pairs={{0,64},{16,80},{32,96},{48,112},{64,0},{80,16},{96,32},{112,48},{1... | collective-permute-start | bytes 196616 | tf_op jit(solution)/shard_map/ppermute | solution.py:41
  323.9 14.8 %all_to_all.24 = bf16[16,32,640]{2,1,0:T(8,128)(2,1)S(1)} all-to-all(bf16[16,32,640]{2,1,0:T(8,128)(2,1)S(1)} %broadcast_in_dim.41), channel_id=1, replica_groups=mesh['row'=8,'col'=16] {'col'}, dimensions={0} | all-to-all | bytes 1310720 | tf_op jit(solution)/shard_map/all_to_all | solution.py:286
  (143 shorter events, 55.8 us)
Async XLA Ops:
  9.3 26.5 %collective-permute-start.17 = (bf16[4,4,128,256]{3,2,1,0:T(8,128)(2,1)}, bf16[4,4,128,256]{3,2,1,0:T(8,128)(2,1)S(1)}, u32[]{:S(2)}, u32[]{:S(2)}) collective-permute-start(bf16[4,4,128,256]{3,2,1,0:T(8,128)(2,1)} %get-tuple-element.61), channel_id=1, source_target_pairs={{0,4},{1,5},{2,6},{3,7},{4,8},{5,9},{6,10},{7,11},{8,12},{9,13},{1... | collective-permute-start | bytes 3145736 | tf_op jit(solution)/shard_map/ppermute | solution.py:33
  11.0 48.4 %collective-permute-start.18 = (bf16[4,4,128,256]{3,2,1,0:T(8,128)(2,1)}, bf16[4,4,128,256]{3,2,1,0:T(8,128)(2,1)S(1)}, u32[]{:S(2)}, u32[]{:S(2)}) collective-permute-start(bf16[4,4,128,256]{3,2,1,0:T(8,128)(2,1)} %get-tuple-element.62), channel_id=1, source_target_pairs={{0,8},{1,9},{2,10},{3,11},{4,12},{5,13},{6,14},{7,15},{8,0},{9,1},... | collective-permute-start | bytes 3145736 | tf_op jit(solution)/shard_map/ppermute | solution.py:33
  13.9 48.1 %collective-permute-start.19 = (bf16[4,4,128,256]{3,2,1,0:T(8,128)(2,1)}, bf16[4,4,128,256]{3,2,1,0:T(8,128)(2,1)}, u32[]{:S(2)}, u32[]{:S(2)}) collective-permute-start(bf16[4,4,128,256]{3,2,1,0:T(8,128)(2,1)} %get-tuple-element.63), channel_id=1, source_target_pairs={{0,12},{1,13},{2,14},{3,15},{4,0},{5,1},{6,2},{7,3},{8,4},{9,5},{1... | collective-permute-start | bytes 3145736 | tf_op jit(solution)/shard_map/ppermute | solution.py:33
  22.6 42.1 %collective-permute-start.14 = (bf16[4,4,128,256]{3,2,1,0:T(8,128)(2,1)}, bf16[4,4,128,256]{3,2,1,0:T(8,128)(2,1)S(1)}, u32[]{:S(2)}, u32[]{:S(2)}) collective-permute-start(bf16[4,4,128,256]{3,2,1,0:T(8,128)(2,1)} %get-tuple-element.57), channel_id=1, source_target_pairs={{0,1},{1,2},{2,3},{3,0},{4,5},{5,6},{6,7},{7,4},{8,9},{9,10},{10,1... | collective-permute-start | bytes 3145736 | tf_op jit(solution)/shard_map/ppermute | solution.py:33
  24.1 98.4 %collective-permute-start.15 = (bf16[4,4,128,256]{3,2,1,0:T(8,128)(2,1)}, bf16[4,4,128,256]{3,2,1,0:T(8,128)(2,1)}, u32[]{:S(2)}, u32[]{:S(2)}) collective-permute-start(bf16[4,4,128,256]{3,2,1,0:T(8,128)(2,1)} %get-tuple-element.58), channel_id=1, source_target_pairs={{0,2},{1,3},{2,0},{3,1},{4,6},{5,7},{6,4},{7,5},{8,10},{9,11},{10,... | collective-permute-start | bytes 3145736 | tf_op jit(solution)/shard_map/ppermute | solution.py:33
  35.8 89.7 %collective-permute-start.16 = (bf16[4,4,128,256]{3,2,1,0:T(8,128)(2,1)}, bf16[4,4,128,256]{3,2,1,0:T(8,128)(2,1)}, u32[]{:S(2)}, u32[]{:S(2)}) collective-permute-start(bf16[4,4,128,256]{3,2,1,0:T(8,128)(2,1)} %get-tuple-element.59), channel_id=1, source_target_pairs={{0,3},{1,0},{2,1},{3,2},{4,7},{5,4},{6,5},{7,6},{8,11},{9,8},{10,9... | collective-permute-start | bytes 3145736 | tf_op jit(solution)/shard_map/ppermute | solution.py:33
  60.5 66.6 %collective-permute-start = (bf16[4,4,128,256]{3,2,1,0:T(8,128)(2,1)}, bf16[4,4,128,256]{3,2,1,0:T(8,128)(2,1)S(1)}, u32[]{:S(2)}, u32[]{:S(2)}) collective-permute-start(bf16[4,4,128,256]{3,2,1,0:T(8,128)(2,1)} %get-tuple-element.41), channel_id=1, source_target_pairs={{0,1},{1,2},{2,3},{3,0},{4,5},{5,6},{6,7},{7,4},{8,9},{9,10},{10,1... | collective-permute-start | bytes 3145736 | tf_op jit(solution)/shard_map/ppermute | solution.py:33
  62.0 65.1 %collective-permute-start.1 = (bf16[4,4,128,256]{3,2,1,0:T(8,128)(2,1)}, bf16[4,4,128,256]{3,2,1,0:T(8,128)(2,1)S(1)}, u32[]{:S(2)}, u32[]{:S(2)}) collective-permute-start(bf16[4,4,128,256]{3,2,1,0:T(8,128)(2,1)} %get-tuple-element.42), channel_id=1, source_target_pairs={{0,2},{1,3},{2,0},{3,1},{4,6},{5,7},{6,4},{7,5},{8,10},{9,11},{10,... | collective-permute-start | bytes 3145736 | tf_op jit(solution)/shard_map/ppermute | solution.py:33
  64.7 64.4 %collective-permute-start.2 = (bf16[4,4,128,256]{3,2,1,0:T(8,128)(2,1)}, bf16[4,4,128,256]{3,2,1,0:T(8,128)(2,1)}, u32[]{:S(2)}, u32[]{:S(2)}) collective-permute-start(bf16[4,4,128,256]{3,2,1,0:T(8,128)(2,1)} %get-tuple-element.43), channel_id=1, source_target_pairs={{0,3},{1,0},{2,1},{3,2},{4,7},{5,4},{6,5},{7,6},{8,11},{9,8},{10,9... | collective-permute-start | bytes 3145736 | tf_op jit(solution)/shard_map/ppermute | solution.py:33
  67.0 15.8 %all-to-all-start.1 = ((bf16[8,64,512]{2,1,0:T(8,128)(2,1)}), bf16[8,64,512]{2,1,0:T(8,128)(2,1)}, u32[]{:S(2)}, u32[]{:S(2)}) async-start(bf16[8,64,512]{2,1,0:T(8,128)(2,1)} %broadcast_in_dim.40), calls=%async_computation.1 | async-start | bytes 1048576 | tf_op jit(solution)/shard_map/all_to_all | solution.py:286
  83.3 35.9 %all-to-all-start = ((s32[16,1,128]{2,1,0:T(1,128)}), s32[16,1,128]{2,1,0:T(1,128)S(1)}, u32[]{:S(2)}, u32[]{:S(2)}) async-start(s32[16,1,128]{2,1,0:T(1,128)} %broadcast_in_dim.23), calls=%async_computation | async-start | bytes 16384 | tf_op jit(solution)/shard_map/all_to_all | solution.py:286
  122.5 12.1 %collective-permute-start.24 = (bf16[8,128,256]{2,1,0:T(8,128)(2,1)}, bf16[8,128,256]{2,1,0:T(8,128)(2,1)}, u32[]{:S(2)}, u32[]{:S(2)}) collective-permute-start(bf16[8,128,256]{2,1,0:T(8,128)(2,1)} %get-tuple-element.68), channel_id=1, source_target_pairs={{0,1},{1,2},{2,3},{3,0},{4,5},{5,6},{6,7},{7,4},{8,9},{9,10},{10,1... | collective-permute-start | bytes 1572872 | tf_op jit(solution)/shard_map/ppermute | solution.py:33
  125.5 10.4 %collective-permute-start.25 = (bf16[8,128,256]{2,1,0:T(8,128)(2,1)}, bf16[8,128,256]{2,1,0:T(8,128)(2,1)}, u32[]{:S(2)}, u32[]{:S(2)}) collective-permute-start(bf16[8,128,256]{2,1,0:T(8,128)(2,1)} %get-tuple-element.69), channel_id=1, source_target_pairs={{0,3},{1,0},{2,1},{3,2},{4,7},{5,4},{6,5},{7,6},{8,11},{9,8},{10,9... | collective-permute-start | bytes 1572872 | tf_op jit(solution)/shard_map/ppermute | solution.py:33
  127.1 68.6 %collective-permute-start.3 = (bf16[4,4,128,256]{3,2,1,0:T(8,128)(2,1)}, bf16[4,4,128,256]{3,2,1,0:T(8,128)(2,1)S(1)}, u32[]{:S(2)}, u32[]{:S(2)}) collective-permute-start(bf16[4,4,128,256]{3,2,1,0:T(8,128)(2,1)} %get-tuple-element.45), channel_id=1, source_target_pairs={{0,4},{1,5},{2,6},{3,7},{4,8},{5,9},{6,10},{7,11},{8,12},{9,13},{1... | collective-permute-start | bytes 3145736 | tf_op jit(solution)/shard_map/ppermute | solution.py:33
  127.1 69.2 %collective-permute-start.4 = (bf16[4,4,128,256]{3,2,1,0:T(8,128)(2,1)}, bf16[4,4,128,256]{3,2,1,0:T(8,128)(2,1)}, u32[]{:S(2)}, u32[]{:S(2)}) collective-permute-start(bf16[4,4,128,256]{3,2,1,0:T(8,128)(2,1)} %get-tuple-element.46), channel_id=1, source_target_pairs={{0,8},{1,9},{2,10},{3,11},{4,12},{5,13},{6,14},{7,15},{8,0},{9,1},... | collective-permute-start | bytes 3145736 | tf_op jit(solution)/shard_map/ppermute | solution.py:33
  129.1 69.9 %collective-permute-start.5 = (bf16[4,4,128,256]{3,2,1,0:T(8,128)(2,1)}, bf16[4,4,128,256]{3,2,1,0:T(8,128)(2,1)}, u32[]{:S(2)}, u32[]{:S(2)}) collective-permute-start(bf16[4,4,128,256]{3,2,1,0:T(8,128)(2,1)} %get-tuple-element.47), channel_id=1, source_target_pairs={{0,12},{1,13},{2,14},{3,15},{4,0},{5,1},{6,2},{7,3},{8,4},{9,5},{1... | collective-permute-start | bytes 3145736 | tf_op jit(solution)/shard_map/ppermute | solution.py:33
  134.6 49.4 %collective-permute-start.20 = (bf16[8,128,256]{2,1,0:T(8,128)(2,1)}, bf16[8,128,256]{2,1,0:T(8,128)(2,1)}, u32[]{:S(2)}, u32[]{:S(2)}) collective-permute-start(bf16[8,128,256]{2,1,0:T(8,128)(2,1)} %get-tuple-element.64), channel_id=1, source_target_pairs={{0,4},{1,5},{2,6},{3,7},{4,8},{5,9},{6,10},{7,11},{8,12},{9,13},{1... | collective-permute-start | bytes 1572872 | tf_op jit(solution)/shard_map/ppermute | solution.py:33
  135.9 48.3 %collective-permute-start.21 = (bf16[8,128,256]{2,1,0:T(8,128)(2,1)}, bf16[8,128,256]{2,1,0:T(8,128)(2,1)}, u32[]{:S(2)}, u32[]{:S(2)}) collective-permute-start(bf16[8,128,256]{2,1,0:T(8,128)(2,1)} %get-tuple-element.65), channel_id=1, source_target_pairs={{0,12},{1,13},{2,14},{3,15},{4,0},{5,1},{6,2},{7,3},{8,4},{9,5},{1... | collective-permute-start | bytes 1572872 | tf_op jit(solution)/shard_map/ppermute | solution.py:33
  184.0 17.8 %collective-permute-start.6 = (bf16[8,128,256]{2,1,0:T(8,128)(2,1)}, bf16[8,128,256]{2,1,0:T(8,128)(2,1)S(1)}, u32[]{:S(2)}, u32[]{:S(2)}) collective-permute-start(bf16[8,128,256]{2,1,0:T(8,128)(2,1)} %get-tuple-element.48), channel_id=1, source_target_pairs={{0,4},{1,5},{2,6},{3,7},{4,8},{5,9},{6,10},{7,11},{8,12},{9,13},{1... | collective-permute-start | bytes 1572872 | tf_op jit(solution)/shard_map/ppermute | solution.py:33
  184.2 17.7 %collective-permute-start.7 = (bf16[8,128,256]{2,1,0:T(8,128)(2,1)}, bf16[8,128,256]{2,1,0:T(8,128)(2,1)S(1)}, u32[]{:S(2)}, u32[]{:S(2)}) collective-permute-start(bf16[8,128,256]{2,1,0:T(8,128)(2,1)} %get-tuple-element.49), channel_id=1, source_target_pairs={{0,12},{1,13},{2,14},{3,15},{4,0},{5,1},{6,2},{7,3},{8,4},{9,5},{1... | collective-permute-start | bytes 1572872 | tf_op jit(solution)/shard_map/ppermute | solution.py:33
  195.7 42.4 %collective-permute-start.26 = (bf16[16,128,256]{2,1,0:T(8,128)(2,1)}, bf16[16,128,256]{2,1,0:T(8,128)(2,1)}, u32[]{:S(2)}, u32[]{:S(2)}) collective-permute-start(bf16[16,128,256]{2,1,0:T(8,128)(2,1)} %get-tuple-element.70), channel_id=1, source_target_pairs={{0,1},{1,2},{2,3},{3,0},{4,5},{5,6},{6,7},{7,4},{8,9},{9,10},{10,1... | collective-permute-start | bytes 3145736 | tf_op jit(solution)/shard_map/ppermute | solution.py:33
  196.3 43.2 %collective-permute-start.27 = (bf16[16,128,256]{2,1,0:T(8,128)(2,1)}, bf16[16,128,256]{2,1,0:T(8,128)(2,1)}, u32[]{:S(2)}, u32[]{:S(2)}) collective-permute-start(bf16[16,128,256]{2,1,0:T(8,128)(2,1)} %get-tuple-element.71), channel_id=1, source_target_pairs={{0,3},{1,0},{2,1},{3,2},{4,7},{5,4},{6,5},{7,6},{8,11},{9,8},{10,9... | collective-permute-start | bytes 3145736 | tf_op jit(solution)/shard_map/ppermute | solution.py:33
  199.0 40.7 %collective-permute-start.22 = (bf16[16,128,256]{2,1,0:T(8,128)(2,1)}, bf16[16,128,256]{2,1,0:T(8,128)(2,1)}, u32[]{:S(2)}, u32[]{:S(2)}) collective-permute-start(bf16[16,128,256]{2,1,0:T(8,128)(2,1)} %get-tuple-element.66), channel_id=1, source_target_pairs={{0,4},{1,5},{2,6},{3,7},{4,8},{5,9},{6,10},{7,11},{8,12},{9,13},{1... | collective-permute-start | bytes 3145736 | tf_op jit(solution)/shard_map/ppermute | solution.py:33
  201.8 30.0 %collective-permute-start.10 = (bf16[8,128,256]{2,1,0:T(8,128)(2,1)}, bf16[8,128,256]{2,1,0:T(8,128)(2,1)S(1)}, u32[]{:S(2)}, u32[]{:S(2)}) collective-permute-start(bf16[8,128,256]{2,1,0:T(8,128)(2,1)} %get-tuple-element.52), channel_id=1, source_target_pairs={{0,1},{1,2},{2,3},{3,0},{4,5},{5,6},{6,7},{7,4},{8,9},{9,10},{10,1... | collective-permute-start | bytes 1572872 | tf_op jit(solution)/shard_map/ppermute | solution.py:33
  201.9 30.0 %collective-permute-start.11 = (bf16[8,128,256]{2,1,0:T(8,128)(2,1)}, bf16[8,128,256]{2,1,0:T(8,128)(2,1)S(1)}, u32[]{:S(2)}, u32[]{:S(2)}) collective-permute-start(bf16[8,128,256]{2,1,0:T(8,128)(2,1)} %get-tuple-element.53), channel_id=1, source_target_pairs={{0,3},{1,0},{2,1},{3,2},{4,7},{5,4},{6,5},{7,6},{8,11},{9,8},{10,9... | collective-permute-start | bytes 1572872 | tf_op jit(solution)/shard_map/ppermute | solution.py:33
  231.8 26.3 %collective-permute-start.23 = (bf16[16,128,256]{2,1,0:T(8,128)(2,1)}, bf16[16,128,256]{2,1,0:T(8,128)(2,1)}, u32[]{:S(2)}, u32[]{:S(2)}) collective-permute-start(bf16[16,128,256]{2,1,0:T(8,128)(2,1)} %get-tuple-element.67), channel_id=1, source_target_pairs={{0,12},{1,13},{2,14},{3,15},{4,0},{5,1},{6,2},{7,3},{8,4},{9,5},{1... | collective-permute-start | bytes 3145736 | tf_op jit(solution)/shard_map/ppermute | solution.py:33
  231.9 42.9 %collective-permute-start.8 = (bf16[16,128,256]{2,1,0:T(8,128)(2,1)}, bf16[16,128,256]{2,1,0:T(8,128)(2,1)}, u32[]{:S(2)}, u32[]{:S(2)}) collective-permute-start(bf16[16,128,256]{2,1,0:T(8,128)(2,1)} %get-tuple-element.50), channel_id=1, source_target_pairs={{0,4},{1,5},{2,6},{3,7},{4,8},{5,9},{6,10},{7,11},{8,12},{9,13},{1... | collective-permute-start | bytes 3145736 | tf_op jit(solution)/shard_map/ppermute | solution.py:33
  238.2 38.9 %collective-permute-start.9 = (bf16[16,128,256]{2,1,0:T(8,128)(2,1)}, bf16[16,128,256]{2,1,0:T(8,128)(2,1)}, u32[]{:S(2)}, u32[]{:S(2)}) collective-permute-start(bf16[16,128,256]{2,1,0:T(8,128)(2,1)} %get-tuple-element.51), channel_id=1, source_target_pairs={{0,12},{1,13},{2,14},{3,15},{4,0},{5,1},{6,2},{7,3},{8,4},{9,5},{1... | collective-permute-start | bytes 3145736 | tf_op jit(solution)/shard_map/ppermute | solution.py:33
  239.5 37.5 %collective-permute-start.12 = (bf16[16,128,256]{2,1,0:T(8,128)(2,1)}, bf16[16,128,256]{2,1,0:T(8,128)(2,1)}, u32[]{:S(2)}, u32[]{:S(2)}) collective-permute-start(bf16[16,128,256]{2,1,0:T(8,128)(2,1)} %get-tuple-element.54), channel_id=1, source_target_pairs={{0,1},{1,2},{2,3},{3,0},{4,5},{5,6},{6,7},{7,4},{8,9},{9,10},{10,1... | collective-permute-start | bytes 3145736 | tf_op jit(solution)/shard_map/ppermute | solution.py:33
  239.7 37.3 %collective-permute-start.13 = (bf16[16,128,256]{2,1,0:T(8,128)(2,1)}, bf16[16,128,256]{2,1,0:T(8,128)(2,1)}, u32[]{:S(2)}, u32[]{:S(2)}) collective-permute-start(bf16[16,128,256]{2,1,0:T(8,128)(2,1)} %get-tuple-element.55), channel_id=1, source_target_pairs={{0,3},{1,0},{2,1},{3,2},{4,7},{5,4},{6,5},{7,6},{8,11},{9,8},{10,9... | collective-permute-start | bytes 3145736 | tf_op jit(solution)/shard_map/ppermute | solution.py:33
  313.2 7.2 %collective-permute-start.29 = (bf16[32,1024]{1,0:T(8,128)(2,1)S(1)}, bf16[32,1024]{1,0:T(8,128)(2,1)S(1)}, u32[]{:S(2)}, u32[]{:S(2)}) collective-permute-start(bf16[32,1024]{1,0:T(8,128)(2,1)S(1)} %fusion), channel_id=1, source_target_pairs={{0,32},{16,48},{32,64},{48,80},{64,96},{80,112},{96,0},{112,16},{1... | collective-permute-start | bytes 196616 | tf_op jit(solution)/shard_map/ppermute | solution.py:41
  315.7 7.4 %collective-permute-start.30 = (bf16[32,1024]{1,0:T(8,128)(2,1)S(1)}, bf16[32,1024]{1,0:T(8,128)(2,1)S(1)}, u32[]{:S(2)}, u32[]{:S(2)}) collective-permute-start(bf16[32,1024]{1,0:T(8,128)(2,1)S(1)} %fusion), channel_id=1, source_target_pairs={{0,64},{16,80},{32,96},{48,112},{64,0},{80,16},{96,32},{112,48},{1... | collective-permute-start | bytes 196616 | tf_op jit(solution)/shard_map/ppermute | solution.py:41
  (27 other events, 355.6 us)

commit v3 on v2

--- a/solution.py
+++ b/solution.py
@@ -77,7 +77,43 @@
     )(order, src, blocks, *[tiles] * RING, *after)
 
 
+def pair_kernel(shift_by, order0_ref, order1_ref, src_ref, emb_ref, *refs):
+    d = pl.program_id(0)
+    part = emb_ref.shape[2] // 2
+    for half, order_ref in enumerate((order0_ref, order1_ref)):
+        tile_ref, out_ref = refs[half], refs[2 + half]
+        p = order_ref[shift_by * RING + d]
+        for q in range(tile_ref.shape[1]):
+            out_ref[0, q] = jnp.dot(
+                tile_ref[0, q], emb_ref[src_ref[p, q], :, half * part:(half + 1) * part],
+                preferred_element_type=F32,
+            ).astype(BF)
+
+
+def message_pair(orders, src, blocks, tiles, row, rows, by):
+    _, cap, blk, _ = tiles.shape
+    n_blk, _, width = blocks.shape
+    at = row // rows
+    shape = (RING, cap, rows, width // 2)
+    return pl.pallas_call(
+        functools.partial(pair_kernel, by),
+        grid_spec=pltpu.PrefetchScalarGridSpec(
+            num_scalar_prefetch=3,
+            grid=(RING,),
+            in_specs=[
+                pl.BlockSpec((n_blk, blk, width), lambda i, a, b, s: (0, 0, 0),
+                             pipeline_mode=pl.Buffered(1)),
+                pl.BlockSpec((1, cap, rows, blk), lambda i, a, b, s: (a[by * RING + i], 0, at, 0)),
+                pl.BlockSpec((1, cap, rows, blk), lambda i, a, b, s: (b[by * RING + i], 0, at, 0)),
+            ],
+            out_specs=[pl.BlockSpec((1,) + shape[1:], lambda i, a, b, s: (i, 0, 0, 0))] * 2,
+        ),
+        out_shape=[jax.ShapeDtypeStruct(shape, BF)] * 2,
+    )(*orders, src, blocks, tiles, tiles)
+
+
 def add_slots(acc_ref, table_ref, y, x, half, ahead, parts, columns):
+    local = table_ref.shape[0] == RING
     n_blk = acc_ref.shape[0]
     cap = parts[0].shape[1]
     for came, ref in enumerate(parts):
@@ -87,6 +123,7 @@
         else:
             s = wrap(y - came) * RING + x
             p = y * RING + wrap(x + ahead)
+        s = came if local else s
 
         def add(q, carry):
             dst = table_ref[s, p * 2 * cap + q]
@@ -165,6 +202,10 @@
     )(pos, table, *parts, *parts, low, high)
 
 
+def sigmoid(v):
+    return 0.5 * jnp.tanh(0.5 * v) + 0.5
+
+
 def head_kernel(first, last, row, blk, labels_total, pos_count,
                 pos_ref, table_ref, inv_ref, near_ref, *refs):
     mine = (refs[:RING], refs[RING:2 * RING])
@@ -176,9 +217,9 @@
         gd_in, gw_in, _ = rest[:3]
         rest = rest[3:]
     if last:
-        hid_ref, both_ref, acc_ref, agg_ref, ds_ref, gd_ref, gw_ref = rest
+        hid_ref, both_ref, acc_ref, agg_ref, ds_ref, prob_ref, gd_ref, gw_ref = rest
     else:
-        hid_ref, gd_ref, gw_ref, acc_ref, agg_ref, ds_ref = rest
+        hid_ref, gd_ref, gw_ref, acc_ref, agg_ref, ds_ref, prob_ref = rest
     step = pl.program_id(0)
 
     @pl.when(step == 0)
@@ -205,26 +246,32 @@
         agg_ref[b * rows:(b + 1) * rows, :] = (acc_ref[b] * inv_ref[b]).astype(BF)
     agg = agg_ref[...]
     pre = jnp.dot(agg, w_ref[...], preferred_element_type=F32)
-    sig = 1.0 / (1.0 + jnp.exp(-pre))
+    sig = sigmoid(pre)
     hid = (pre * sig).astype(BF)
     for b in range(n_blk):
         hid_ref[b] = hid[b * rows:(b + 1) * rows, :]
     scores = lax.dot_general(hid, docs_ref[...], (((1,), (1,)), ((), ())),
                              preferred_element_type=F32)
-    prob = 1.0 / (1.0 + jnp.exp(-scores))
-    for b in range(n_blk):
-        one = prob[b * rows:(b + 1) * rows, :]
-        ds_ref[b * rows:(b + 1) * rows, :] = (one * (1.0 / labels_total)).astype(BF)
-
-        @pl.when(near_ref[(b * blk + row) // rows + step] > 0)
+    prob = sigmoid(scores)
+    prob_ref[...] = prob
+    ds_ref[...] = (prob * (1.0 / labels_total)).astype(BF)
+
+    def mark(b, carry):
+        @pl.when(near_ref[b * (blk // rows) + row // rows + step] > 0)
         def _():
+            here = pl.ds(pl.multiple_of(b * rows, rows), rows)
+            one = prob_ref[here, :]
             ids = b * blk + row + step * rows + lax.broadcasted_iota(jnp.int32, one.shape, 0)
             hit = labels_ref[0:1, :] == ids
             for j in range(1, labels_ref.shape[0]):
                 hit = hit | (labels_ref[j:j + 1, :] == ids)
-            ds_ref[b * rows:(b + 1) * rows, :] = jnp.where(
+            ds_ref[here, :] = jnp.where(
                 hit, (one - 1.0) * (1.0 / pos_count), one * (1.0 / labels_total)
             ).astype(BF)
+
+        return carry
+
+    lax.fori_loop(0, n_blk, mark, 0)
     ds = ds_ref[...]
     gd_ref[...] += lax.dot_general(ds, hid, (((0,), (0,)), ((), ())),
                                    preferred_element_type=F32)
@@ -275,7 +322,8 @@
         + [jax.ShapeDtypeStruct(a, t) for a, t in grads],
         scratch_shapes=[pltpu.VMEM((n_blk, step_rows, width), F32),
                         pltpu.VMEM((n_blk * step_rows, width), BF),
-                        pltpu.VMEM((n_blk * step_rows, n_doc), BF)]
+                        pltpu.VMEM((n_blk * step_rows, n_doc), BF),
+                        pltpu.VMEM((n_blk * step_rows, n_doc), F32)]
         + ([pltpu.VMEM((n_doc, width), F32), pltpu.VMEM((width, width), F32)] if last else []),
         input_output_aliases=aliases,
         compiler_params=pltpu.CompilerParams(vmem_limit_bytes=48 << 20),
@@ -308,7 +356,9 @@
     orders = (wrap(y + inner) * RING + wrap(x + outer), wrap(y + outer) * RING + wrap(x + inner))
     axes = (("x", "y"), ("y", "x"))
 
-    table = jnp.concatenate([msg_dst, msg_count], axis=1).reshape(-1)
+    own_table = jnp.concatenate([msg_dst, msg_count], axis=1).reshape(1, -1)
+    near_table = jnp.concatenate([own_table] + [shift(own_table, "x", j) for j in range(1, RING)])
+    table = own_table.reshape(-1)
     table = spread(table, "col", n_col).reshape(n_col, n_col * 2 * cap)
     share = docs.shape[0] // n_col
     regroup = lambda a: a.reshape((n_row, n_col, share) + a.shape[1:]).swapaxes(0, 1).reshape(a.shape)
@@ -323,25 +373,32 @@
     lows = [[None, None] for _ in CHUNK_ROWS]
     ends = [[None, None] for _ in CHUNK_ROWS]
 
+    def send_first():
+        came[0] = [[None] * RING, [None] * RING]
+        for j in (1, 3, 2, 0):
+            out = message_pair(orders, msg_src, blocks, tiles,
+                        starts[0], CHUNK_ROWS[0], j)
+            for half in range(2):
+                came[0][half][j] = shift(out[half], axes[half][0], j) if j else out[half]
+
     def send(k):
         for half in range(2):
-            after = [gathered] if (k, half) == (1, 1) else []
-            after = after + lows[k - 2] if k >= 2 else after
             out = messages_of(orders[half], msg_src, blocks, tiles,
-                        starts[k], CHUNK_ROWS[k], half, after)
+                        starts[k], CHUNK_ROWS[k], half, [came[0][0][0]])
             came[k][half] = [out[0]] + [shift(out[j], axes[half][0], j) for j in range(1, RING)]
 
     def combine(k):
         for half in range(2):
             second = axes[half][1]
             after = [came[k + 1][h][0] for h in range(2)] if k + 1 < n_chunk else []
-            low, high = far_sums(half, pos, table, came[k][half],
+            rows_of = near_table if (k, half) == (0, 0) else table
+            low, high = far_sums(half, pos, rows_of, came[k][half],
                               blk_dev, after)
             lows[k][half] = low
             ends[k][half] = (shift(low, second, 1),
                              shift(high, second, -1))
 
-    send(0)
+    send_first()
     for k in range(n_chunk):
         if k + 1 < n_chunk:
             send(k + 1)

time: 342 us -> 330 us (0.965)
  waiting for transfers between devices: 135 us -> 112 us
  Pallas kernels: 84.9 us -> 95.8 us
    pallas_call x0 -> x4, Pallas kernels: none -> 25.4 us  [message_pair(): pl.pallas_call(functools.partial(pair_kernel, by), grid_spec=pltpu.Prefet...]
    ppermute x28 -> x31, waiting for transfers between devices: 103 us -> 79.8 us  [shift(): return lax.ppermute(v, 'col', shift_pairs(axis, by))]
    pallas_call x4 -> x2, Pallas kernels: 27.4 us -> 13.6 us  [messages_of(): pl.pallas_call(message_kernel, grid_spec=pltpu.PrefetchScalarGridSpec(num...]
    all_to_all x2, starting transfers between devices: 17 us -> 11.5 us  [swap(): return lax.all_to_all(x, axis, split_axis=0, concat_axis=0, tiled=True)]
    ppermute x28 -> x31, starting transfers between devices: 46.5 us -> 49.8 us  [shift(): return lax.ppermute(v, 'col', shift_pairs(axis, by))]
  transfers between devices with their start and end apart: 34 -> 37, of which waited for: 14 -> 14; matrix products, arithmetic and copies ran while one was open for 2% -> 3% of each run, Pallas kernels for 18% -> 23%
where the time goes in v3:
time: 330 us; the launch traced here: 329 us
  waiting for transfers between devices  112 us (34%)
  Pallas kernels  95.8 us (29%)
  starting transfers between devices  67.7 us (21%)
  blocking collectives  36.4 us (11%)
  local copies, waits for them, and re-layouts  13.2 us (4%)
  other arithmetic  3.66 us (1%)
    ppermute x31, waiting for transfers between devices, shift(): return lax.ppermute(v, 'col', shift_pairs(axis, by))  79.8 us
    ppermute x31, starting transfers between devices, shift(): return lax.ppermute(v, 'col', shift_pairs(axis, by))  49.8 us
    all_to_all x2, blocking collectives, swap(): return lax.all_to_all(x, axis, split_axis=0, concat_axis=0, tiled=True)  36.4 us
    pallas_call x2, Pallas kernels, head(): pl.pallas_call(functools.partial(head_kernel, first, last, row, blk, labe...  28.7 us
    all_to_all x2, waiting for transfers between devices, swap(): return lax.all_to_all(x, axis, split_axis=0, concat_axis=0, tiled=True)  27.9 us
    pallas_call x4, Pallas kernels, message_pair(): pl.pallas_call(functools.partial(pair_kernel, by), grid_spec=pltpu.Prefet...  25.4 us
    pallas_call x4, Pallas kernels, near_sums(): pl.pallas_call(functools.partial(near_kernel, half), grid=(rows // step_r...  17.1 us
    pallas_call x2, Pallas kernels, messages_of(): pl.pallas_call(message_kernel, grid_spec=pltpu.PrefetchScalarGridSpec(num...  13.6 us
  transfers between devices with their start and end apart: 37, of which 14 were waited for; matrix products, arithmetic and copies ran while one was open for 3% of the time, Pallas kernels for 23%

profile of v3, /device:TPU:0, one launch (start us, length us, event | category | flops | bytes accessed | tf_op | source)
XLA Modules:
  0.0 329.3 jit_solution(10735079180359232186)
XLA Ops:
  2.6 6.3 %shard_map.110 = (bf16[4,4,128,256]{3,2,1,0:T(8,128)(2,1)}, bf16[4,4,128,256]{3,2,1,0:T(8,128)(2,1)}) custom-call(s32[16]{0:T(128)} %get-tuple-element.81.order0_ref.order_ref, s32[16]{0:T(128)} %get-tuple-element.82.order1_ref.order_ref, s32[16,4]{1,0:T(8,128)} %copy.63.src_ref, bf16[16,256,512]{2,1,0:T(8,128)(2,1)} %bitcast.34, ...), custom_call_target="tpu_custom_call" | custom-call | tf_op jit(solution)/shard_map/pallas_call | solution.py:98
  10.6 6.4 %shard_map.111 = (bf16[4,4,128,256]{3,2,1,0:T(8,128)(2,1)}, bf16[4,4,128,256]{3,2,1,0:T(8,128)(2,1)}) custom-call(s32[16]{0:T(128)} %get-tuple-element.81.order0_ref.order_ref, s32[16]{0:T(128)} %get-tuple-element.82.order1_ref.order_ref, s32[16,4]{1,0:T(8,128)} %copy.63.src_ref, bf16[16,256,512]{2,1,0:T(8,128)(2,1)} %bitcast.35, ...), custom_call_target="tpu_custom_call" | custom-call | tf_op jit(solution)/shard_map/pallas_call | solution.py:98
  17.0 3.0 collective-permute-start.18
  20.0 6.3 %shard_map.112 = (bf16[4,4,128,256]{3,2,1,0:T(8,128)(2,1)}, bf16[4,4,128,256]{3,2,1,0:T(8,128)(2,1)}) custom-call(s32[16]{0:T(128)} %get-tuple-element.81.order0_ref.order_ref, s32[16]{0:T(128)} %get-tuple-element.82.order1_ref.order_ref, s32[16,4]{1,0:T(8,128)} %copy.63.src_ref, bf16[16,256,512]{2,1,0:T(8,128)(2,1)} %bitcast.36, ...), custom_call_target="tpu_custom_call" | custom-call | tf_op jit(solution)/shard_map/pallas_call | solution.py:98
  30.9 22.3 %collective-permute-done.20 = s32[1,128]{1,0:T(1,128)S(1)} collective-permute-done((s32[1,128]{1,0:T(1,128)S(1)}, s32[1,128]{1,0:T(1,128)S(1)}, u32[]{:S(2)}, u32[]{:S(2)}) %collective-permute-start.20) | collective-permute-done | bytes 544 | tf_op jit(solution)/shard_map/ppermute | solution.py:33
  55.0 3.3 collective-permute-done.21
  64.8 6.3 %shard_map.103 = (bf16[4,4,128,256]{3,2,1,0:T(8,128)(2,1)}, bf16[4,4,128,256]{3,2,1,0:T(8,128)(2,1)}) custom-call(s32[16]{0:T(128)} %get-tuple-element.81.order0_ref.order_ref, s32[16]{0:T(128)} %get-tuple-element.82.order1_ref.order_ref, s32[16,4]{1,0:T(8,128)} %copy.63.src_ref, bf16[16,256,512]{2,1,0:T(8,128)(2,1)} %bitcast.37, ...), custom_call_target="tpu_custom_call" | custom-call | tf_op jit(solution)/shard_map/pallas_call | solution.py:98
  71.1 6.8 %shard_map.105 = (bf16[4,4,128,256]{3,2,1,0:T(8,128)(2,1)}, bf16[4,4,128,256]{3,2,1,0:T(8,128)(2,1)}, bf16[4,4,128,256]{3,2,1,0:T(8,128)(2,1)}, bf16[4,4,128,256]{3,2,1,0:T(8,128)(2,1)}) custom-call(s32[16]{0:T(128)} %get-tuple-element.82.order1_ref.order_ref, s32[16,4]{1,0:T(8,128)} %copy.63.src_ref, bf16[16,256,512]{2,1,0:T(8,128)(2,1)} %bitcast.38, ...), custom_call_target="tpu_custom_call" | custom-call | tf_op jit(solution)/shard_map/pallas_call | solution.py:61
  82.2 6.3 %all-to-all-start = ((s32[16,1,128]{2,1,0:T(1,128)}), s32[16,1,128]{2,1,0:T(1,128)S(1)}, u32[]{:S(2)}, u32[]{:S(2)}) async-start(s32[16,1,128]{2,1,0:T(1,128)} %broadcast_in_dim.23), calls=%async_computation | async-start | bytes 16384 | tf_op jit(solution)/shard_map/all_to_all | solution.py:334
  89.1 6.8 %shard_map.104 = (bf16[4,4,128,256]{3,2,1,0:T(8,128)(2,1)}, bf16[4,4,128,256]{3,2,1,0:T(8,128)(2,1)}, bf16[4,4,128,256]{3,2,1,0:T(8,128)(2,1)}, bf16[4,4,128,256]{3,2,1,0:T(8,128)(2,1)}) custom-call(s32[16]{0:T(128)} %get-tuple-element.81.order0_ref.order_ref, s32[16,4]{1,0:T(8,128)} %copy.63.src_ref, bf16[16,256,512]{2,1,0:T(8,128)(2,1)} %bitcast.39, ...), custom_call_target="tpu_custom_call" | custom-call | tf_op jit(solution)/shard_map/pallas_call | solution.py:61
  96.0 27.9 %all-to-all-done = s32[16,1,128]{2,1,0:T(1,128)S(1)} async-done(((s32[16,1,128]{2,1,0:T(1,128)}), s32[16,1,128]{2,1,0:T(1,128)S(1)}, u32[]{:S(2)}, u32[]{:S(2)}) %all-to-all-start) | async-done | bytes 8224 | tf_op jit(solution)/shard_map/all_to_all | solution.py:334
  124.5 2.7 shard_map.115
  138.8 4.8 %collective-permute-done.27.refs_8_ = bf16[8,128,256]{2,1,0:T(8,128)(2,1)} collective-permute-done((bf16[8,128,256]{2,1,0:T(8,128)(2,1)}, bf16[8,128,256]{2,1,0:T(8,128)(2,1)}, u32[]{:S(2)}, u32[]{:S(2)}) %collective-permute-start.27) | collective-permute-done | bytes 524320 | tf_op jit(solution)/shard_map/ppermute | solution.py:33
  143.8 21.6 %collective-permute-done.28.refs_9_ = bf16[8,128,256]{2,1,0:T(8,128)(2,1)} collective-permute-done((bf16[8,128,256]{2,1,0:T(8,128)(2,1)}, bf16[8,128,256]{2,1,0:T(8,128)(2,1)}, u32[]{:S(2)}, u32[]{:S(2)}) %collective-permute-start.28) | collective-permute-done | bytes 524320 | tf_op jit(solution)/shard_map/ppermute | solution.py:33
  168.0 2.8 shard_map.108
  175.0 3.8 %collective-permute-start.11 = (bf16[8,128,256]{2,1,0:T(8,128)(2,1)}, bf16[8,128,256]{2,1,0:T(8,128)(2,1)}, u32[]{:S(2)}, u32[]{:S(2)}) collective-permute-start(bf16[8,128,256]{2,1,0:T(8,128)(2,1)} %get-tuple-element.54), channel_id=1, source_target_pairs={{0,3},{1,0},{2,1},{3,2},{4,7},{5,4},{6,5},{7,6},{8,11},{9,8},{10,9... | collective-permute-start | bytes 1572872 | tf_op jit(solution)/shard_map/ppermute | solution.py:33
  178.8 4.2 %shard_map.116 = (bf16[16,128,256]{2,1,0:T(8,128)(2,1)}, bf16[16,128,256]{2,1,0:T(8,128)(2,1)}) custom-call(s32[2]{0:T(128)} %pad_add_fusion.2.pos_ref, s32[16,128]{1,0:T(8,128)} %bitcast.25, bf16[4,4,128,256]{3,2,1,0:T(8,128)(2,1)} %get-tuple-element.60.refs_0_.refs_4_, bf16[4,4,128,256]{3,2,1,0:T(8,128)(2,1)} %copy-done.14, ...), custom_call_target="tpu_custom_call" | custom-call | tf_op jit(solution)/shard_map/pallas_call | solution.py:194
  183.1 4.3 %shard_map.114 = (bf16[16,128,256]{2,1,0:T(8,128)(2,1)}, bf16[16,128,256]{2,1,0:T(8,128)(2,1)}) custom-call(s32[2]{0:T(128)} %pad_add_fusion.2.pos_ref, s32[16,128]{1,0:T(8,128)} %bitcast.26, bf16[4,4,128,256]{3,2,1,0:T(8,128)(2,1)} %get-tuple-element.40.refs_4_.refs_0_, bf16[4,4,128,256]{3,2,1,0:T(8,128)(2,1)} %copy-done.6, ...), custom_call_target="tpu_custom_call" | custom-call | tf_op jit(solution)/shard_map/pallas_call | solution.py:194
  188.4 3.2 collective-permute-start.30
  195.3 4.4 %collective-permute-done.10.refs_8_ = bf16[8,128,256]{2,1,0:T(8,128)(2,1)} collective-permute-done((bf16[8,128,256]{2,1,0:T(8,128)(2,1)}, bf16[8,128,256]{2,1,0:T(8,128)(2,1)}, u32[]{:S(2)}, u32[]{:S(2)}) %collective-permute-start.10) | collective-permute-done | bytes 524320 | tf_op jit(solution)/shard_map/ppermute | solution.py:33
  200.0 3.0 collective-permute-start.7
  203.8 5.3 %all-to-all-start.1 = ((bf16[8,64,512]{2,1,0:T(8,128)(2,1)}), bf16[8,64,512]{2,1,0:T(8,128)(2,1)S(1)}, u32[]{:S(2)}, u32[]{:S(2)}) async-start(bf16[8,64,512]{2,1,0:T(8,128)(2,1)} %broadcast_in_dim.40), calls=%async_computation.1 | async-start | bytes 1048576 | tf_op jit(solution)/shard_map/all_to_all | solution.py:334
  209.1 4.3 %shard_map.109 = (bf16[16,128,256]{2,1,0:T(8,128)(2,1)}, bf16[16,128,256]{2,1,0:T(8,128)(2,1)}) custom-call(s32[2]{0:T(128)} %pad_add_fusion.2.pos_ref, s32[16,128]{1,0:T(8,128)} %bitcast.28, bf16[4,4,128,256]{3,2,1,0:T(8,128)(2,1)} %get-tuple-element.45.refs_0_.refs_4_.refs_5_, bf16[4,4,128,256]{3,2,1,0:T(8,128)(2,1)} %copy-done.16, ...), custom_call_target="tpu_custom_call" | custom-call | tf_op jit(solution)/shard_map/pallas_call | solution.py:194
  213.4 9.9 %collective-permute-done.6.refs_8_ = bf16[8,128,256]{2,1,0:T(8,128)(2,1)S(1)} collective-permute-done((bf16[8,128,256]{2,1,0:T(8,128)(2,1)}, bf16[8,128,256]{2,1,0:T(8,128)(2,1)S(1)}, u32[]{:S(2)}, u32[]{:S(2)}) %collective-permute-start.6) | collective-permute-done | bytes 524320 | tf_op jit(solution)/shard_map/ppermute | solution.py:33
  226.8 4.3 %shard_map.107 = (bf16[16,128,256]{2,1,0:T(8,128)(2,1)}, bf16[16,128,256]{2,1,0:T(8,128)(2,1)}) custom-call(s32[2]{0:T(128)} %pad_add_fusion.2.pos_ref, s32[16,128]{1,0:T(8,128)} %bitcast.29, bf16[4,4,128,256]{3,2,1,0:T(8,128)(2,1)} %get-tuple-element.41.refs_0_.refs_4_, bf16[4,4,128,256]{3,2,1,0:T(8,128)(2,1)} %copy-done.2, ...), custom_call_target="tpu_custom_call" | custom-call | tf_op jit(solution)/shard_map/pallas_call | solution.py:194
  233.0 3.1 collective-permute-start.9
  241.6 8.1 %collective-permute-done.26.refs_9_ = bf16[16,128,256]{2,1,0:T(8,128)(2,1)} collective-permute-done((bf16[16,128,256]{2,1,0:T(8,128)(2,1)}, bf16[16,128,256]{2,1,0:T(8,128)(2,1)}, u32[]{:S(2)}, u32[]{:S(2)}) %collective-permute-start.26) | collective-permute-done | bytes 1048608 | tf_op jit(solution)/shard_map/ppermute | solution.py:33
  249.7 14.2 %shard_map.117 = (bf16[16,256,512]{2,1,0:T(8,128)(2,1)}, f32[512,512]{1,0:T(8,128)S(1)}, f32[512,512]{1,0:T(8,128)S(1)}) custom-call(s32[2]{0:T(128)S(1)} %copy-done.13, s32[16,128]{1,0:T(8,128)S(1)} %bitcast.30, f32[16]{0:T(128)S(1)} %add_divide_fusion.inv_ref, s32[64]{0:T(128)S(1)} %convert_reduce_fusion.1.near_ref, bf16[4,4,128,256]{3,2,1,0:T(8,128)(2,1)S(1)} %copy-done, ...), custom_call_target="tpu_custom_call" | custom-call | tf_op jit(solution)/shard_map/pallas_call | solution.py:316
  265.9 14.6 %shard_map.118 = (bf16[16,256,512]{2,1,0:T(8,128)(2,1)}, bf16[512,1024]{1,0:T(8,128)(2,1)S(1)}) custom-call(s32[2]{0:T(128)S(1)} %copy-done.13, s32[16,128]{1,0:T(8,128)S(1)} %bitcast.31, f32[16]{0:T(128)S(1)} %add_divide_fusion.inv_ref, s32[64]{0:T(128)S(1)} %convert_reduce_fusion.1.near_ref, ...), custom_call_target="tpu_custom_call", output_to_operand_aliasing={{0}: (22, {})} | custom-call | tf_op jit(solution)/shard_map/pallas_call | solution.py:316
  280.4 21.6 %all_to_all.23 = bf16[16,32,1024]{2,1,0:T(8,128)(2,1)S(1)} all-to-all(bf16[16,32,1024]{2,1,0:T(8,128)(2,1)S(1)} %bitcast.22), channel_id=1, replica_groups=mesh['row'=8,'col'=16] {'col'}, dimensions={0} | all-to-all | bytes 2097152 | tf_op jit(solution)/shard_map/all_to_all | solution.py:334
  304.9 3.2 collective-permute-start.33
  312.6 14.9 %all_to_all.24 = bf16[16,32,640]{2,1,0:T(8,128)(2,1)S(1)} all-to-all(bf16[16,32,640]{2,1,0:T(8,128)(2,1)S(1)} %broadcast_in_dim.41), channel_id=1, replica_groups=mesh['row'=8,'col'=16] {'col'}, dimensions={0} | all-to-all | bytes 1310720 | tf_op jit(solution)/shard_map/all_to_all | solution.py:334
  (150 shorter events, 68.3 us)
Async XLA Ops:
  8.9 54.8 %collective-permute-start.17 = (bf16[4,4,128,256]{3,2,1,0:T(8,128)(2,1)}, bf16[4,4,128,256]{3,2,1,0:T(8,128)(2,1)S(1)}, u32[]{:S(2)}, u32[]{:S(2)}) collective-permute-start(bf16[4,4,128,256]{3,2,1,0:T(8,128)(2,1)} %get-tuple-element.61), channel_id=1, source_target_pairs={{0,4},{1,5},{2,6},{3,7},{4,8},{5,9},{6,10},{7,11},{8,12},{9,13},{1... | collective-permute-start | bytes 3145736 | tf_op jit(solution)/shard_map/ppermute | solution.py:33
  17.0 61.0 %collective-permute-start.18 = (bf16[4,4,128,256]{3,2,1,0:T(8,128)(2,1)}, bf16[4,4,128,256]{3,2,1,0:T(8,128)(2,1)S(1)}, u32[]{:S(2)}, u32[]{:S(2)}) collective-permute-start(bf16[4,4,128,256]{3,2,1,0:T(8,128)(2,1)} %get-tuple-element.62), channel_id=1, source_target_pairs={{0,8},{1,9},{2,10},{3,11},{4,12},{5,13},{6,14},{7,15},{8,0},{9,1},... | collective-permute-start | bytes 3145736 | tf_op jit(solution)/shard_map/ppermute | solution.py:33
  26.3 52.4 %collective-permute-start.19 = (bf16[4,4,128,256]{3,2,1,0:T(8,128)(2,1)}, bf16[4,4,128,256]{3,2,1,0:T(8,128)(2,1)}, u32[]{:S(2)}, u32[]{:S(2)}) collective-permute-start(bf16[4,4,128,256]{3,2,1,0:T(8,128)(2,1)} %get-tuple-element.63), channel_id=1, source_target_pairs={{0,12},{1,13},{2,14},{3,15},{4,0},{5,1},{6,2},{7,3},{8,4},{9,5},{1... | collective-permute-start | bytes 3145736 | tf_op jit(solution)/shard_map/ppermute | solution.py:33
  27.7 52.2 %collective-permute-start.14 = (bf16[4,4,128,256]{3,2,1,0:T(8,128)(2,1)}, bf16[4,4,128,256]{3,2,1,0:T(8,128)(2,1)S(1)}, u32[]{:S(2)}, u32[]{:S(2)}) collective-permute-start(bf16[4,4,128,256]{3,2,1,0:T(8,128)(2,1)} %get-tuple-element.57), channel_id=1, source_target_pairs={{0,1},{1,2},{2,3},{3,0},{4,5},{5,6},{6,7},{7,4},{8,9},{9,10},{10,1... | collective-permute-start | bytes 3145736 | tf_op jit(solution)/shard_map/ppermute | solution.py:33
  29.3 23.9 %collective-permute-start.20 = (s32[1,128]{1,0:T(1,128)S(1)}, s32[1,128]{1,0:T(1,128)S(1)}, u32[]{:S(2)}, u32[]{:S(2)}) collective-permute-start(s32[1,128]{1,0:T(1,128)S(1)} %broadcast_in_dim_reshape_reshape.3), channel_id=1, source_target_pairs={{0,1},{1,2},{2,3},{3,0},{4,5},{5,6},{6,7},{7,4},{8,9},{9,10},{10,1... | collective-permute-start | bytes 1544 | tf_op jit(solution)/shard_map/ppermute | solution.py:33
  61.9 65.4 %collective-permute-start.15 = (bf16[4,4,128,256]{3,2,1,0:T(8,128)(2,1)}, bf16[4,4,128,256]{3,2,1,0:T(8,128)(2,1)}, u32[]{:S(2)}, u32[]{:S(2)}) collective-permute-start(bf16[4,4,128,256]{3,2,1,0:T(8,128)(2,1)} %get-tuple-element.58), channel_id=1, source_target_pairs={{0,2},{1,3},{2,0},{3,1},{4,6},{5,7},{6,4},{7,5},{8,10},{9,11},{10,... | collective-permute-start | bytes 3145736 | tf_op jit(solution)/shard_map/ppermute | solution.py:33
  63.7 64.3 %collective-permute-start.16 = (bf16[4,4,128,256]{3,2,1,0:T(8,128)(2,1)}, bf16[4,4,128,256]{3,2,1,0:T(8,128)(2,1)}, u32[]{:S(2)}, u32[]{:S(2)}) collective-permute-start(bf16[4,4,128,256]{3,2,1,0:T(8,128)(2,1)} %get-tuple-element.59), channel_id=1, source_target_pairs={{0,3},{1,0},{2,1},{3,2},{4,7},{5,4},{6,5},{7,6},{8,11},{9,8},{10,9... | collective-permute-start | bytes 3145736 | tf_op jit(solution)/shard_map/ppermute | solution.py:33
  78.0 52.5 %collective-permute-start.3 = (bf16[4,4,128,256]{3,2,1,0:T(8,128)(2,1)}, bf16[4,4,128,256]{3,2,1,0:T(8,128)(2,1)S(1)}, u32[]{:S(2)}, u32[]{:S(2)}) collective-permute-start(bf16[4,4,128,256]{3,2,1,0:T(8,128)(2,1)} %get-tuple-element.46), channel_id=1, source_target_pairs={{0,4},{1,5},{2,6},{3,7},{4,8},{5,9},{6,10},{7,11},{8,12},{9,13},{1... | collective-permute-start | bytes 3145736 | tf_op jit(solution)/shard_map/ppermute | solution.py:33
  78.7 52.8 %collective-permute-start.4 = (bf16[4,4,128,256]{3,2,1,0:T(8,128)(2,1)}, bf16[4,4,128,256]{3,2,1,0:T(8,128)(2,1)}, u32[]{:S(2)}, u32[]{:S(2)}) collective-permute-start(bf16[4,4,128,256]{3,2,1,0:T(8,128)(2,1)} %get-tuple-element.47), channel_id=1, source_target_pairs={{0,8},{1,9},{2,10},{3,11},{4,12},{5,13},{6,14},{7,15},{8,0},{9,1},... | collective-permute-start | bytes 3145736 | tf_op jit(solution)/shard_map/ppermute | solution.py:33
  79.8 53.1 %collective-permute-start.5 = (bf16[4,4,128,256]{3,2,1,0:T(8,128)(2,1)}, bf16[4,4,128,256]{3,2,1,0:T(8,128)(2,1)}, u32[]{:S(2)}, u32[]{:S(2)}) collective-permute-start(bf16[4,4,128,256]{3,2,1,0:T(8,128)(2,1)} %get-tuple-element.48), channel_id=1, source_target_pairs={{0,12},{1,13},{2,14},{3,15},{4,0},{5,1},{6,2},{7,3},{8,4},{9,5},{1... | collective-permute-start | bytes 3145736 | tf_op jit(solution)/shard_map/ppermute | solution.py:33
  82.2 41.7 %all-to-all-start = ((s32[16,1,128]{2,1,0:T(1,128)}), s32[16,1,128]{2,1,0:T(1,128)S(1)}, u32[]{:S(2)}, u32[]{:S(2)}) async-start(s32[16,1,128]{2,1,0:T(1,128)} %broadcast_in_dim.23), calls=%async_computation | async-start | bytes 16384 | tf_op jit(solution)/shard_map/all_to_all | solution.py:334
  127.2 16.3 %collective-permute-start.27 = (bf16[8,128,256]{2,1,0:T(8,128)(2,1)}, bf16[8,128,256]{2,1,0:T(8,128)(2,1)}, u32[]{:S(2)}, u32[]{:S(2)}) collective-permute-start(bf16[8,128,256]{2,1,0:T(8,128)(2,1)} %get-tuple-element.68), channel_id=1, source_target_pairs={{0,1},{1,2},{2,3},{3,0},{4,5},{5,6},{6,7},{7,4},{8,9},{9,10},{10,1... | collective-permute-start | bytes 1572872 | tf_op jit(solution)/shard_map/ppermute | solution.py:33
  128.0 37.4 %collective-permute-start.28 = (bf16[8,128,256]{2,1,0:T(8,128)(2,1)}, bf16[8,128,256]{2,1,0:T(8,128)(2,1)}, u32[]{:S(2)}, u32[]{:S(2)}) collective-permute-start(bf16[8,128,256]{2,1,0:T(8,128)(2,1)} %get-tuple-element.69), channel_id=1, source_target_pairs={{0,3},{1,0},{2,1},{3,2},{4,7},{5,4},{6,5},{7,6},{8,11},{9,8},{10,9... | collective-permute-start | bytes 1572872 | tf_op jit(solution)/shard_map/ppermute | solution.py:33
  131.5 56.9 %collective-permute-start = (bf16[4,4,128,256]{3,2,1,0:T(8,128)(2,1)}, bf16[4,4,128,256]{3,2,1,0:T(8,128)(2,1)S(1)}, u32[]{:S(2)}, u32[]{:S(2)}) collective-permute-start(bf16[4,4,128,256]{3,2,1,0:T(8,128)(2,1)} %get-tuple-element.42), channel_id=1, source_target_pairs={{0,1},{1,2},{2,3},{3,0},{4,5},{5,6},{6,7},{7,4},{8,9},{9,10},{10,1... | collective-permute-start | bytes 3145736 | tf_op jit(solution)/shard_map/ppermute | solution.py:33
  131.5 56.9 %collective-permute-start.1 = (bf16[4,4,128,256]{3,2,1,0:T(8,128)(2,1)}, bf16[4,4,128,256]{3,2,1,0:T(8,128)(2,1)S(1)}, u32[]{:S(2)}, u32[]{:S(2)}) collective-permute-start(bf16[4,4,128,256]{3,2,1,0:T(8,128)(2,1)} %get-tuple-element.43), channel_id=1, source_target_pairs={{0,2},{1,3},{2,0},{3,1},{4,6},{5,7},{6,4},{7,5},{8,10},{9,11},{10,... | collective-permute-start | bytes 3145736 | tf_op jit(solution)/shard_map/ppermute | solution.py:33
  132.9 58.7 %collective-permute-start.2 = (bf16[4,4,128,256]{3,2,1,0:T(8,128)(2,1)}, bf16[4,4,128,256]{3,2,1,0:T(8,128)(2,1)S(1)}, u32[]{:S(2)}, u32[]{:S(2)}) collective-permute-start(bf16[4,4,128,256]{3,2,1,0:T(8,128)(2,1)} %get-tuple-element.44), channel_id=1, source_target_pairs={{0,3},{1,0},{2,1},{3,2},{4,7},{5,4},{6,5},{7,6},{8,11},{9,8},{10,9... | collective-permute-start | bytes 3145736 | tf_op jit(solution)/shard_map/ppermute | solution.py:33
  143.5 27.2 %collective-permute-start.23 = (bf16[8,128,256]{2,1,0:T(8,128)(2,1)}, bf16[8,128,256]{2,1,0:T(8,128)(2,1)}, u32[]{:S(2)}, u32[]{:S(2)}) collective-permute-start(bf16[8,128,256]{2,1,0:T(8,128)(2,1)} %get-tuple-element.64), channel_id=1, source_target_pairs={{0,4},{1,5},{2,6},{3,7},{4,8},{5,9},{6,10},{7,11},{8,12},{9,13},{1... | collective-permute-start | bytes 1572872 | tf_op jit(solution)/shard_map/ppermute | solution.py:33
  165.4 9.6 %collective-permute-start.24 = (bf16[8,128,256]{2,1,0:T(8,128)(2,1)}, bf16[8,128,256]{2,1,0:T(8,128)(2,1)}, u32[]{:S(2)}, u32[]{:S(2)}) collective-permute-start(bf16[8,128,256]{2,1,0:T(8,128)(2,1)} %get-tuple-element.65), channel_id=1, source_target_pairs={{0,12},{1,13},{2,14},{3,15},{4,0},{5,1},{6,2},{7,3},{8,4},{9,5},{1... | collective-permute-start | bytes 1572872 | tf_op jit(solution)/shard_map/ppermute | solution.py:33
  170.8 29.0 %collective-permute-start.10 = (bf16[8,128,256]{2,1,0:T(8,128)(2,1)}, bf16[8,128,256]{2,1,0:T(8,128)(2,1)}, u32[]{:S(2)}, u32[]{:S(2)}) collective-permute-start(bf16[8,128,256]{2,1,0:T(8,128)(2,1)} %get-tuple-element.53), channel_id=1, source_target_pairs={{0,1},{1,2},{2,3},{3,0},{4,5},{5,6},{6,7},{7,4},{8,9},{9,10},{10,1... | collective-permute-start | bytes 1572872 | tf_op jit(solution)/shard_map/ppermute | solution.py:33
  175.0 25.0 %collective-permute-start.11 = (bf16[8,128,256]{2,1,0:T(8,128)(2,1)}, bf16[8,128,256]{2,1,0:T(8,128)(2,1)}, u32[]{:S(2)}, u32[]{:S(2)}) collective-permute-start(bf16[8,128,256]{2,1,0:T(8,128)(2,1)} %get-tuple-element.54), channel_id=1, source_target_pairs={{0,3},{1,0},{2,1},{3,2},{4,7},{5,4},{6,5},{7,6},{8,11},{9,8},{10,9... | collective-permute-start | bytes 1572872 | tf_op jit(solution)/shard_map/ppermute | solution.py:33
  188.4 42.7 %collective-permute-start.29 = (bf16[16,128,256]{2,1,0:T(8,128)(2,1)}, bf16[16,128,256]{2,1,0:T(8,128)(2,1)}, u32[]{:S(2)}, u32[]{:S(2)}) collective-permute-start(bf16[16,128,256]{2,1,0:T(8,128)(2,1)} %get-tuple-element.70), channel_id=1, source_target_pairs={{0,1},{1,2},{2,3},{3,0},{4,5},{5,6},{6,7},{7,4},{8,9},{9,10},{10,1... | collective-permute-start | bytes 3145736 | tf_op jit(solution)/shard_map/ppermute | solution.py:33
  188.4 44.5 %collective-permute-start.30 = (bf16[16,128,256]{2,1,0:T(8,128)(2,1)}, bf16[16,128,256]{2,1,0:T(8,128)(2,1)}, u32[]{:S(2)}, u32[]{:S(2)}) collective-permute-start(bf16[16,128,256]{2,1,0:T(8,128)(2,1)} %get-tuple-element.71), channel_id=1, source_target_pairs={{0,3},{1,0},{2,1},{3,2},{4,7},{5,4},{6,5},{7,6},{8,11},{9,8},{10,9... | collective-permute-start | bytes 3145736 | tf_op jit(solution)/shard_map/ppermute | solution.py:33
  191.6 41.4 %collective-permute-start.25 = (bf16[16,128,256]{2,1,0:T(8,128)(2,1)}, bf16[16,128,256]{2,1,0:T(8,128)(2,1)}, u32[]{:S(2)}, u32[]{:S(2)}) collective-permute-start(bf16[16,128,256]{2,1,0:T(8,128)(2,1)} %get-tuple-element.66), channel_id=1, source_target_pairs={{0,4},{1,5},{2,6},{3,7},{4,8},{5,9},{6,10},{7,11},{8,12},{9,13},{1... | collective-permute-start | bytes 3145736 | tf_op jit(solution)/shard_map/ppermute | solution.py:33
  199.7 23.6 %collective-permute-start.6 = (bf16[8,128,256]{2,1,0:T(8,128)(2,1)}, bf16[8,128,256]{2,1,0:T(8,128)(2,1)S(1)}, u32[]{:S(2)}, u32[]{:S(2)}) collective-permute-start(bf16[8,128,256]{2,1,0:T(8,128)(2,1)} %get-tuple-element.49), channel_id=1, source_target_pairs={{0,4},{1,5},{2,6},{3,7},{4,8},{5,9},{6,10},{7,11},{8,12},{9,13},{1... | collective-permute-start | bytes 1572872 | tf_op jit(solution)/shard_map/ppermute | solution.py:33
  200.0 25.1 %collective-permute-start.7 = (bf16[8,128,256]{2,1,0:T(8,128)(2,1)}, bf16[8,128,256]{2,1,0:T(8,128)(2,1)S(1)}, u32[]{:S(2)}, u32[]{:S(2)}) collective-permute-start(bf16[8,128,256]{2,1,0:T(8,128)(2,1)} %get-tuple-element.50), channel_id=1, source_target_pairs={{0,12},{1,13},{2,14},{3,15},{4,0},{5,1},{6,2},{7,3},{8,4},{9,5},{1... | collective-permute-start | bytes 1572872 | tf_op jit(solution)/shard_map/ppermute | solution.py:33
  203.8 35.2 %all-to-all-start.1 = ((bf16[8,64,512]{2,1,0:T(8,128)(2,1)}), bf16[8,64,512]{2,1,0:T(8,128)(2,1)S(1)}, u32[]{:S(2)}, u32[]{:S(2)}) async-start(bf16[8,64,512]{2,1,0:T(8,128)(2,1)} %broadcast_in_dim.40), calls=%async_computation.1 | async-start | bytes 1048576 | tf_op jit(solution)/shard_map/all_to_all | solution.py:334
  223.3 26.3 %collective-permute-start.26 = (bf16[16,128,256]{2,1,0:T(8,128)(2,1)}, bf16[16,128,256]{2,1,0:T(8,128)(2,1)}, u32[]{:S(2)}, u32[]{:S(2)}) collective-permute-start(bf16[16,128,256]{2,1,0:T(8,128)(2,1)} %get-tuple-element.67), channel_id=1, source_target_pairs={{0,12},{1,13},{2,14},{3,15},{4,0},{5,1},{6,2},{7,3},{8,4},{9,5},{1... | collective-permute-start | bytes 3145736 | tf_op jit(solution)/shard_map/ppermute | solution.py:33
  225.1 40.8 %collective-permute-start.12 = (bf16[16,128,256]{2,1,0:T(8,128)(2,1)}, bf16[16,128,256]{2,1,0:T(8,128)(2,1)}, u32[]{:S(2)}, u32[]{:S(2)}) collective-permute-start(bf16[16,128,256]{2,1,0:T(8,128)(2,1)} %get-tuple-element.55), channel_id=1, source_target_pairs={{0,1},{1,2},{2,3},{3,0},{4,5},{5,6},{6,7},{7,4},{8,9},{9,10},{10,1... | collective-permute-start | bytes 3145736 | tf_op jit(solution)/shard_map/ppermute | solution.py:33
  231.1 34.7 %collective-permute-start.13 = (bf16[16,128,256]{2,1,0:T(8,128)(2,1)}, bf16[16,128,256]{2,1,0:T(8,128)(2,1)}, u32[]{:S(2)}, u32[]{:S(2)}) collective-permute-start(bf16[16,128,256]{2,1,0:T(8,128)(2,1)} %get-tuple-element.56), channel_id=1, source_target_pairs={{0,3},{1,0},{2,1},{3,2},{4,7},{5,4},{6,5},{7,6},{8,11},{9,8},{10,9... | collective-permute-start | bytes 3145736 | tf_op jit(solution)/shard_map/ppermute | solution.py:33
  232.9 33.0 %collective-permute-start.8 = (bf16[16,128,256]{2,1,0:T(8,128)(2,1)}, bf16[16,128,256]{2,1,0:T(8,128)(2,1)}, u32[]{:S(2)}, u32[]{:S(2)}) collective-permute-start(bf16[16,128,256]{2,1,0:T(8,128)(2,1)} %get-tuple-element.51), channel_id=1, source_target_pairs={{0,4},{1,5},{2,6},{3,7},{4,8},{5,9},{6,10},{7,11},{8,12},{9,13},{1... | collective-permute-start | bytes 3145736 | tf_op jit(solution)/shard_map/ppermute | solution.py:33
  233.0 32.8 %collective-permute-start.9 = (bf16[16,128,256]{2,1,0:T(8,128)(2,1)}, bf16[16,128,256]{2,1,0:T(8,128)(2,1)}, u32[]{:S(2)}, u32[]{:S(2)}) collective-permute-start(bf16[16,128,256]{2,1,0:T(8,128)(2,1)} %get-tuple-element.52), channel_id=1, source_target_pairs={{0,12},{1,13},{2,14},{3,15},{4,0},{5,1},{6,2},{7,3},{8,4},{9,5},{1... | collective-permute-start | bytes 3145736 | tf_op jit(solution)/shard_map/ppermute | solution.py:33
  304.9 6.7 %collective-permute-start.33 = (bf16[32,1024]{1,0:T(8,128)(2,1)S(1)}, bf16[32,1024]{1,0:T(8,128)(2,1)S(1)}, u32[]{:S(2)}, u32[]{:S(2)}) collective-permute-start(bf16[32,1024]{1,0:T(8,128)(2,1)S(1)} %fusion), channel_id=1, source_target_pairs={{0,64},{16,80},{32,96},{48,112},{64,0},{80,16},{96,32},{112,48},{1... | collective-permute-start | bytes 196616 | tf_op jit(solution)/shard_map/ppermute | solution.py:41
  (29 other events, 265.9 us)

commit v4 on v2

--- a/solution.py
+++ b/solution.py
@@ -78,6 +78,7 @@
 
 
 def add_slots(acc_ref, table_ref, y, x, half, ahead, parts, columns):
+    local = table_ref.shape[0] == RING
     n_blk = acc_ref.shape[0]
     cap = parts[0].shape[1]
     for came, ref in enumerate(parts):
@@ -87,6 +88,7 @@
         else:
             s = wrap(y - came) * RING + x
             p = y * RING + wrap(x + ahead)
+        s = came if local else s
 
         def add(q, carry):
             dst = table_ref[s, p * 2 * cap + q]
@@ -100,7 +102,7 @@
 
             return carry
 
-        lax.fori_loop(0, cap, add, 0)
+        lax.fori_loop(0, cap, add, 0, unroll=columns == slice(None))
 
 
 def far_kernel(half, pos_ref, table_ref, *refs):
@@ -165,6 +167,10 @@
     )(pos, table, *parts, *parts, low, high)
 
 
+def sigmoid(v):
+    return 0.5 * jnp.tanh(0.5 * v) + 0.5
+
+
 def head_kernel(first, last, row, blk, labels_total, pos_count,
                 pos_ref, table_ref, inv_ref, near_ref, *refs):
     mine = (refs[:RING], refs[RING:2 * RING])
@@ -176,9 +182,9 @@
         gd_in, gw_in, _ = rest[:3]
         rest = rest[3:]
     if last:
-        hid_ref, both_ref, acc_ref, agg_ref, ds_ref, gd_ref, gw_ref = rest
+        hid_ref, both_ref, acc_ref, agg_ref, ds_ref, prob_ref, gd_ref, gw_ref = rest
     else:
-        hid_ref, gd_ref, gw_ref, acc_ref, agg_ref, ds_ref = rest
+        hid_ref, gd_ref, gw_ref, acc_ref, agg_ref, ds_ref, prob_ref = rest
     step = pl.program_id(0)
 
     @pl.when(step == 0)
@@ -205,26 +211,32 @@
         agg_ref[b * rows:(b + 1) * rows, :] = (acc_ref[b] * inv_ref[b]).astype(BF)
     agg = agg_ref[...]
     pre = jnp.dot(agg, w_ref[...], preferred_element_type=F32)
-    sig = 1.0 / (1.0 + jnp.exp(-pre))
+    sig = sigmoid(pre)
     hid = (pre * sig).astype(BF)
     for b in range(n_blk):
         hid_ref[b] = hid[b * rows:(b + 1) * rows, :]
     scores = lax.dot_general(hid, docs_ref[...], (((1,), (1,)), ((), ())),
                              preferred_element_type=F32)
-    prob = 1.0 / (1.0 + jnp.exp(-scores))
-    for b in range(n_blk):
-        one = prob[b * rows:(b + 1) * rows, :]
-        ds_ref[b * rows:(b + 1) * rows, :] = (one * (1.0 / labels_total)).astype(BF)
-
-        @pl.when(near_ref[(b * blk + row) // rows + step] > 0)
+    prob = sigmoid(scores)
+    prob_ref[...] = prob
+    ds_ref[...] = (prob * (1.0 / labels_total)).astype(BF)
+
+    def mark(b, carry):
+        @pl.when(near_ref[b * (blk // rows) + row // rows + step] > 0)
         def _():
+            here = pl.ds(pl.multiple_of(b * rows, rows), rows)
+            one = prob_ref[here, :]
             ids = b * blk + row + step * rows + lax.broadcasted_iota(jnp.int32, one.shape, 0)
             hit = labels_ref[0:1, :] == ids
             for j in range(1, labels_ref.shape[0]):
                 hit = hit | (labels_ref[j:j + 1, :] == ids)
-            ds_ref[b * rows:(b + 1) * rows, :] = jnp.where(
+            ds_ref[here, :] = jnp.where(
                 hit, (one - 1.0) * (1.0 / pos_count), one * (1.0 / labels_total)
             ).astype(BF)
+
+        return carry
+
+    lax.fori_loop(0, n_blk, mark, 0)
     ds = ds_ref[...]
     gd_ref[...] += lax.dot_general(ds, hid, (((0,), (0,)), ((), ())),
                                    preferred_element_type=F32)
@@ -275,7 +287,8 @@
         + [jax.ShapeDtypeStruct(a, t) for a, t in grads],
         scratch_shapes=[pltpu.VMEM((n_blk, step_rows, width), F32),
                         pltpu.VMEM((n_blk * step_rows, width), BF),
-                        pltpu.VMEM((n_blk * step_rows, n_doc), BF)]
+                        pltpu.VMEM((n_blk * step_rows, n_doc), BF),
+                        pltpu.VMEM((n_blk * step_rows, n_doc), F32)]
         + ([pltpu.VMEM((n_doc, width), F32), pltpu.VMEM((width, width), F32)] if last else []),
         input_output_aliases=aliases,
         compiler_params=pltpu.CompilerParams(vmem_limit_bytes=48 << 20),
@@ -308,7 +321,9 @@
     orders = (wrap(y + inner) * RING + wrap(x + outer), wrap(y + outer) * RING + wrap(x + inner))
     axes = (("x", "y"), ("y", "x"))
 
-    table = jnp.concatenate([msg_dst, msg_count], axis=1).reshape(-1)
+    own_table = jnp.concatenate([msg_dst, msg_count], axis=1).reshape(1, -1)
+    near_table = jnp.concatenate([own_table] + [shift(own_table, "x", j) for j in range(1, RING)])
+    table = own_table.reshape(-1)
     table = spread(table, "col", n_col).reshape(n_col, n_col * 2 * cap)
     share = docs.shape[0] // n_col
     regroup = lambda a: a.reshape((n_row, n_col, share) + a.shape[1:]).swapaxes(0, 1).reshape(a.shape)
@@ -335,7 +350,8 @@
         for half in range(2):
             second = axes[half][1]
             after = [came[k + 1][h][0] for h in range(2)] if k + 1 < n_chunk else []
-            low, high = far_sums(half, pos, table, came[k][half],
+            rows_of = near_table if (k, half) == (0, 0) else table
+            low, high = far_sums(half, pos, rows_of, came[k][half],
                               blk_dev, after)
             lows[k][half] = low
             ends[k][half] = (shift(low, second, 1),

time: 342 us -> 373 us (1.091)
  waiting for transfers between devices: 135 us -> 173 us
  starting transfers between devices: 70.2 us -> 64.7 us
    all_to_all x2, waiting for transfers between devices: 26.9 us -> 56.9 us  [swap(): return lax.all_to_all(x, axis, split_axis=0, concat_axis=0, tiled=True)]
    ppermute x28 -> x31, waiting for transfers between devices: 103 us -> 112 us  [shift(): return lax.ppermute(v, 'col', shift_pairs(axis, by))]
    all_to_all x2, starting transfers between devices: 17 us -> 9.8 us  [swap(): return lax.all_to_all(x, axis, split_axis=0, concat_axis=0, tiled=True)]
    ppermute x28 -> x31, starting transfers between devices: 46.5 us -> 48.4 us  [shift(): return lax.ppermute(v, 'col', shift_pairs(axis, by))]
  transfers between devices with their start and end apart: 34 -> 37, of which waited for: 14 -> 14; matrix products, arithmetic and copies ran while one was open for 2% -> 2% of each run, Pallas kernels for 18% -> 17%
where the time goes in v4:
time: 373 us; the launch traced here: 372 us
  waiting for transfers between devices  173 us (46%)
  Pallas kernels  82.9 us (22%)
  starting transfers between devices  64.7 us (17%)
  blocking collectives  34.4 us (9%)
  local copies, waits for them, and re-layouts  11 us (3%)
  other arithmetic  4.08 us (1%)
    ppermute x31, waiting for transfers between devices, shift(): return lax.ppermute(v, 'col', shift_pairs(axis, by))  112 us
    all_to_all x2, waiting for transfers between devices, swap(): return lax.all_to_all(x, axis, split_axis=0, concat_axis=0, tiled=True)  56.9 us
    ppermute x31, starting transfers between devices, shift(): return lax.ppermute(v, 'col', shift_pairs(axis, by))  48.4 us
    all_to_all x2, blocking collectives, swap(): return lax.all_to_all(x, axis, split_axis=0, concat_axis=0, tiled=True)  34.4 us
    pallas_call x2, Pallas kernels, head(): pl.pallas_call(functools.partial(head_kernel, first, last, row, blk, labe...  28.8 us
    pallas_call x4, Pallas kernels, messages_of(): pl.pallas_call(message_kernel, grid_spec=pltpu.PrefetchScalarGridSpec(num...  27.5 us
    pallas_call x4, Pallas kernels, near_sums(): pl.pallas_call(functools.partial(near_kernel, half), grid=(rows // step_r...  16.2 us
    pallas_call x4, Pallas kernels, far_sums(): pl.pallas_call(functools.partial(far_kernel, half), grid=(rows // step_ro...  10.4 us
  transfers between devices with their start and end apart: 37, of which 14 were waited for; matrix products, arithmetic and copies ran while one was open for 2% of the time, Pallas kernels for 17%

profile of v4, /device:TPU:0, one launch (start us, length us, event | category | flops | bytes accessed | tf_op | source)
XLA Modules:
  0.0 371.7 jit_solution(2382748875429501986)
XLA Ops:
  2.5 6.8 %shard_map.110 = (bf16[4,4,128,256]{3,2,1,0:T(8,128)(2,1)}, bf16[4,4,128,256]{3,2,1,0:T(8,128)(2,1)}, bf16[4,4,128,256]{3,2,1,0:T(8,128)(2,1)}, bf16[4,4,128,256]{3,2,1,0:T(8,128)(2,1)}) custom-call(s32[16]{0:T(128)} %fusion.13.order_ref, s32[16,4]{1,0:T(8,128)} %copy.57.src_ref, bf16[16,256,512]{2,1,0:T(8,128)(2,1)} %bitcast.35, ...), custom_call_target="tpu_custom_call" | custom-call | tf_op jit(solution)/shard_map/pallas_call | solution.py:61
  11.0 2.9 collective-permute-start.18
  15.8 7.0 %shard_map.109 = (bf16[4,4,128,256]{3,2,1,0:T(8,128)(2,1)}, bf16[4,4,128,256]{3,2,1,0:T(8,128)(2,1)}, bf16[4,4,128,256]{3,2,1,0:T(8,128)(2,1)}, bf16[4,4,128,256]{3,2,1,0:T(8,128)(2,1)}) custom-call(s32[16]{0:T(128)} %fusion.9.order_ref, s32[16,4]{1,0:T(8,128)} %copy.57.src_ref, bf16[16,256,512]{2,1,0:T(8,128)(2,1)} %bitcast.36, ...), custom_call_target="tpu_custom_call" | custom-call | tf_op jit(solution)/shard_map/pallas_call | solution.py:61
  26.0 22.4 %collective-permute-done.20 = s32[1,128]{1,0:T(1,128)S(1)} collective-permute-done((s32[1,128]{1,0:T(1,128)S(1)}, s32[1,128]{1,0:T(1,128)S(1)}, u32[]{:S(2)}, u32[]{:S(2)}) %collective-permute-start.20) | collective-permute-done | bytes 544 | tf_op jit(solution)/shard_map/ppermute | solution.py:33
  50.1 3.3 collective-permute-done.21
  60.0 6.8 %shard_map.103 = (bf16[4,4,128,256]{3,2,1,0:T(8,128)(2,1)}, bf16[4,4,128,256]{3,2,1,0:T(8,128)(2,1)}, bf16[4,4,128,256]{3,2,1,0:T(8,128)(2,1)}, bf16[4,4,128,256]{3,2,1,0:T(8,128)(2,1)}) custom-call(s32[16]{0:T(128)} %fusion.9.order_ref, s32[16,4]{1,0:T(8,128)} %copy.57.src_ref, bf16[16,256,512]{2,1,0:T(8,128)(2,1)} %bitcast.37, ...), custom_call_target="tpu_custom_call" | custom-call | tf_op jit(solution)/shard_map/pallas_call | solution.py:61
  67.8 2.7 collective-permute-start.1
  73.0 5.3 %all-to-all-start.1 = ((bf16[8,64,512]{2,1,0:T(8,128)(2,1)}), bf16[8,64,512]{2,1,0:T(8,128)(2,1)}, u32[]{:S(2)}, u32[]{:S(2)}) async-start(bf16[8,64,512]{2,1,0:T(8,128)(2,1)} %broadcast_in_dim.40), calls=%async_computation.1 | async-start | bytes 1048576 | tf_op jit(solution)/shard_map/all_to_all | solution.py:299
  78.4 10.3 %all-to-all-done.1 = bf16[8,64,512]{2,1,0:T(8,128)(2,1)} async-done(((bf16[8,64,512]{2,1,0:T(8,128)(2,1)}), bf16[8,64,512]{2,1,0:T(8,128)(2,1)}, u32[]{:S(2)}, u32[]{:S(2)}) %all-to-all-start.1) | async-done | bytes 524320 | tf_op jit(solution)/shard_map/all_to_all | solution.py:299
  89.3 4.5 %all-to-all-start = ((s32[16,1,128]{2,1,0:T(1,128)}), s32[16,1,128]{2,1,0:T(1,128)S(1)}, u32[]{:S(2)}, u32[]{:S(2)}) async-start(s32[16,1,128]{2,1,0:T(1,128)} %broadcast_in_dim.23), calls=%async_computation | async-start | bytes 16384 | tf_op jit(solution)/shard_map/all_to_all | solution.py:299
  94.5 6.9 %shard_map.104 = (bf16[4,4,128,256]{3,2,1,0:T(8,128)(2,1)}, bf16[4,4,128,256]{3,2,1,0:T(8,128)(2,1)}, bf16[4,4,128,256]{3,2,1,0:T(8,128)(2,1)}, bf16[4,4,128,256]{3,2,1,0:T(8,128)(2,1)}) custom-call(s32[16]{0:T(128)} %fusion.13.order_ref, s32[16,4]{1,0:T(8,128)} %copy.57.src_ref, bf16[16,256,512]{2,1,0:T(8,128)(2,1)} %bitcast.38, ...), custom_call_target="tpu_custom_call" | custom-call | tf_op jit(solution)/shard_map/pallas_call | solution.py:61
  101.4 46.5 %all-to-all-done = s32[16,1,128]{2,1,0:T(1,128)S(1)} async-done(((s32[16,1,128]{2,1,0:T(1,128)}), s32[16,1,128]{2,1,0:T(1,128)S(1)}, u32[]{:S(2)}, u32[]{:S(2)}) %all-to-all-start) | async-done | bytes 8224 | tf_op jit(solution)/shard_map/all_to_all | solution.py:299
  151.6 2.8 collective-permute-start.28
  155.7 2.7 collective-permute-start.4
  163.1 2.8 collective-permute-done.27.refs_8_
  171.7 41.9 %collective-permute-done.23.refs_8_ = bf16[8,128,256]{2,1,0:T(8,128)(2,1)} collective-permute-done((bf16[8,128,256]{2,1,0:T(8,128)(2,1)}, bf16[8,128,256]{2,1,0:T(8,128)(2,1)}, u32[]{:S(2)}, u32[]{:S(2)}) %collective-permute-start.23) | collective-permute-done | bytes 524320 | tf_op jit(solution)/shard_map/ppermute | solution.py:33
  214.2 2.6 collective-permute-start.7
  216.9 4.0 %shard_map.114 = (bf16[16,128,256]{2,1,0:T(8,128)(2,1)}, bf16[16,128,256]{2,1,0:T(8,128)(2,1)}) custom-call(s32[2]{0:T(128)} %pad_add_fusion.2.pos_ref, s32[16,128]{1,0:T(8,128)} %bitcast.26, bf16[4,4,128,256]{3,2,1,0:T(8,128)(2,1)} %get-tuple-element.60.refs_0_.refs_4_, bf16[4,4,128,256]{3,2,1,0:T(8,128)(2,1)} %copy-done.14, ...), custom_call_target="tpu_custom_call" | custom-call | tf_op jit(solution)/shard_map/pallas_call | solution.py:159
  220.9 4.1 %shard_map.112 = (bf16[16,128,256]{2,1,0:T(8,128)(2,1)}, bf16[16,128,256]{2,1,0:T(8,128)(2,1)}) custom-call(s32[2]{0:T(128)} %pad_add_fusion.2.pos_ref, s32[16,128]{1,0:T(8,128)} %bitcast.27, bf16[4,4,128,256]{3,2,1,0:T(8,128)(2,1)} %get-tuple-element.56.refs_0_.refs_4_, bf16[4,4,128,256]{3,2,1,0:T(8,128)(2,1)} %copy-done.6, ...), custom_call_target="tpu_custom_call" | custom-call | tf_op jit(solution)/shard_map/pallas_call | solution.py:159
  225.1 3.2 collective-permute-start.30
  231.0 3.2 collective-permute-start.11
  234.2 4.1 %shard_map.106 = (bf16[16,128,256]{2,1,0:T(8,128)(2,1)}, bf16[16,128,256]{2,1,0:T(8,128)(2,1)}) custom-call(s32[2]{0:T(128)} %pad_add_fusion.2.pos_ref, s32[16,128]{1,0:T(8,128)} %bitcast.29, bf16[4,4,128,256]{3,2,1,0:T(8,128)(2,1)} %get-tuple-element.40.refs_0_.refs_4_, bf16[4,4,128,256]{3,2,1,0:T(8,128)(2,1)} %copy-done.1, ...), custom_call_target="tpu_custom_call" | custom-call | tf_op jit(solution)/shard_map/pallas_call | solution.py:159
  238.3 24.4 %collective-permute-done.10.refs_8_ = bf16[8,128,256]{2,1,0:T(8,128)(2,1)S(1)} collective-permute-done((bf16[8,128,256]{2,1,0:T(8,128)(2,1)}, bf16[8,128,256]{2,1,0:T(8,128)(2,1)S(1)}, u32[]{:S(2)}, u32[]{:S(2)}) %collective-permute-start.10) | collective-permute-done | bytes 524320 | tf_op jit(solution)/shard_map/ppermute | solution.py:33
  264.8 4.0 %shard_map.108 = (bf16[16,128,256]{2,1,0:T(8,128)(2,1)}, bf16[16,128,256]{2,1,0:T(8,128)(2,1)}) custom-call(s32[2]{0:T(128)} %pad_add_fusion.2.pos_ref, s32[16,128]{1,0:T(8,128)} %bitcast.30, bf16[4,4,128,256]{3,2,1,0:T(8,128)(2,1)} %get-tuple-element.44.refs_0_.refs_4_.refs_5_, bf16[4,4,128,256]{3,2,1,0:T(8,128)(2,1)} %copy-done.16, ...), custom_call_target="tpu_custom_call" | custom-call | tf_op jit(solution)/shard_map/pallas_call | solution.py:159
  270.2 3.2 collective-permute-start.13
  278.3 10.7 %collective-permute-done.26.refs_9_ = bf16[16,128,256]{2,1,0:T(8,128)(2,1)} collective-permute-done((bf16[16,128,256]{2,1,0:T(8,128)(2,1)}, bf16[16,128,256]{2,1,0:T(8,128)(2,1)}, u32[]{:S(2)}, u32[]{:S(2)}) %collective-permute-start.26) | collective-permute-done | bytes 1048608 | tf_op jit(solution)/shard_map/ppermute | solution.py:33
  289.0 14.2 %shard_map.115 = (bf16[16,256,512]{2,1,0:T(8,128)(2,1)}, f32[512,512]{1,0:T(8,128)S(1)}, f32[512,512]{1,0:T(8,128)S(1)}) custom-call(s32[2]{0:T(128)S(1)} %copy-done.13, s32[16,128]{1,0:T(8,128)S(1)} %bitcast.31, f32[16]{0:T(128)S(1)} %add_divide_fusion.inv_ref, s32[64]{0:T(128)S(1)} %convert_reduce_fusion.1.near_ref, ...), custom_call_target="tpu_custom_call" | custom-call | tf_op jit(solution)/shard_map/pallas_call | solution.py:281
  305.3 4.2 %collective-permute-done.9.refs_9_ = bf16[16,128,256]{2,1,0:T(8,128)(2,1)} collective-permute-done((bf16[16,128,256]{2,1,0:T(8,128)(2,1)}, bf16[16,128,256]{2,1,0:T(8,128)(2,1)}, u32[]{:S(2)}, u32[]{:S(2)}) %collective-permute-start.9) | collective-permute-done | bytes 1048608 | tf_op jit(solution)/shard_map/ppermute | solution.py:33
  309.6 14.6 %shard_map.116 = (bf16[16,256,512]{2,1,0:T(8,128)(2,1)}, bf16[512,1024]{1,0:T(8,128)(2,1)S(1)}) custom-call(s32[2]{0:T(128)S(1)} %copy-done.13, s32[16,128]{1,0:T(8,128)S(1)} %bitcast.32, f32[16]{0:T(128)S(1)} %add_divide_fusion.inv_ref, s32[64]{0:T(128)S(1)} %convert_reduce_fusion.1.near_ref, ...), custom_call_target="tpu_custom_call", output_to_operand_aliasing={{0}: (22, {})} | custom-call | tf_op jit(solution)/shard_map/pallas_call | solution.py:281
  324.2 19.7 %all_to_all.23 = bf16[16,32,1024]{2,1,0:T(8,128)(2,1)S(1)} all-to-all(bf16[16,32,1024]{2,1,0:T(8,128)(2,1)S(1)} %bitcast.23), channel_id=1, replica_groups=mesh['row'=8,'col'=16] {'col'}, dimensions={0} | all-to-all | bytes 2097152 | tf_op jit(solution)/shard_map/all_to_all | solution.py:299
  346.3 4.4 %collective-permute-start.33 = (bf16[32,1024]{1,0:T(8,128)(2,1)S(1)}, bf16[32,1024]{1,0:T(8,128)(2,1)S(1)}, u32[]{:S(2)}, u32[]{:S(2)}) collective-permute-start(bf16[32,1024]{1,0:T(8,128)(2,1)S(1)} %fusion), channel_id=1, source_target_pairs={{0,64},{16,80},{32,96},{48,112},{64,0},{80,16},{96,32},{112,48},{1... | collective-permute-start | bytes 196616 | tf_op jit(solution)/shard_map/ppermute | solution.py:41
  355.1 14.8 %all_to_all.24 = bf16[16,32,640]{2,1,0:T(8,128)(2,1)S(1)} all-to-all(bf16[16,32,640]{2,1,0:T(8,128)(2,1)S(1)} %broadcast_in_dim.41), channel_id=1, replica_groups=mesh['row'=8,'col'=16] {'col'}, dimensions={0} | all-to-all | bytes 1310720 | tf_op jit(solution)/shard_map/all_to_all | solution.py:299
  (151 shorter events, 59.8 us)
Async XLA Ops:
  9.3 49.5 %collective-permute-start.17 = (bf16[4,4,128,256]{3,2,1,0:T(8,128)(2,1)}, bf16[4,4,128,256]{3,2,1,0:T(8,128)(2,1)S(1)}, u32[]{:S(2)}, u32[]{:S(2)}) collective-permute-start(bf16[4,4,128,256]{3,2,1,0:T(8,128)(2,1)} %get-tuple-element.61), channel_id=1, source_target_pairs={{0,4},{1,5},{2,6},{3,7},{4,8},{5,9},{6,10},{7,11},{8,12},{9,13},{1... | collective-permute-start | bytes 3145736 | tf_op jit(solution)/shard_map/ppermute | solution.py:33
  11.0 55.7 %collective-permute-start.18 = (bf16[4,4,128,256]{3,2,1,0:T(8,128)(2,1)}, bf16[4,4,128,256]{3,2,1,0:T(8,128)(2,1)S(1)}, u32[]{:S(2)}, u32[]{:S(2)}) collective-permute-start(bf16[4,4,128,256]{3,2,1,0:T(8,128)(2,1)} %get-tuple-element.62), channel_id=1, source_target_pairs={{0,8},{1,9},{2,10},{3,11},{4,12},{5,13},{6,14},{7,15},{8,0},{9,1},... | collective-permute-start | bytes 3145736 | tf_op jit(solution)/shard_map/ppermute | solution.py:33
  13.9 53.8 %collective-permute-start.19 = (bf16[4,4,128,256]{3,2,1,0:T(8,128)(2,1)}, bf16[4,4,128,256]{3,2,1,0:T(8,128)(2,1)}, u32[]{:S(2)}, u32[]{:S(2)}) collective-permute-start(bf16[4,4,128,256]{3,2,1,0:T(8,128)(2,1)} %get-tuple-element.63), channel_id=1, source_target_pairs={{0,12},{1,13},{2,14},{3,15},{4,0},{5,1},{6,2},{7,3},{8,4},{9,5},{1... | collective-permute-start | bytes 3145736 | tf_op jit(solution)/shard_map/ppermute | solution.py:33
  22.8 47.7 %collective-permute-start.14 = (bf16[4,4,128,256]{3,2,1,0:T(8,128)(2,1)}, bf16[4,4,128,256]{3,2,1,0:T(8,128)(2,1)S(1)}, u32[]{:S(2)}, u32[]{:S(2)}) collective-permute-start(bf16[4,4,128,256]{3,2,1,0:T(8,128)(2,1)} %get-tuple-element.57), channel_id=1, source_target_pairs={{0,1},{1,2},{2,3},{3,0},{4,5},{5,6},{6,7},{7,4},{8,9},{9,10},{10,1... | collective-permute-start | bytes 3145736 | tf_op jit(solution)/shard_map/ppermute | solution.py:33
  24.4 23.9 %collective-permute-start.20 = (s32[1,128]{1,0:T(1,128)S(1)}, s32[1,128]{1,0:T(1,128)S(1)}, u32[]{:S(2)}, u32[]{:S(2)}) collective-permute-start(s32[1,128]{1,0:T(1,128)S(1)} %broadcast_in_dim_reshape_reshape.3), channel_id=1, source_target_pairs={{0,1},{1,2},{2,3},{3,0},{4,5},{5,6},{6,7},{7,4},{8,9},{9,10},{10,1... | collective-permute-start | bytes 1544 | tf_op jit(solution)/shard_map/ppermute | solution.py:33
  57.0 94.1 %collective-permute-start.15 = (bf16[4,4,128,256]{3,2,1,0:T(8,128)(2,1)}, bf16[4,4,128,256]{3,2,1,0:T(8,128)(2,1)}, u32[]{:S(2)}, u32[]{:S(2)}) collective-permute-start(bf16[4,4,128,256]{3,2,1,0:T(8,128)(2,1)} %get-tuple-element.58), channel_id=1, source_target_pairs={{0,2},{1,3},{2,0},{3,1},{4,6},{5,7},{6,4},{7,5},{8,10},{9,11},{10,... | collective-permute-start | bytes 3145736 | tf_op jit(solution)/shard_map/ppermute | solution.py:33
  58.8 92.8 %collective-permute-start.16 = (bf16[4,4,128,256]{3,2,1,0:T(8,128)(2,1)}, bf16[4,4,128,256]{3,2,1,0:T(8,128)(2,1)}, u32[]{:S(2)}, u32[]{:S(2)}) collective-permute-start(bf16[4,4,128,256]{3,2,1,0:T(8,128)(2,1)} %get-tuple-element.59), channel_id=1, source_target_pairs={{0,3},{1,0},{2,1},{3,2},{4,7},{5,4},{6,5},{7,6},{8,11},{9,8},{10,9... | collective-permute-start | bytes 3145736 | tf_op jit(solution)/shard_map/ppermute | solution.py:33
  66.8 87.6 %collective-permute-start = (bf16[4,4,128,256]{3,2,1,0:T(8,128)(2,1)}, bf16[4,4,128,256]{3,2,1,0:T(8,128)(2,1)S(1)}, u32[]{:S(2)}, u32[]{:S(2)}) collective-permute-start(bf16[4,4,128,256]{3,2,1,0:T(8,128)(2,1)} %get-tuple-element.41), channel_id=1, source_target_pairs={{0,1},{1,2},{2,3},{3,0},{4,5},{5,6},{6,7},{7,4},{8,9},{9,10},{10,1... | collective-permute-start | bytes 3145736 | tf_op jit(solution)/shard_map/ppermute | solution.py:33
  67.8 87.9 %collective-permute-start.1 = (bf16[4,4,128,256]{3,2,1,0:T(8,128)(2,1)}, bf16[4,4,128,256]{3,2,1,0:T(8,128)(2,1)S(1)}, u32[]{:S(2)}, u32[]{:S(2)}) collective-permute-start(bf16[4,4,128,256]{3,2,1,0:T(8,128)(2,1)} %get-tuple-element.42), channel_id=1, source_target_pairs={{0,2},{1,3},{2,0},{3,1},{4,6},{5,7},{6,4},{7,5},{8,10},{9,11},{10,... | collective-permute-start | bytes 3145736 | tf_op jit(solution)/shard_map/ppermute | solution.py:33
  70.5 87.9 %collective-permute-start.2 = (bf16[4,4,128,256]{3,2,1,0:T(8,128)(2,1)}, bf16[4,4,128,256]{3,2,1,0:T(8,128)(2,1)}, u32[]{:S(2)}, u32[]{:S(2)}) collective-permute-start(bf16[4,4,128,256]{3,2,1,0:T(8,128)(2,1)} %get-tuple-element.43), channel_id=1, source_target_pairs={{0,3},{1,0},{2,1},{3,2},{4,7},{5,4},{6,5},{7,6},{8,11},{9,8},{10,9... | collective-permute-start | bytes 3145736 | tf_op jit(solution)/shard_map/ppermute | solution.py:33
  73.0 15.7 %all-to-all-start.1 = ((bf16[8,64,512]{2,1,0:T(8,128)(2,1)}), bf16[8,64,512]{2,1,0:T(8,128)(2,1)}, u32[]{:S(2)}, u32[]{:S(2)}) async-start(bf16[8,64,512]{2,1,0:T(8,128)(2,1)} %broadcast_in_dim.40), calls=%async_computation.1 | async-start | bytes 1048576 | tf_op jit(solution)/shard_map/all_to_all | solution.py:299
  89.3 58.6 %all-to-all-start = ((s32[16,1,128]{2,1,0:T(1,128)}), s32[16,1,128]{2,1,0:T(1,128)S(1)}, u32[]{:S(2)}, u32[]{:S(2)}) async-start(s32[16,1,128]{2,1,0:T(1,128)} %broadcast_in_dim.23), calls=%async_computation | async-start | bytes 16384 | tf_op jit(solution)/shard_map/all_to_all | solution.py:299
  151.1 14.8 %collective-permute-start.27 = (bf16[8,128,256]{2,1,0:T(8,128)(2,1)}, bf16[8,128,256]{2,1,0:T(8,128)(2,1)}, u32[]{:S(2)}, u32[]{:S(2)}) collective-permute-start(bf16[8,128,256]{2,1,0:T(8,128)(2,1)} %get-tuple-element.68), channel_id=1, source_target_pairs={{0,1},{1,2},{2,3},{3,0},{4,5},{5,6},{6,7},{7,4},{8,9},{9,10},{10,1... | collective-permute-start | bytes 1572872 | tf_op jit(solution)/shard_map/ppermute | solution.py:33
  151.6 15.4 %collective-permute-start.28 = (bf16[8,128,256]{2,1,0:T(8,128)(2,1)}, bf16[8,128,256]{2,1,0:T(8,128)(2,1)}, u32[]{:S(2)}, u32[]{:S(2)}) collective-permute-start(bf16[8,128,256]{2,1,0:T(8,128)(2,1)} %get-tuple-element.69), channel_id=1, source_target_pairs={{0,3},{1,0},{2,1},{3,2},{4,7},{5,4},{6,5},{7,6},{8,11},{9,8},{10,9... | collective-permute-start | bytes 1572872 | tf_op jit(solution)/shard_map/ppermute | solution.py:33
  154.4 70.6 %collective-permute-start.3 = (bf16[4,4,128,256]{3,2,1,0:T(8,128)(2,1)}, bf16[4,4,128,256]{3,2,1,0:T(8,128)(2,1)S(1)}, u32[]{:S(2)}, u32[]{:S(2)}) collective-permute-start(bf16[4,4,128,256]{3,2,1,0:T(8,128)(2,1)} %get-tuple-element.45), channel_id=1, source_target_pairs={{0,4},{1,5},{2,6},{3,7},{4,8},{5,9},{6,10},{7,11},{8,12},{9,13},{1... | collective-permute-start | bytes 3145736 | tf_op jit(solution)/shard_map/ppermute | solution.py:33
  155.7 69.3 %collective-permute-start.4 = (bf16[4,4,128,256]{3,2,1,0:T(8,128)(2,1)}, bf16[4,4,128,256]{3,2,1,0:T(8,128)(2,1)}, u32[]{:S(2)}, u32[]{:S(2)}) collective-permute-start(bf16[4,4,128,256]{3,2,1,0:T(8,128)(2,1)} %get-tuple-element.46), channel_id=1, source_target_pairs={{0,8},{1,9},{2,10},{3,11},{4,12},{5,13},{6,14},{7,15},{8,0},{9,1},... | collective-permute-start | bytes 3145736 | tf_op jit(solution)/shard_map/ppermute | solution.py:33
  158.4 69.9 %collective-permute-start.5 = (bf16[4,4,128,256]{3,2,1,0:T(8,128)(2,1)}, bf16[4,4,128,256]{3,2,1,0:T(8,128)(2,1)}, u32[]{:S(2)}, u32[]{:S(2)}) collective-permute-start(bf16[4,4,128,256]{3,2,1,0:T(8,128)(2,1)} %get-tuple-element.47), channel_id=1, source_target_pairs={{0,12},{1,13},{2,14},{3,15},{4,0},{5,1},{6,2},{7,3},{8,4},{9,5},{1... | collective-permute-start | bytes 3145736 | tf_op jit(solution)/shard_map/ppermute | solution.py:33
  165.9 47.7 %collective-permute-start.23 = (bf16[8,128,256]{2,1,0:T(8,128)(2,1)}, bf16[8,128,256]{2,1,0:T(8,128)(2,1)}, u32[]{:S(2)}, u32[]{:S(2)}) collective-permute-start(bf16[8,128,256]{2,1,0:T(8,128)(2,1)} %get-tuple-element.64), channel_id=1, source_target_pairs={{0,4},{1,5},{2,6},{3,7},{4,8},{5,9},{6,10},{7,11},{8,12},{9,13},{1... | collective-permute-start | bytes 1572872 | tf_op jit(solution)/shard_map/ppermute | solution.py:33
  167.0 47.2 %collective-permute-start.24 = (bf16[8,128,256]{2,1,0:T(8,128)(2,1)}, bf16[8,128,256]{2,1,0:T(8,128)(2,1)}, u32[]{:S(2)}, u32[]{:S(2)}) collective-permute-start(bf16[8,128,256]{2,1,0:T(8,128)(2,1)} %get-tuple-element.65), channel_id=1, source_target_pairs={{0,12},{1,13},{2,14},{3,15},{4,0},{5,1},{6,2},{7,3},{8,4},{9,5},{1... | collective-permute-start | bytes 1572872 | tf_op jit(solution)/shard_map/ppermute | solution.py:33
  213.6 17.3 %collective-permute-start.6 = (bf16[8,128,256]{2,1,0:T(8,128)(2,1)}, bf16[8,128,256]{2,1,0:T(8,128)(2,1)S(1)}, u32[]{:S(2)}, u32[]{:S(2)}) collective-permute-start(bf16[8,128,256]{2,1,0:T(8,128)(2,1)} %get-tuple-element.48), channel_id=1, source_target_pairs={{0,4},{1,5},{2,6},{3,7},{4,8},{5,9},{6,10},{7,11},{8,12},{9,13},{1... | collective-permute-start | bytes 1572872 | tf_op jit(solution)/shard_map/ppermute | solution.py:33
  214.2 16.8 %collective-permute-start.7 = (bf16[8,128,256]{2,1,0:T(8,128)(2,1)}, bf16[8,128,256]{2,1,0:T(8,128)(2,1)S(1)}, u32[]{:S(2)}, u32[]{:S(2)}) collective-permute-start(bf16[8,128,256]{2,1,0:T(8,128)(2,1)} %get-tuple-element.49), channel_id=1, source_target_pairs={{0,12},{1,13},{2,14},{3,15},{4,0},{5,1},{6,2},{7,3},{8,4},{9,5},{1... | collective-permute-start | bytes 1572872 | tf_op jit(solution)/shard_map/ppermute | solution.py:33
  225.0 43.9 %collective-permute-start.29 = (bf16[16,128,256]{2,1,0:T(8,128)(2,1)}, bf16[16,128,256]{2,1,0:T(8,128)(2,1)}, u32[]{:S(2)}, u32[]{:S(2)}) collective-permute-start(bf16[16,128,256]{2,1,0:T(8,128)(2,1)} %get-tuple-element.70), channel_id=1, source_target_pairs={{0,1},{1,2},{2,3},{3,0},{4,5},{5,6},{6,7},{7,4},{8,9},{9,10},{10,1... | collective-permute-start | bytes 3145736 | tf_op jit(solution)/shard_map/ppermute | solution.py:33
  225.1 45.2 %collective-permute-start.30 = (bf16[16,128,256]{2,1,0:T(8,128)(2,1)}, bf16[16,128,256]{2,1,0:T(8,128)(2,1)}, u32[]{:S(2)}, u32[]{:S(2)}) collective-permute-start(bf16[16,128,256]{2,1,0:T(8,128)(2,1)} %get-tuple-element.71), channel_id=1, source_target_pairs={{0,3},{1,0},{2,1},{3,2},{4,7},{5,4},{6,5},{7,6},{8,11},{9,8},{10,9... | collective-permute-start | bytes 3145736 | tf_op jit(solution)/shard_map/ppermute | solution.py:33
  228.3 41.9 %collective-permute-start.25 = (bf16[16,128,256]{2,1,0:T(8,128)(2,1)}, bf16[16,128,256]{2,1,0:T(8,128)(2,1)}, u32[]{:S(2)}, u32[]{:S(2)}) collective-permute-start(bf16[16,128,256]{2,1,0:T(8,128)(2,1)} %get-tuple-element.66), channel_id=1, source_target_pairs={{0,4},{1,5},{2,6},{3,7},{4,8},{5,9},{6,10},{7,11},{8,12},{9,13},{1... | collective-permute-start | bytes 3145736 | tf_op jit(solution)/shard_map/ppermute | solution.py:33
  230.9 31.7 %collective-permute-start.10 = (bf16[8,128,256]{2,1,0:T(8,128)(2,1)}, bf16[8,128,256]{2,1,0:T(8,128)(2,1)S(1)}, u32[]{:S(2)}, u32[]{:S(2)}) collective-permute-start(bf16[8,128,256]{2,1,0:T(8,128)(2,1)} %get-tuple-element.52), channel_id=1, source_target_pairs={{0,1},{1,2},{2,3},{3,0},{4,5},{5,6},{6,7},{7,4},{8,9},{9,10},{10,1... | collective-permute-start | bytes 1572872 | tf_op jit(solution)/shard_map/ppermute | solution.py:33
  231.0 31.7 %collective-permute-start.11 = (bf16[8,128,256]{2,1,0:T(8,128)(2,1)}, bf16[8,128,256]{2,1,0:T(8,128)(2,1)S(1)}, u32[]{:S(2)}, u32[]{:S(2)}) collective-permute-start(bf16[8,128,256]{2,1,0:T(8,128)(2,1)} %get-tuple-element.53), channel_id=1, source_target_pairs={{0,3},{1,0},{2,1},{3,2},{4,7},{5,4},{6,5},{7,6},{8,11},{9,8},{10,9... | collective-permute-start | bytes 1572872 | tf_op jit(solution)/shard_map/ppermute | solution.py:33
  262.6 26.3 %collective-permute-start.26 = (bf16[16,128,256]{2,1,0:T(8,128)(2,1)}, bf16[16,128,256]{2,1,0:T(8,128)(2,1)}, u32[]{:S(2)}, u32[]{:S(2)}) collective-permute-start(bf16[16,128,256]{2,1,0:T(8,128)(2,1)} %get-tuple-element.67), channel_id=1, source_target_pairs={{0,12},{1,13},{2,14},{3,15},{4,0},{5,1},{6,2},{7,3},{8,4},{9,5},{1... | collective-permute-start | bytes 3145736 | tf_op jit(solution)/shard_map/ppermute | solution.py:33
  262.8 42.6 %collective-permute-start.8 = (bf16[16,128,256]{2,1,0:T(8,128)(2,1)}, bf16[16,128,256]{2,1,0:T(8,128)(2,1)}, u32[]{:S(2)}, u32[]{:S(2)}) collective-permute-start(bf16[16,128,256]{2,1,0:T(8,128)(2,1)} %get-tuple-element.50), channel_id=1, source_target_pairs={{0,4},{1,5},{2,6},{3,7},{4,8},{5,9},{6,10},{7,11},{8,12},{9,13},{1... | collective-permute-start | bytes 3145736 | tf_op jit(solution)/shard_map/ppermute | solution.py:33
  268.8 40.7 %collective-permute-start.9 = (bf16[16,128,256]{2,1,0:T(8,128)(2,1)}, bf16[16,128,256]{2,1,0:T(8,128)(2,1)}, u32[]{:S(2)}, u32[]{:S(2)}) collective-permute-start(bf16[16,128,256]{2,1,0:T(8,128)(2,1)} %get-tuple-element.51), channel_id=1, source_target_pairs={{0,12},{1,13},{2,14},{3,15},{4,0},{5,1},{6,2},{7,3},{8,4},{9,5},{1... | collective-permute-start | bytes 3145736 | tf_op jit(solution)/shard_map/ppermute | solution.py:33
  270.2 39.3 %collective-permute-start.12 = (bf16[16,128,256]{2,1,0:T(8,128)(2,1)}, bf16[16,128,256]{2,1,0:T(8,128)(2,1)}, u32[]{:S(2)}, u32[]{:S(2)}) collective-permute-start(bf16[16,128,256]{2,1,0:T(8,128)(2,1)} %get-tuple-element.54), channel_id=1, source_target_pairs={{0,1},{1,2},{2,3},{3,0},{4,5},{5,6},{6,7},{7,4},{8,9},{9,10},{10,1... | collective-permute-start | bytes 3145736 | tf_op jit(solution)/shard_map/ppermute | solution.py:33
  270.2 39.3 %collective-permute-start.13 = (bf16[16,128,256]{2,1,0:T(8,128)(2,1)}, bf16[16,128,256]{2,1,0:T(8,128)(2,1)}, u32[]{:S(2)}, u32[]{:S(2)}) collective-permute-start(bf16[16,128,256]{2,1,0:T(8,128)(2,1)} %get-tuple-element.55), channel_id=1, source_target_pairs={{0,3},{1,0},{2,1},{3,2},{4,7},{5,4},{6,5},{7,6},{8,11},{9,8},{10,9... | collective-permute-start | bytes 3145736 | tf_op jit(solution)/shard_map/ppermute | solution.py:33
  346.3 7.9 %collective-permute-start.33 = (bf16[32,1024]{1,0:T(8,128)(2,1)S(1)}, bf16[32,1024]{1,0:T(8,128)(2,1)S(1)}, u32[]{:S(2)}, u32[]{:S(2)}) collective-permute-start(bf16[32,1024]{1,0:T(8,128)(2,1)S(1)} %fusion), channel_id=1, source_target_pairs={{0,64},{16,80},{32,96},{48,112},{64,0},{80,16},{96,32},{112,48},{1... | collective-permute-start | bytes 196616 | tf_op jit(solution)/shard_map/ppermute | solution.py:41
  (30 other events, 300.0 us)
